TPU v7x, 32 devices: a whole 2x2x4 slice. The times are simulated.
32 devices in a mesh: dp: 8 (over y, x, core), fsdp: 4 (over z).
Axes of the slice: x: 2, y: 2, z: 4, core: 2. Of those that a mesh axis runs over, the one named last changes fastest.
Arguments:
- states_in: bfloat16 [16, 256, 2048], P('dp', 'fsdp'), may hold values from -6 to 6
- out_cotangent: bfloat16 [16, 256, 2048], P('dp', 'fsdp'), may hold values from -6 to 6
- segments: int32 [16, 256], P('dp'), may hold values from 0 to 31, as said below
- starts: int32 [16, 256], P('dp'), may hold values from 0 to 1
- norm_gain: bfloat16 [2048], replicated, may hold values from 0.5 to 1.5
- in_x_weight: bfloat16 [2048, 4096], P(None, 'fsdp'), may hold values from -0.125 to 0.125
- in_z_weight: bfloat16 [2048, 4096], P(None, 'fsdp'), may hold values from -0.125 to 0.125
- conv_weight: bfloat16 [4, 4096], P(None, 'fsdp'), may hold values from -3 to 3
- conv_bias: bfloat16 [4096], P('fsdp'), may hold values from -0.5 to 0.5
- x_proj_weight: bfloat16 [4096, 160], P('fsdp'), may hold values from -0.09375 to 0.09375
- dt_weight: bfloat16 [128, 4096], P(None, 'fsdp'), may hold values from -0.5 to 0.5
- dt_bias: bfloat16 [4096], P('fsdp'), may hold values from -4 to 0
- skip_weight: bfloat16 [4096], P('fsdp'), may hold values from 0.5 to 1.5
- out_weight: bfloat16 [4096, 2048], P('fsdp'), may hold values from -0.1875 to 0.1875
Outputs:
- output: bfloat16 [16, 256, 2048], P('dp', 'fsdp')
- input_grad: float32 [16, 256, 2048], P('dp', 'fsdp')
- norm_gain_grad: float32 [2048], replicated
- in_x_grad: float32 [2048, 4096], P('dp', 'fsdp')
- in_z_grad: float32 [2048, 4096], P('dp', 'fsdp')
- conv_grad: float32 [4, 4096], P(None, 'fsdp')
- conv_bias_grad: float32 [4096], P('fsdp')
- x_proj_grad: float32 [4096, 160], P('fsdp')
- dt_grad: float32 [128, 4096], P('dp', 'fsdp')
- dt_bias_grad: float32 [4096], P('fsdp')
- skip_grad: float32 [4096], P('fsdp')
- out_grad: float32 [4096, 2048], P('fsdp', 'dp')
Inputs may be any that keep to these rules, and one draw needn't show every extreme that they name: Within each sequence, segments start at 0 at its first token, never fall, and rise by one exactly at the tokens where starts is 1; starts is 1 at every sequence's first token, and 1 only at positions that are multiples of 8.
All inputs are finite; a program needn't handle non-finite values.
Results may differ from a plain program's by a relative error of at most 0.012.
Values may be sent and summed in bfloat16 or wider, within the bound.
No kernel may reach another device: no remote copies, remote signals or barrier semaphores. Data moves between devices by JAX's collectives and lax.ppermute only.
A program may use at most 224 MiB of HBM per device.

v0:
```python
import jax
import jax.numpy as jnp
from jax import lax
from jax.sharding import PartitionSpec as P

BLOCK = 16


norm_eps = 1e-05


def from_behind(block, axis, distance):
    devices = range(lax.axis_size(axis))
    route = [(i - distance, i) for i in devices if i - distance in devices]
    return lax.ppermute(block, axis, route)


def prefix(x, axis, join, neutral, backward):
    count = lax.axis_size(axis)
    place = lax.axis_index(axis)
    ahead = count - 1 - place if backward else place
    gathered = jax.tree.map(
        lambda a, kind: lax.all_gather(a.astype(kind), axis), x, (jnp.bfloat16, jnp.bfloat16)
    )
    state = jax.tree.map(lambda a, e: jnp.zeros_like(a) + jnp.asarray(e, a.dtype), x, neutral)

    def one(step, state):
        source = count - 1 - step if backward else step
        return join(
            state,
            jax.tree.map(
                lambda a, own: lax.dynamic_index_in_dim(a, source, 0, False).astype(own.dtype),
                gathered,
                x,
            ),
        )

    return lax.fori_loop(0, ahead, one, state)


def norm_rows(tokens, scale):
    return tokens * lax.rsqrt(jnp.mean(tokens * tokens, axis=1, keepdims=True) + norm_eps) * scale


def silu_slope(value):
    sigma = jax.nn.sigmoid(value)
    return sigma * (1.0 + value * (1.0 - sigma))


def conv_masks(seg_ext, count, span):
    own = seg_ext[span - 1 : span - 1 + count]
    return [(seg_ext[tap : tap + count] == own).astype(jnp.float32)[:, None] for tap in range(span)]


def conv_apply(extended, taps, bias, masks):
    count = extended.shape[0] - len(masks) + 1
    total = bias[None, :]
    for tap in range(len(masks)):
        total = total + taps[tap][None, :] * extended[tap : tap + count] * masks[tap]
    return jax.nn.silu(total)


def split_blocks(array):
    return array.reshape((array.shape[0] // BLOCK, BLOCK) + array.shape[1:])


def step_scale(rates, keys):
    return rates / (1.0 + rates * jnp.sum(keys * keys, axis=1, keepdims=True))


def recur_block(state, rates, keys, queries, values, keep):
    scale = step_scale(rates, keys)
    results = []
    for position in range(rates.shape[0]):
        column = keys[position][:, None]
        decay = keep[position] * (1.0 - column * column * scale[position][None, :])
        state = decay * state + column * (scale[position] * values[position])[None, :]
        results.append(jnp.sum(queries[position][:, None] * state, axis=0))
    return (jnp.stack(results), state)


def summary_block(carry, block):
    state, product = carry
    rates, keys, queries, values, keep = block
    scale = step_scale(rates, keys)
    for position in range(rates.shape[0]):
        column = keys[position][:, None]
        decay = keep[position] * (1.0 - column * column * scale[position][None, :])
        state = decay * state + column * (scale[position] * values[position])[None, :]
        product = decay * product
    return ((state, product), None)


def output_block(state, block):
    results, state_next = recur_block(state, block[0], block[1], block[2], block[3], block[4])
    return (state_next, (results, state))


def reverse_block(carry, block):
    rates, keys, queries, values, keep, grad_mixed = block
    scale = step_scale(rates, keys)
    for position in reversed(range(rates.shape[0])):
        column = keys[position][:, None]
        decay = keep[position] * (1.0 - column * column * scale[position][None, :])
        carry = decay * (queries[position][:, None] * grad_mixed[position][None, :] + carry)
    return (carry, None)


def gradient_block(carry, block):
    rates, keys, queries, values, keep, grad_mixed, start_state = block

    def run(start_state, rates, keys, queries, values):
        return recur_block(start_state, rates, keys, queries, values, keep)

    _, back = jax.vjp(run, start_state, rates, keys, queries, values)
    grad_state, grad_rates, grad_keys, grad_queries, grad_values = back((grad_mixed, carry))
    return (grad_state, (grad_rates, grad_keys, grad_queries, grad_values))


def combine_pairs(earlier, later):
    return (earlier[0] * later[0], later[0] * earlier[1] + later[1])


def rows_product(left, right):
    return lax.dot_general(
        left, right, (((0,), (0,)), ((), ())), preferred_element_type=jnp.float32
    )


def cols_product(left, right):
    return lax.dot_general(
        left, right, (((1,), (1,)), ((), ())), preferred_element_type=jnp.float32
    )


def add_terms(totals, terms):
    if totals is None:
        return terms
    return tuple((total + term for total, term in zip(totals, terms)))


def per_device(
    states_in,
    out_cotangent,
    segments,
    starts,
    norm_gain,
    in_x_weight,
    in_z_weight,
    conv_weight,
    conv_bias,
    x_proj_weight,
    dt_weight,
    dt_bias,
    skip_weight,
    out_weight,
):
    micro_count, seq_rows, width = states_in.shape
    inner_local = in_x_weight.shape[1]
    span = conv_weight.shape[0]
    rank = dt_weight.shape[0]
    state_dim = (x_proj_weight.shape[1] - rank) // 2
    offset = lax.axis_index("fsdp") * inner_local
    gain = norm_gain.astype(jnp.float32)
    outputs = []
    input_grads = []
    totals = None
    first = lax.axis_index("fsdp") * seq_rows
    for micro in range(micro_count):
        whole = (
            lax.all_gather(in_x_weight, "fsdp", axis=1, tiled=True),
            lax.all_gather(in_z_weight, "fsdp", axis=1, tiled=True),
            lax.all_gather(conv_weight, "fsdp", axis=1, tiled=True),
            lax.all_gather(conv_bias, "fsdp", axis=0, tiled=True),
            lax.all_gather(x_proj_weight, "fsdp", axis=0, tiled=True),
            lax.all_gather(dt_weight, "fsdp", axis=1, tiled=True),
            lax.all_gather(dt_bias, "fsdp", axis=0, tiled=True),
            lax.all_gather(skip_weight, "fsdp", axis=0, tiled=True),
            lax.all_gather(out_weight, "fsdp", axis=0, tiled=True),
        )
        full_x, full_z, taps, bias, full_proj, full_dt, rate_bias, skip, full_out = whole
        taps = taps.astype(jnp.float32)
        bias = bias.astype(jnp.float32)
        rate_bias = rate_bias.astype(jnp.float32)
        skip = skip.astype(jnp.float32)
        inner = full_x.shape[1]
        tok_rows = states_in[micro].astype(jnp.float32)
        normed_f, norm_back = jax.vjp(norm_rows, tok_rows, gain)
        normed = normed_f.astype(jnp.bfloat16)
        x_in = jnp.dot(normed, full_x, preferred_element_type=jnp.float32).astype(jnp.bfloat16)
        gate_pre = jnp.dot(normed, full_z, preferred_element_type=jnp.float32)
        prior = from_behind(x_in[seq_rows - span + 1 :], "fsdp", 1)
        extended = jnp.concatenate([prior, x_in], 0).astype(jnp.float32)
        padded = jnp.concatenate([jnp.full((span - 1,), -1, jnp.int32), segments[micro]], 0)
        seg_ext = lax.dynamic_slice_in_dim(padded, first, seq_rows + span - 1)
        masks = conv_masks(seg_ext, seq_rows, span)

        def conv_here(extended, taps, bias):
            return conv_apply(extended, taps, bias, masks)

        mixer_f, conv_back = jax.vjp(conv_here, extended, taps, bias)
        mixer_in = mixer_f.astype(jnp.bfloat16)
        values = mixer_in.astype(jnp.float32)
        projected = jnp.dot(mixer_in, full_proj, preferred_element_type=jnp.float32)
        dt_low = projected[:, :rank].astype(jnp.bfloat16)
        keys = projected[:, rank : rank + state_dim]
        queries = projected[:, rank + state_dim :]
        dt_pre = jnp.dot(dt_low, full_dt, preferred_element_type=jnp.float32) + rate_bias
        rates = jax.nn.softplus(dt_pre)
        keep = 1.0 - lax.dynamic_slice_in_dim(starts[micro], first, seq_rows).astype(jnp.float32)
        inputs = (
            split_blocks(rates),
            split_blocks(keys),
            split_blocks(queries),
            split_blocks(values),
            split_blocks(keep),
        )
        zeros = jnp.zeros((state_dim, inner), jnp.float32)
        ones = jnp.ones((state_dim, inner), jnp.float32)
        (local_end, product), _ = lax.scan(summary_block, (zeros, ones), inputs)
        _, state_in = prefix((product, local_end), "fsdp", combine_pairs, (ones, zeros), False)
        _, (mixed_blocks, start_states) = lax.scan(output_block, state_in, inputs)
        mixed = mixed_blocks.reshape(seq_rows, inner) + skip * values
        gate = jax.nn.silu(gate_pre)
        gated = (mixed * gate).astype(jnp.bfloat16)
        branch = jnp.dot(gated, full_out, preferred_element_type=jnp.float32)
        outputs.append((tok_rows + branch).astype(jnp.bfloat16))
        grad_out = out_cotangent[micro]
        grad_gated = cols_product(grad_out, full_out)
        grad_mixed = grad_gated * gate
        grad_gate = (grad_gated * mixed * silu_slope(gate_pre)).astype(jnp.bfloat16)
        grad_skip = jnp.sum(grad_mixed * values, axis=0)
        back_inputs = inputs + (split_blocks(grad_mixed),)
        local_in, _ = lax.scan(reverse_block, zeros, back_inputs, reverse=True)
        _, incoming = prefix((product, local_in), "fsdp", combine_pairs, (ones, zeros), True)
        _, (grad_rates, grad_keys, grad_queries, grad_rec) = lax.scan(
            gradient_block, incoming, back_inputs + (start_states,), reverse=True
        )
        grad_rates = grad_rates.reshape(seq_rows, inner)
        grad_keys = grad_keys.reshape(seq_rows, state_dim)
        grad_queries = grad_queries.reshape(seq_rows, state_dim)
        grad_rec = grad_rec.reshape(seq_rows, inner)
        grad_dt = (grad_rates * jax.nn.sigmoid(dt_pre)).astype(jnp.bfloat16)
        grad_proj = jnp.concatenate(
            [cols_product(grad_dt, full_dt), grad_keys, grad_queries], 1
        ).astype(jnp.bfloat16)
        grad_mixer = cols_product(grad_proj, full_proj) + grad_mixed * skip + grad_rec
        grad_ext, grad_taps, grad_bias = conv_back(grad_mixer)
        from_next = from_behind(grad_ext[: span - 1].astype(jnp.bfloat16), "fsdp", -1).astype(
            jnp.float32
        )
        own_part = grad_ext[span - 1 :]
        grad_xin = jnp.concatenate(
            [own_part[: seq_rows - span + 1], own_part[seq_rows - span + 1 :] + from_next], 0
        ).astype(jnp.bfloat16)
        grad_normed = cols_product(grad_xin, full_x) + cols_product(grad_gate, full_z)
        grad_rows, grad_gain = norm_back(grad_normed)
        input_grads.append(grad_out.astype(jnp.float32) + grad_rows)
        terms = (
            rows_product(normed, grad_xin),
            rows_product(normed, grad_gate),
            grad_taps,
            grad_bias,
            rows_product(mixer_in, grad_proj),
            rows_product(dt_low, grad_dt),
            jnp.sum(grad_dt.astype(jnp.float32), axis=0),
            grad_skip,
            rows_product(gated, grad_out),
            grad_gain,
        )
        totals = add_terms(totals, terms)
    small = (totals[2], totals[3], totals[4], totals[6], totals[7])
    grad_big = (
        lax.psum_scatter(totals[0], "dp", scatter_dimension=0, tiled=True),
        lax.psum_scatter(totals[1], "dp", scatter_dimension=0, tiled=True),
        lax.psum_scatter(totals[5], "dp", scatter_dimension=0, tiled=True),
        lax.psum_scatter(totals[8], "dp", scatter_dimension=1, tiled=True),
    )
    grad_big = (
        lax.psum_scatter(
            grad_big[0].astype(jnp.bfloat16), "fsdp", scatter_dimension=1, tiled=True
        ).astype(jnp.float32),
        lax.psum_scatter(
            grad_big[1].astype(jnp.bfloat16), "fsdp", scatter_dimension=1, tiled=True
        ).astype(jnp.float32),
        lax.psum_scatter(
            grad_big[2].astype(jnp.bfloat16), "fsdp", scatter_dimension=1, tiled=True
        ).astype(jnp.float32),
        lax.psum_scatter(
            grad_big[3].astype(jnp.bfloat16), "fsdp", scatter_dimension=0, tiled=True
        ).astype(jnp.float32),
    )
    summed = lax.psum((small[0], small[1], small[2], small[3], small[4], totals[9]), ("dp", "fsdp"))
    conv_grad = lax.dynamic_slice_in_dim(summed[0], offset, inner_local, 1)
    conv_bias_grad = lax.dynamic_slice_in_dim(summed[1], offset, inner_local, 0)
    proj_grad = lax.dynamic_slice_in_dim(summed[2], offset, inner_local, 0)
    dt_bias_grad = lax.dynamic_slice_in_dim(summed[3], offset, inner_local, 0)
    skip_grad = lax.dynamic_slice_in_dim(summed[4], offset, inner_local, 0)
    return (
        jnp.stack(outputs),
        jnp.stack(input_grads),
        summed[5],
        grad_big[0],
        grad_big[1],
        conv_grad,
        conv_bias_grad,
        proj_grad,
        grad_big[2],
        dt_bias_grad,
        skip_grad,
        grad_big[3],
    )


def solution(mesh):
    in_specs = (
        P("dp", "fsdp", None),
        P("dp", "fsdp", None),
        P("dp", None),
        P("dp", None),
        P(),
        P(None, "fsdp"),
        P(None, "fsdp"),
        P(None, "fsdp"),
        P("fsdp"),
        P("fsdp", None),
        P(None, "fsdp"),
        P("fsdp"),
        P("fsdp"),
        P("fsdp", None),
    )
    out_specs = (
        P("dp", "fsdp", None),
        P("dp", "fsdp", None),
        P(),
        P("dp", "fsdp"),
        P("dp", "fsdp"),
        P(None, "fsdp"),
        P("fsdp"),
        P("fsdp", None),
        P("dp", "fsdp"),
        P("fsdp"),
        P("fsdp"),
        P("fsdp", "dp"),
    )
    return jax.shard_map(
        per_device, mesh=mesh, in_specs=in_specs, out_specs=out_specs, check_vma=False
    )
```

profile of v0, /device:TPU:0, one launch (start us, length us, event | category | flops | bytes accessed | tf_op | source)
XLA Modules:
  0.0 3006.2 jit_solution(13884338503993642044)
XLA Ops:
  13.8 13.6 all_gather.76
  27.4 24.1 all_gather.81
  51.4 15.9 all_gather.86
  68.0 28.8 all_gather.77
  97.5 202.4 %all-gather.12.cloned.1.call-done = bf16[2048,4096]{1,0:T(8,128)(2,1)} async-done(((bf16[2048,1024]{1,0:T(8,128)(2,1)}), bf16[2048,4096]{1,0:T(8,128)(2,1)}) %all-gather.12.cloned.1.call-update) | async-done | bytes 16777232 | tf_op jit(solution)/shard_map/all_gather | solution.py:171
  318.8 267.6 %all-gather.18.cloned.1.call-done = bf16[2048,4096]{1,0:T(8,128)(2,1)} async-done(((bf16[2048,1024]{1,0:T(8,128)(2,1)}), bf16[2048,4096]{1,0:T(8,128)(2,1)}) %all-gather.18.cloned.1.call-update) | async-done | bytes 16777232 | tf_op jit(solution)/shard_map/all_gather | solution.py:172
  603.9 269.7 %all-gather.20.cloned.1.call-done = bf16[4096,2048]{1,0:T(8,128)(2,1)} async-done(((bf16[1024,2048]{1,0:T(8,128)(2,1)}), bf16[4096,2048]{1,0:T(8,128)(2,1)}) %all-gather.20.cloned.1.call-update) | async-done | bytes 16777232 | tf_op jit(solution)/shard_map/all_gather | solution.py:179
  873.6 15.3 multiply_reduce_fusion.194
  889.0 16.9 all-gather.14.cloned.1.call-done
  908.5 25.8 all-gather.16.cloned.1.call-done
  937.3 98.2 %while.189 = (s32[]{:T(128)}, f32[16,4096]{1,0:T(8,128)S(1)}, f32[16,4096]{1,0:T(8,128)S(1)}, f32[4,16]{1,0:T(4,128)}, f32[4,16,16]{2,1,0:T(8,128)S(1)}, /*index...) while((s32[]{:T(128)}, f32[16,4096]{1,0:T(8,128)S(1)}, ...), condition=%wide.region_28.29_spmd.clone, body=%wide.region_26.28_spmd.clone.sunk | while | flops 10879746 | bytes 3661868 | solution.py:220
  1036.2 67.5 %while.191 = (s32[]{:T(128)}, f32[16,4096]{1,0:T(8,128)S(1)}, f32[4,16]{1,0:T(4,128)}, f32[4,16,16]{2,1,0:T(8,128)S(1)}, f32[4,16,4096]{2,1,0:T(8,128)S(1)}, /*i...) while((s32[]{:T(128)}, f32[16,4096]{1,0:T(8,128)S(1)}, ...), condition=%wide.region_142.143_spmd.clone, body=%wide.region_140.142_spmd.clone.sunk | while | flops 6554371 | bytes 2629627 | solution.py:234
  1103.8 15.7 all-gather.3
  1119.5 16.5 all-gather.5
  1136.0 16.9 all-gather.2
  1158.4 120.2 %while.183 = (s32[]{:T(128)}, f32[16,4096]{1,0:T(8,128)S(1)}, f32[4,16,4096]{2,1,0:T(8,128)}, f32[4,16,4096]{2,1,0:T(8,128)}, f32[4,16]{1,0:T(4,128)}, /*index=5...) while((s32[]{:T(128)}, f32[16,4096]{1,0:T(8,128)S(1)}, ...), condition=%wide.region_49.50_spmd, body=%wide.region_31.49_spmd.sunk | while | flops 11731713 | bytes 9415765 | solution.py:222
  1162.8 11.7 multiply_reduce_fusion.251
  1192.8 11.7 multiply_reduce_fusion.251
  1222.9 11.7 multiply_reduce_fusion.251
  1252.9 11.7 multiply_reduce_fusion.251
  1280.8 198.9 %while.187 = (s32[]{:T(128)}, f32[16,4096]{1,0:T(8,128)S(1)}, f32[4,16,4096]{2,1,0:T(8,128)}, bf16[4,16,16]{2,1,0:T(8,128)(2,1)S(1)}, bf16[4,16,16]{2,1,0:T(8,12...) while((s32[]{:T(128)}, f32[16,4096]{1,0:T(8,128)S(1)}, ...), condition=%wide.region_228.229_spmd, body=%wide.region_145.228_spmd.sunk | while | flops 36381680 | bytes 18347452 | solution.py:236
  1286.7 11.7 multiply_add_fusion.149
  1336.5 11.7 multiply_add_fusion.149
  1386.3 11.7 multiply_add_fusion.149
  1482.0 14.0 multiply_reduce_fusion.195
  1501.8 94.7 %while.188 = (s32[]{:T(128)}, f32[16,4096]{1,0:T(8,128)S(1)}, f32[16,4096]{1,0:T(8,128)S(1)}, f32[4,16]{1,0:T(4,128)S(1)}, f32[4,16,16]{2,1,0:T(8,128)S(1)}, /*i...) while((s32[]{:T(128)}, f32[16,4096]{1,0:T(8,128)S(1)}, ...), condition=%wide.region_3.4_spmd.clone, body=%wide.region_1.3_spmd.clone.sunk | while | flops 10879746 | bytes 3661868 | solution.py:220
  1597.2 64.1 %while.190 = (s32[]{:T(128)}, f32[16,4096]{1,0:T(8,128)S(1)}, f32[4,16]{1,0:T(4,128)S(1)}, f32[4,16,16]{2,1,0:T(8,128)S(1)}, f32[4,16,4096]{2,1,0:T(8,128)S(1)},...) while((s32[]{:T(128)}, f32[16,4096]{1,0:T(8,128)S(1)}, ...), condition=%wide.region_52.53_spmd.clone, body=%wide.region_50.52_spmd.clone.sunk | while | flops 6554371 | bytes 2629627 | solution.py:234
  1661.4 16.9 all-gather.1
  1678.3 16.7 all-gather.4
  1695.0 15.7 all-gather
  1716.2 115.0 %while.181 = (s32[]{:T(128)}, f32[16,4096]{1,0:T(8,128)S(1)}, f32[4,16,4096]{2,1,0:T(8,128)}, f32[4,16,4096]{2,1,0:T(8,128)}, f32[4,16]{1,0:T(4,128)S(1)}, /*ind...) while((s32[]{:T(128)}, f32[16,4096]{1,0:T(8,128)S(1)}, ...), condition=%wide.region_24.25_spmd, body=%wide.region_6.24_spmd.sunk | while | flops 11731713 | bytes 9415765 | solution.py:222
  1833.4 191.7 %while.185 = (s32[]{:T(128)}, f32[16,4096]{1,0:T(8,128)S(1)}, f32[4,16,4096]{2,1,0:T(8,128)}, bf16[4,16,16]{2,1,0:T(8,128)(2,1)S(1)}, bf16[4,16,16]{2,1,0:T(8,12...) while((s32[]{:T(128)}, f32[16,4096]{1,0:T(8,128)S(1)}, ...), condition=%wide.region_138.139_spmd, body=%wide.region_55.138_spmd.sunk | while | flops 36381680 | bytes 18347452 | solution.py:236
  2035.3 13.6 fusion.624
  2049.0 25.2 convolution_add_fusion
  2075.2 18.4 fusion.594
  2093.6 30.5 %convolution_add_fusion.2 = f32[4096,2048]{1,0:T(8,128)} fusion(f32[4096,2048]{1,0:T(8,128)} %fusion.594, bf16[64,4096]{1,0:T(8,128)(2,1)S(1)} %get-tuple-element.2918, bf16[2,64,2048]{2,1,0:T(8,128)(2,1)S(1)} %copy-done.26), kind=kOutput, calls=%fused_computation.1524 | convolution fusion | flops 1082130432 | bytes 67895296 | tf_op jit(solution)/shard_map/dot_general | solution.py:125
  2144.1 14.2 fusion.589
  2158.3 25.8 convolution_add_fusion.1
  2190.0 90.1 %reduce-scatter.13.cloned.1.call-done = f32[256,4096]{1,0:T(8,128)} async-done(((f32[2048,4096]{1,0:T(8,128)}), f32[256,4096]{1,0:T(8,128)}) %reduce-scatter.13.cloned.1.call-update) | async-done | bytes 4194320 | tf_op jit(solution)/shard_map/reduce_scatter | solution.py:275
  2284.0 204.9 %reduce-scatter.21.cloned.1.call-done = f32[4096,256]{1,0:T(8,128)} async-done(((f32[4096,2048]{1,0:T(8,128)}), f32[4096,256]{1,0:T(8,128)}) %reduce-scatter.21.cloned.1.call-update) | async-done | bytes 4194320 | tf_op jit(solution)/shard_map/reduce_scatter | solution.py:277
  2502.5 11.8 fusion.562
  2515.1 183.0 %reduce-scatter.9.cloned.1.call-done = f32[256,4096]{1,0:T(8,128)} async-done(((f32[2048,4096]{1,0:T(8,128)}), f32[256,4096]{1,0:T(8,128)}) %reduce-scatter.9.cloned.1.call-update) | async-done | bytes 4194320 | tf_op jit(solution)/shard_map/reduce_scatter | solution.py:274
  2747.0 40.2 %all-reduce.178 = (f32[2048]{0:T(1024)}, f32[4096]{0:T(1024)S(1)}, f32[4096]{0:T(1024)S(1)}, f32[4096]{0:T(1024)S(1)}) all-reduce(f32[2048]{0:T(1024)S(1)} %add.1576, f32[4096]{0:T(1024)S(1)} %add.1581, f32[4096]{0:T(1024)S(1)} %add.1584, f32[4096]{0:T(1024)S(1)} %add.1585), channel_id=1, replica_groups=mesh['dp'=8,'fsdp'=4] {'dp','fsdp'}, use_global_device_ids=true, to_apply=%region_232.233 | all-reduce | flops 14336 | bytes 114688 | tf_op jit(solution)/shard_map/psum | solution.py:293
  2790.4 50.3 %all-reduce.182.cloned.1.call-done = (f32[4,4096]{1,0:T(4,128)}, f32[4096,160]{0,1:T(8,128)}) async-done(((f32[4,4096]{1,0:T(4,128)}, f32[4096,160]{0,1:T(8,128)}), (f32[4,4096]{1,0:T(4,128)}, f32[4096,160]{0,1:T(8,128)})) %all-reduce.182.cloned.1.call-update) | async-done | bytes 2686992 | tf_op jit(solution)/shard_map/psum | solution.py:293
  2844.0 18.0 reduce-scatter.19.cloned.1.call-done
  2863.4 42.8 %reduce-scatter.15.cloned.1.call-done = bf16[256,1024]{1,0:T(8,128)(2,1)} async-done(((bf16[256,4096]{1,0:T(8,128)(2,1)}), bf16[256,1024]{1,0:T(8,128)(2,1)}) %reduce-scatter.15.cloned.1.call-update) | async-done | bytes 524304 | tf_op jit(solution)/shard_map/reduce_scatter | solution.py:283
  2908.3 43.5 %reduce-scatter.23.cloned.1.call-done = bf16[1024,256]{1,0:T(8,128)(2,1)} async-done(((bf16[4096,256]{1,0:T(8,128)(2,1)}), bf16[1024,256]{1,0:T(8,128)(2,1)}) %reduce-scatter.23.cloned.1.call-update) | async-done | bytes 524304 | tf_op jit(solution)/shard_map/reduce_scatter | solution.py:289
  2953.8 43.2 %reduce-scatter.11.cloned.1.call-done = bf16[256,1024]{1,0:T(8,128)(2,1)} async-done(((bf16[256,4096]{1,0:T(8,128)(2,1)}), bf16[256,1024]{1,0:T(8,128)(2,1)}) %reduce-scatter.11.cloned.1.call-update) | async-done | bytes 524304 | tf_op jit(solution)/shard_map/reduce_scatter | solution.py:280
  (920 shorter events, 1063.0 us)
Async XLA Ops:
  7.2 292.7 %all-gather.12.cloned.1.call-start = ((), (), s32[]{:S(2)}) async-start(), calls=%async_computation.8 | async-start | bytes 20971520 | tf_op jit(solution)/shard_map/all_gather | solution.py:171
  8.0 19.4 copy-start.60
  8.0 43.5 %copy-start.61 = (bf16[1024]{0:T(1024)(128)(2,1)S(1)}, bf16[1024]{0:T(1024)(128)(2,1)}, u32[]{:S(2)}) copy-start(bf16[1024]{0:T(1024)(128)(2,1)} %param.50) | copy-start | bytes 6148
  8.0 60.0 %copy-start.57 = (bf16[4,1024]{1,0:T(4,128)(2,1)S(1)}, bf16[4,1024]{1,0:T(4,128)(2,1)}, u32[]{:S(2)}) copy-start(bf16[4,1024]{1,0:T(4,128)(2,1)} %param.45) | copy-start | bytes 24580
  8.0 578.4 %all-gather.18.cloned.1.call-start = ((), (), s32[]{:S(2)}) async-start(), calls=%async_computation.11 | async-start | bytes 20971520 | tf_op jit(solution)/shard_map/all_gather | solution.py:172
  8.7 864.8 %all-gather.20.cloned.1.call-start = ((), (), s32[]{:S(2)}) async-start(), calls=%async_computation.12 | async-start | bytes 20971520 | tf_op jit(solution)/shard_map/all_gather | solution.py:179
  9.5 896.5 %all-gather.14.cloned.1.call-start = ((), (), s32[]{:S(2)}) async-start(), calls=%async_computation.9 | async-start | bytes 1638400 | tf_op jit(solution)/shard_map/all_gather | solution.py:175
  10.1 924.3 %all-gather.16.cloned.1.call-start = ((), (), s32[]{:S(2)}) async-start(), calls=%async_computation.10 | async-start | bytes 1310720 | tf_op jit(solution)/shard_map/all_gather | solution.py:176
  10.6 2177.7 %reduce-scatter.17.cloned.1.call-start = ((), (), s32[]{:S(2)}) async-start(), calls=%async_computation.17 | async-start | bytes 2359296 | tf_op jit(solution)/shard_map/reduce_scatter | solution.py:276
  11.5 585.0 %copy-start.46 = (f32[64]{0:T(128)}, f32[64]{0:T(128)S(1)}, u32[]{:S(2)}) copy-start(f32[64]{0:T(128)S(1)} %fusion.615) | copy-start | bytes 772
  27.4 846.2 %copy-start.50 = (f32[4096]{0:T(1024)}, f32[4096]{0:T(1024)S(1)}, u32[]{:S(2)}) copy-start(f32[4096]{0:T(1024)S(1)} %convert_element_type.260) | copy-start | bytes 49156
  51.4 882.9 %copy-start.35 = (f32[4096]{0:T(1024)}, f32[4096]{0:T(1024)S(1)}, u32[]{:S(2)}) copy-start(f32[4096]{0:T(1024)S(1)} %convert_element_type.270) | copy-start | bytes 49156
  97.5 776.1 %copy-start.51 = (f32[1,4096]{1,0:T(1,128)}, f32[1,4096]{1,0:T(1,128)S(1)}, u32[]{:S(2)}) copy-start(f32[1,4096]{1,0:T(1,128)S(1)} %get-tuple-element.2914) | copy-start | bytes 49156
  308.9 293.7 %collective-permute-start.1 = (bf16[3,4096]{1,0:T(4,128)(2,1)S(1)}, bf16[3,4096]{1,0:T(4,128)(2,1)S(1)}, u32[]{:S(2)}, u32[]{:S(2)}) collective-permute-start(bf16[3,4096]{1,0:T(4,128)(2,1)S(1)} %slice.5158), channel_id=1, source_target_pairs={{0,1},{1,2},{2,3},{4,5},{5,6},{6,7},{8,9},{9,10},{10,11},{12,13},{... | collective-permute-start | bytes 73736 | tf_op jit(solution)/shard_map/ppermute | solution.py:15
  316.0 280.5 %copy-start.25 = (bf16[64,4096]{1,0:T(8,128)(2,1)}, bf16[64,4096]{1,0:T(8,128)(2,1)S(1)}, u32[]{:S(2)}) copy-start(bf16[64,4096]{1,0:T(8,128)(2,1)S(1)} %convolution_convert_fusion.1) | copy-start | bytes 1572868
  316.7 1163.1 %collective-permute-start = (bf16[3,4096]{1,0:T(4,128)(2,1)}, bf16[3,4096]{1,0:T(4,128)(2,1)}, u32[]{:S(2)}, u32[]{:S(2)}) collective-permute-start(bf16[3,4096]{1,0:T(4,128)(2,1)} %slice.5147), channel_id=1, source_target_pairs={{0,1},{1,2},{2,3},{4,5},{5,6},{6,7},{8,9},{9,10},{10,11},{12,13},{... | collective-permute-start | bytes 73736 | tf_op jit(solution)/shard_map/ppermute | solution.py:15
  599.4 274.2 %copy-start.71 = (f32[64]{0:T(128)S(1)}, f32[64]{0:T(128)}, u32[]{:S(2)}) copy-start(f32[64]{0:T(128)} %get-tuple-element.2927) | copy-start | bytes 772
  599.4 274.2 %copy-start.73 = (f32[64]{0:T(128)S(1)}, f32[64]{0:T(128)}, u32[]{:S(2)}) copy-start(f32[64]{0:T(128)} %get-tuple-element.2928) | copy-start | bytes 772
  599.4 274.2 %copy-start.75 = (f32[64]{0:T(128)S(1)}, f32[64]{0:T(128)}, u32[]{:S(2)}) copy-start(f32[64]{0:T(128)} %get-tuple-element.2929) | copy-start | bytes 772
  602.6 286.3 %copy-start.22 = (f32[64,4096]{1,0:T(8,128)}, f32[64,4096]{1,0:T(8,128)S(1)}, u32[]{:S(2)}) copy-start(f32[64,4096]{1,0:T(8,128)S(1)} %fusion.632) | copy-start | bytes 3145732
  888.9 19.6 copy-start.9
  907.8 29.4 copy-start.31
  1479.8 16.2 copy-start.44
  1482.0 16.8 copy-start.36
  1501.8 95.4 %copy-start.4 = (f32[16,4096]{1,0:T(8,128)S(1)}, f32[16,4096]{1,0:T(8,128)}, u32[]{:S(2)}) copy-start(f32[16,4096]{1,0:T(8,128)} %custom-call.4) | copy-start | bytes 786436
  1833.4 194.4 %copy-start.34 = (f32[64,160]{1,0:T(8,128)S(1)}, f32[64,160]{1,0:T(8,128)}, u32[]{:S(2)}) copy-start(f32[64,160]{1,0:T(8,128)} %copy-done.33) | copy-start | bytes 122884
  2025.1 109.9 %copy-start.40 = (bf16[4,16,16]{2,1,0:T(8,128)(2,1)}, bf16[4,16,16]{2,1,0:T(8,128)(2,1)S(1)}, u32[]{:S(2)}) copy-start(bf16[4,16,16]{2,1,0:T(8,128)(2,1)S(1)} %get-tuple-element.1251) | copy-start | bytes 6148
  2031.3 248.8 %reduce-scatter.13.cloned.1.call-start = ((), (), s32[]{:S(2)}) async-start(), calls=%async_computation.15 | async-start | bytes 37748736 | tf_op jit(solution)/shard_map/reduce_scatter | solution.py:275
  2035.3 13.7 copy-start.15
  2035.3 13.7 copy-start.17
  2035.3 58.3 %copy-start.11 = (bf16[64,4096]{1,0:T(8,128)(2,1)}, bf16[64,4096]{1,0:T(8,128)(2,1)S(1)}, u32[]{:S(2)}) copy-start(bf16[64,4096]{1,0:T(8,128)(2,1)S(1)} %get-tuple-element.2918) | copy-start | bytes 1572868
  2035.3 13.7 copy-start.47
  2074.2 414.7 %reduce-scatter.21.cloned.1.call-start = ((), (), s32[]{:S(2)}) async-start(), calls=%async_computation.19 | async-start | bytes 37748736 | tf_op jit(solution)/shard_map/reduce_scatter | solution.py:277
  2124.2 574.0 %reduce-scatter.9.cloned.1.call-start = ((), (), s32[]{:S(2)}) async-start(), calls=%async_computation.13 | async-start | bytes 37748736 | tf_op jit(solution)/shard_map/reduce_scatter | solution.py:274
  2133.0 6.4 collective-permute-start.3
  2138.1 6.0 collective-permute-start.2
  2184.2 656.5 %all-reduce.182.cloned.1.call-start = ((), (), s32[]{:S(2)}) async-start(), calls=%async_computation.21 | async-start | bytes 5373952 | tf_op jit(solution)/shard_map/psum | solution.py:293
  2188.3 673.7 %reduce-scatter.19.cloned.1.call-start = ((), (), s32[]{:S(2)}) async-start(), calls=%async_computation.18 | async-start | bytes 163840 | tf_op jit(solution)/shard_map/reduce_scatter | solution.py:286
  2190.0 716.2 %reduce-scatter.15.cloned.1.call-start = ((), (), s32[]{:S(2)}) async-start(), calls=%async_computation.16 | async-start | bytes 2621440 | tf_op jit(solution)/shard_map/reduce_scatter | solution.py:283
  2283.9 209.0 %copy-start.48 = (f32[4096]{0:T(1024)S(1)}, f32[4096]{0:T(1024)}, u32[]{:S(2)}) copy-start(f32[4096]{0:T(1024)} %get-tuple-element.2026) | copy-start | bytes 49156
  2284.0 209.0 %copy-start.49 = (f32[4096]{0:T(1024)S(1)}, f32[4096]{0:T(1024)}, u32[]{:S(2)}) copy-start(f32[4096]{0:T(1024)} %get-tuple-element.2030) | copy-start | bytes 49156
  2284.0 209.1 %copy-start.37 = (f32[4096]{0:T(1024)S(1)}, f32[4096]{0:T(1024)}, u32[]{:S(2)}) copy-start(f32[4096]{0:T(1024)} %get-tuple-element.2036) | copy-start | bytes 49156
  2284.0 209.1 %copy-start.38 = (f32[4096]{0:T(1024)S(1)}, f32[4096]{0:T(1024)}, u32[]{:S(2)}) copy-start(f32[4096]{0:T(1024)} %get-tuple-element.2034) | copy-start | bytes 49156
  2284.0 667.8 %reduce-scatter.23.cloned.1.call-start = ((), (), s32[]{:S(2)}) async-start(), calls=%async_computation.20 | async-start | bytes 2621440 | tf_op jit(solution)/shard_map/reduce_scatter | solution.py:289
  2492.7 504.4 %reduce-scatter.11.cloned.1.call-start = ((), (), s32[]{:S(2)}) async-start(), calls=%async_computation.14 | async-start | bytes 2621440 | tf_op jit(solution)/shard_map/reduce_scatter | solution.py:280
  2735.6 53.4 %copy-start.65 = (f32[64]{0:T(128)S(1)}, f32[64]{0:T(128)}, u32[]{:S(2)}) copy-start(f32[64]{0:T(128)} %copy-done.64) | copy-start | bytes 772
  2735.6 53.4 %copy-start.67 = (f32[64]{0:T(128)S(1)}, f32[64]{0:T(128)}, u32[]{:S(2)}) copy-start(f32[64]{0:T(128)} %copy-done.66) | copy-start | bytes 772
  2735.6 53.4 %copy-start.27 = (bf16[2,64,2048]{2,1,0:T(8,128)(2,1)S(1)}, bf16[2,64,2048]{2,1,0:T(8,128)(2,1)}, u32[]{:S(2)}) copy-start(bf16[2,64,2048]{2,1,0:T(8,128)(2,1)} %param.39) | copy-start | bytes 1572868
  (48 other events, 181.7 us)
Sparse Core Ops, SparseCore 0:
  9.6 290.2 all-gather.11
  301.4 284.9 all-gather.17
  588.0 285.5 all-gather.19
  875.0 30.8 all-gather.13
  907.4 26.9 all-gather.15
  2031.4 39.3 reduce-scatter.16
  2074.8 205.2 reduce-scatter.12
  2283.7 205.2 reduce-scatter.20
  2492.9 205.1 reduce-scatter.8
  2704.2 136.4 all-reduce.181
  2843.6 18.3 reduce-scatter.18
  2864.1 41.9 reduce-scatter.14
  2908.6 43.1 reduce-scatter.22
  2953.9 43.1 reduce-scatter.10
where the time goes:
time: 3020 us; the launch traced here: 3010 us
  waiting for transfers between devices  1470 us (49%)
  other arithmetic  854 us (28%)
  matrix products  273 us (9%)
  blocking collectives  221 us (7%)
  local copies, waits for them, and re-layouts  165 us (5%)
    all_gather x1, waiting for transfers between devices, per_device(): lax.all_gather(out_weight, 'fsdp', axis=0, tiled=True)  270 us
    all_gather x1, waiting for transfers between devices, per_device(): lax.all_gather(in_z_weight, 'fsdp', axis=1, tiled=True)  268 us
    reduce_sum x72, other arithmetic, recur_block(): decay = keep[position] * (1.0 - column * column * scale[position][None, :])  223 us
    reduce_scatter x1, waiting for transfers between devices, per_device(): lax.psum_scatter(totals[8], 'dp', scatter_dimension=1, tiled=True)  205 us
    all_gather x1, waiting for transfers between devices, per_device(): lax.all_gather(in_x_weight, 'fsdp', axis=1, tiled=True)  202 us
    reduce_scatter x1, waiting for transfers between devices, per_device(): lax.psum_scatter(totals[0], 'dp', scatter_dimension=0, tiled=True)  183 us
    reduce_sum x72, other arithmetic, recur_block(): results.append(jnp.sum(queries[position][:, None] * state, axis=0))  170 us
    dot_general x10, matrix products, rows_product(): lax.dot_general(left, right, (((0,), (0,)), ((), ())), preferred_element_...  133 us
  transfers between devices with their start and end apart: 18, of which 14 were waited for; matrix products, arithmetic and copies ran while one was open for 26% of the time, Pallas kernels for 0%

commit v1 on v0

v1 whole, which is shorter than its diff:
```python
import functools

import jax
import jax.numpy as jnp
from jax import lax
from jax.experimental import pallas as pl
from jax.experimental.pallas import tpu as pltpu
from jax.sharding import PartitionSpec as P

BLOCK = 16
LANES = 128
norm_eps = 1e-05
f32 = jnp.float32
bf16 = jnp.bfloat16


def mm(left, right, contract):
    return lax.dot_general(left, right, ((contract[:1], contract[1:]), ((), ())), preferred_element_type=f32)


def swap(x, axis, bit):
    return lax.ppermute(x, axis, [(i, i ^ bit) for i in range(lax.axis_size(axis))])


def bits_of(count):
    return [1 << k for k in range(count.bit_length() - 1)]


def gather_parts(x, axis):
    held = {0: x}
    for bit in reversed(bits_of(lax.axis_size(axis))):
        for mask in list(held):
            held[mask | bit] = swap(held[mask], axis, bit)
    return [held[mask] for mask in range(len(held))]


def take_bit(x, dim, value):
    return lax.dynamic_index_in_dim(x, value, dim, keepdims=False)


class Scatter:
    def __init__(self, x, axis, bits, dims):
        self.x, self.axis, self.left = x, axis, list(zip(bits, dims))

    def send(self):
        bit, dim = self.left[0]
        own = (lax.axis_index(self.axis) // bit) % 2
        self.got = swap(take_bit(self.x, dim, 1 - own).astype(bf16), self.axis, bit)
        self.kept = take_bit(self.x, dim, own)
        return self.got

    def add(self):
        _, dim = self.left.pop(0)
        self.left = [(bit, d - 1 if d > dim else d) for bit, d in self.left]
        self.x = self.kept.astype(f32) + self.got.astype(f32)

    def finish(self):
        while self.left:
            self.send()
            self.add()
        return self.x


def scatter_of(x, axis):
    count = lax.axis_size(axis)
    bits = bits_of(count)
    n = len(bits)
    return Scatter(x.reshape((2,) * n + (x.shape[0] // count,) + x.shape[1:]), axis, bits, range(n - 1, -1, -1))


def scatter_rest(x):
    bits = bits_of(lax.axis_size("dp"))[1:]
    n = len(bits)
    half = x.shape[1] // 2
    parts = []
    for start, order in ((0, list(range(n))), (half, list(range(n))[::-1])):
        piece = x[:, start : start + half].reshape((2,) * n + (half,) + x.shape[2:])
        parts.append(Scatter(piece, "dp", [bits[k] for k in order], [n - 1 - k for k in order]))
    return parts


def all_sum(x, axis, kind=bf16):
    for bit in bits_of(lax.axis_size(axis)):
        low = x.astype(kind)
        x = low.astype(f32) + swap(low, axis, bit).astype(f32)
    return x


def exchange_all(x, axis):
    return [x] + [swap(x, axis, mask) for mask in range(1, lax.axis_size(axis))]


def add_up(refs):
    total = refs[0][...].astype(f32)
    for ref in refs[1:]:
        total = total + ref[...].astype(f32)
    return total


def silu_slope(v):
    s = jax.nn.sigmoid(v)
    return s * (1.0 + v * (1.0 - s))


def conv_sum(x, masks, taps, bias):
    span = taps.shape[0]
    total = bias + taps[span - 1 : span] * x
    shifted = []
    for w in range(span - 1):
        moved = pltpu.roll(x, span - 1 - w, 0) * masks[:, w : w + 1]
        shifted.append(moved)
        total = total + taps[w : w + 1] * moved
    return total, shifted + [x]


def enter_kernel(count, offs_ref, *refs):
    parts = refs[:count]
    gain_ref, mask_ref, wx_ref, wz_ref, taps_ref, bias_ref, wp_ref = refs[count : count + 7]
    normed_ref, xin_ref, z_ref, xs_ref, proj_ref, acc_s = refs[count + 7 :]
    step = pl.program_id(0)

    @pl.when(step == 0)
    def _():
        gain = gain_ref[...].astype(f32)
        for m, part in enumerate(parts):
            v = part[...].astype(f32)
            rscale = lax.rsqrt(jnp.mean(v * v, axis=1, keepdims=True) + norm_eps)
            rows = part.shape[0]
            normed_ref[pl.ds(pl.multiple_of(offs_ref[0, m], rows), rows), :] = (v * rscale * gain).astype(bf16)
        acc_s[...] = jnp.zeros_like(acc_s)

    normed = normed_ref[...]
    z_ref[...] = jnp.dot(normed, wz_ref[...], preferred_element_type=f32)
    x_in = jnp.dot(normed, wx_ref[...], preferred_element_type=f32).astype(bf16)
    xin_ref[...] = x_in
    pre, _ = conv_sum(x_in.astype(f32), mask_ref[...], taps_ref[...].astype(f32), bias_ref[...].astype(f32))
    xs = jax.nn.silu(pre).astype(bf16)
    xs_ref[...] = xs
    acc_s[...] += mm(wp_ref[...], xs, (1, 1))

    @pl.when(step == pl.num_programs(0) - 1)
    def _():
        proj_ref[...] = acc_s[...].astype(bf16)


def blocks_of(rows, wide):
    return pl.BlockSpec((rows, wide), lambda c: (0, c))


def whole_of(shape):
    return pl.BlockSpec(shape, lambda c: (0,) * len(shape))


def enter(offs, parts, gain, masks, wx, wz, taps, bias, wp):
    rows, model = parts[0].shape
    seq_len = rows * len(parts)
    inner = wx.shape[1]
    wide = 256
    return pl.pallas_call(
        functools.partial(enter_kernel, len(parts)),
        grid=(inner // wide,),
        in_specs=[pl.BlockSpec(memory_space=pltpu.SMEM)]
        + [whole_of((rows, model))] * len(parts)
        + [
            whole_of((1, model)),
            whole_of(masks.shape),
            blocks_of(model, wide),
            blocks_of(model, wide),
            blocks_of(taps.shape[0], wide),
            blocks_of(1, wide),
            blocks_of(wp.shape[0], wide),
        ],
        out_specs=[
            whole_of((seq_len, model)),
            blocks_of(seq_len, wide),
            blocks_of(seq_len, wide),
            blocks_of(seq_len, wide),
            whole_of((wp.shape[0], seq_len)),
        ],
        out_shape=[
            jax.ShapeDtypeStruct((seq_len, model), bf16),
            jax.ShapeDtypeStruct((seq_len, inner), bf16),
            jax.ShapeDtypeStruct((seq_len, inner), f32),
            jax.ShapeDtypeStruct((seq_len, inner), bf16),
            jax.ShapeDtypeStruct((wp.shape[0], seq_len), bf16),
        ],
        scratch_shapes=[pltpu.VMEM((wp.shape[0], seq_len), f32)],
        name="enter",
        cost_estimate=pl.CostEstimate(
            flops=4 * seq_len * model * inner,
            bytes_accessed=4 * model * inner + 10 * seq_len * inner,
            transcendentals=seq_len * inner,
        ),
    )(offs, *parts, gain, masks, wx, wz, taps, bias, wp)


def leave_kernel(count, *refs):
    terms = refs[:count]
    wp_ref, gxs_ref, xin_ref, xs_ref, gz_ref, mask_ref, taps_ref, bias_ref, wx_ref, wz_ref, normed_ref = refs[
        count : count + 11
    ]
    gxin_ref, gn_ref, rows_ref, xpg_ref, gain_ref, acc_s = refs[count + 11 :]
    step = pl.program_id(0)
    span = taps_ref.shape[0]
    seq_len = xin_ref.shape[0]
    gproj = add_up(terms).astype(bf16)
    xpg_ref[...] = mm(gproj, xs_ref[...], (1, 0))
    g_xs = gxs_ref[...] + mm(gproj, wp_ref[...], (0, 0))
    masks = mask_ref[...]
    taps = taps_ref[...].astype(f32)
    pre, shifted = conv_sum(xin_ref[...].astype(f32), masks, taps, bias_ref[...].astype(f32))
    g_conv = g_xs * silu_slope(pre)
    total = taps[span - 1 : span] * g_conv
    for w in range(span):
        rows_ref[w : w + 1, :] = jnp.sum(g_conv * shifted[w], axis=0, keepdims=True)
        if w < span - 1:
            term = g_conv * masks[:, w : w + 1] * taps[w : w + 1]
            total = total + pltpu.roll(term, seq_len - (span - 1 - w), 0)
    rows_ref[span : span + 1, :] = jnp.sum(g_conv, axis=0, keepdims=True)
    rows_ref[span + 1 :, :] = jnp.zeros((8 - span - 1, g_conv.shape[1]), f32)
    g_x_in = total.astype(bf16)
    gxin_ref[...] = g_x_in
    gn = mm(g_x_in, wx_ref[...], (1, 1)) + mm(gz_ref[...], wz_ref[...], (1, 1))

    @pl.when(step == 0)
    def _():
        acc_s[...] = gn

    @pl.when(step > 0)
    def _():
        acc_s[...] += gn

    @pl.when(step == pl.num_programs(0) - 1)
    def _():
        gn = acc_s[...]
        gn_ref[...] = gn.astype(bf16)
        gain_ref[...] = jnp.sum(gn * normed_ref[...].astype(f32), axis=0, keepdims=True)


def leave(terms, wp, gxs, xin, xs, gz, masks, taps, bias, wx, wz, normed):
    seq_len, model = normed.shape
    inner = wx.shape[1]
    wide = 256
    return pl.pallas_call(
        functools.partial(leave_kernel, len(terms)),
        grid=(inner // wide,),
        in_specs=[whole_of(terms[0].shape)] * len(terms)
        + [
            blocks_of(wp.shape[0], wide),
            blocks_of(seq_len, wide),
            blocks_of(seq_len, wide),
            blocks_of(seq_len, wide),
            blocks_of(seq_len, wide),
            whole_of(masks.shape),
            blocks_of(taps.shape[0], wide),
            blocks_of(1, wide),
            blocks_of(model, wide),
            blocks_of(model, wide),
            whole_of((seq_len, model)),
        ],
        out_specs=[
            blocks_of(seq_len, wide),
            whole_of((seq_len, model)),
            blocks_of(8, wide),
            blocks_of(wp.shape[0], wide),
            whole_of((1, model)),
        ],
        out_shape=[
            jax.ShapeDtypeStruct((seq_len, inner), bf16),
            jax.ShapeDtypeStruct((seq_len, model), bf16),
            jax.ShapeDtypeStruct((8, inner), f32),
            jax.ShapeDtypeStruct((wp.shape[0], inner), f32),
            jax.ShapeDtypeStruct((1, model), f32),
        ],
        scratch_shapes=[pltpu.VMEM((seq_len, model), f32)],
        name="leave",
        cost_estimate=pl.CostEstimate(
            flops=4 * seq_len * model * inner,
            bytes_accessed=4 * model * inner + 14 * seq_len * inner,
            transcendentals=seq_len * inner,
        ),
    )(*terms, wp, gxs, xin, xs, gz, masks, taps, bias, wx, wz, normed)


def recurrence_kernel(state_dim, rank, count, keep_ref, offs_ref, *refs):
    parts, terms = refs[:count], refs[count : 2 * count]
    xs_ref, z_ref, wo_ref, wdt_ref, dtb_ref, skip_ref = refs[2 * count : 2 * count + 6]
    gated_ref, gz_ref, gxs_ref, gproj_ref, small_ref, dtg_ref, cot_ref, out_ref = refs[2 * count + 6 : 2 * count + 14]
    (
        gg_s,
        proj_s,
        gproj_s,
        acc_s,
        slope_s,
        eps_s,
        u_s,
        gm_s,
        y_s,
        s1_s,
        s2_s,
        hist_s,
        even_g_s,
        odd_g_s,
        even_p_s,
        odd_p_s,
        kt_s,
        qt_s,
        kd_s,
        k2d_s,
        qd_s,
        norm_s,
        sum_s,
        tail_s,
        gq_s,
        ge_s,
        pe_s,
        gqt_s,
        get_s,
        pet_s,
    ) = refs[2 * count + 14 :]
    step = pl.program_id(0)
    seq_len, width = xs_ref.shape
    blocks = seq_len // BLOCK
    flat = BLOCK * state_dim
    lane = lax.broadcasted_iota(jnp.int32, (state_dim, BLOCK), 1)

    @pl.when(step == 0)
    def _():
        proj_s[...] = add_up(terms)
        for m, part in enumerate(parts):
            rows = part.shape[0]
            cot_ref[pl.ds(pl.multiple_of(offs_ref[0, m], rows), rows), :] = part[...]
        turned = proj_s[rank:, :]
        for b in range(blocks):
            cols = slice(b * BLOCK, (b + 1) * BLOCK)
            kt_s[b] = jnp.pad(turned[:state_dim, cols], ((0, 0), (0, LANES - BLOCK)))
            qt_s[b] = jnp.pad(turned[state_dim:, cols], ((0, 0), (0, LANES - BLOCK)))
        source = lax.broadcasted_iota(jnp.int32, (2 * state_dim, flat), 0)
        target = lax.rem(lax.broadcasted_iota(jnp.int32, (2 * state_dim, flat), 1), state_dim)
        take_k = (source == target).astype(bf16)
        take_q = (source == target + state_dim).astype(bf16)
        own = (
            lax.rem(lax.broadcasted_iota(jnp.int32, (seq_len, flat), 0), BLOCK)
            == lax.broadcasted_iota(jnp.int32, (seq_len, flat), 1) // state_dim
        )
        kd_s[...] = jnp.where(own, mm(turned.astype(bf16), take_k, (0, 0)), 0.0).astype(bf16)
        k2d_s[...] = jnp.where(own, mm((turned * turned).astype(bf16), take_k, (0, 0)), 0.0).astype(bf16)
        qd_s[...] = jnp.where(own, mm(turned.astype(bf16), take_q, (0, 0)), 0.0).astype(bf16)
        square = jnp.sum(turned[:state_dim] * turned[:state_dim], axis=0, keepdims=True)
        norm_s[...] = jnp.broadcast_to(square, (LANES, seq_len)).T
        sum_s[...] = jnp.zeros_like(sum_s)
        gq_s[...] = jnp.zeros_like(gq_s)
        ge_s[...] = jnp.zeros_like(ge_s)
        pe_s[...] = jnp.zeros_like(pe_s)

    gg_s[...] = mm(cot_ref[...], wo_ref[...], (1, 1))
    low = proj_s[:rank, :].astype(bf16)
    dt_pre = mm(low, wdt_ref[...], (0, 0)) + dtb_ref[...].astype(f32)
    rates = jnp.maximum(dt_pre, 0.0) + jnp.log1p(jnp.exp(-jnp.abs(dt_pre)))
    ratio = 1.0 / (1.0 + rates * norm_s[:, 0:1])
    eps_s[...] = rates * ratio
    slope_s[...] = ratio * ratio * jax.nn.sigmoid(dt_pre)
    u_s[...] = eps_s[...] * xs_ref[...].astype(f32)
    gm_s[...] = gg_s[...] * jax.nn.silu(z_ref[...])
    hist_s[0:state_dim, :] = jnp.zeros((state_dim, width), bf16)

    def own_token(pairs):
        picked = pairs[:state_dim]
        for t in range(1, BLOCK):
            picked = jnp.where(lane == t, pairs[t * state_dim : (t + 1) * state_dim], picked)
        return picked

    def read_states(b, buf):
        toks = pl.ds(pl.multiple_of(b * BLOCK, BLOCK), BLOCK)
        hblk = buf[...]
        y_s[toks, :] = jnp.dot(qd_s[toks, :], hblk, preferred_element_type=f32)
        gqt_s[b, :, :BLOCK] = own_token(mm(hblk, gm_s[toks, :].astype(bf16), (1, 1)))

    def scan_block(b, h, buf):
        base = pl.multiple_of(b * BLOCK, BLOCK)
        kt = kt_s[b]
        for t in range(BLOCK):
            if t % 8 == 0:
                h = h * keep_ref[0, b * 2 + t // 8]
            col = jnp.broadcast_to(kt[:, t : t + 1], (state_dim, width))
            e = eps_s[pl.ds(base + t, 1), :]
            u = u_s[pl.ds(base + t, 1), :]
            h = (1.0 - (col * col) * e) * h + col * u
            kept = h.astype(bf16)
            hist_s[pl.ds(pl.multiple_of((base + t + 1) * state_dim, state_dim), state_dim), :] = kept
            buf[t * state_dim : (t + 1) * state_dim, :] = kept
        return h

    def forward(i, h):
        read_states(jnp.maximum(2 * i - 1, 0), odd_g_s)
        h = scan_block(2 * i, h, even_g_s)
        read_states(2 * i, even_g_s)
        return scan_block(2 * i + 1, h, odd_g_s)

    lax.fori_loop(0, blocks // 2, forward, jnp.zeros((state_dim, width), f32))
    read_states(blocks - 1, odd_g_s)

    def read_grads(b, gbuf, pbuf):
        toks = pl.ds(pl.multiple_of(b * BLOCK, BLOCK), BLOCK)
        gblk = gbuf[...]
        pblk = pbuf[...]
        s1_s[toks, :] = jnp.dot(kd_s[toks, :], gblk, preferred_element_type=f32)
        s2_s[toks, :] = jnp.dot(k2d_s[toks, :], pblk, preferred_element_type=f32)
        get_s[b, :, :BLOCK] = own_token(mm(gblk, u_s[toks, :].astype(bf16), (1, 1)))
        pet_s[b, :, :BLOCK] = own_token(mm(pblk, eps_s[toks, :].astype(bf16), (1, 1)))

    def back_block(b, carry, gbuf, pbuf):
        base = pl.multiple_of(b * BLOCK, BLOCK)
        kt = kt_s[b]
        qt = qt_s[b]
        for t in reversed(range(BLOCK)):
            colq = jnp.broadcast_to(qt[:, t : t + 1], (state_dim, width))
            col = jnp.broadcast_to(kt[:, t : t + 1], (state_dim, width))
            e = eps_s[pl.ds(base + t, 1), :]
            gm = gm_s[pl.ds(base + t, 1), :]
            g = colq * gm + carry
            before = hist_s[pl.ds(pl.multiple_of((base + t) * state_dim, state_dim), state_dim), :].astype(f32)
            p = g * before
            carry = (1.0 - (col * col) * e) * g
            if t % 8 == 0:
                k = keep_ref[0, b * 2 + t // 8]
                carry = carry * k
                p = p * k
            gbuf[t * state_dim : (t + 1) * state_dim, :] = g.astype(bf16)
            pbuf[t * state_dim : (t + 1) * state_dim, :] = p.astype(bf16)
        return carry

    def backward(i, carry):
        last = blocks - 1 - 2 * i
        read_grads(jnp.minimum(last + 1, blocks - 1), even_g_s, even_p_s)
        carry = back_block(last, carry, odd_g_s, odd_p_s)
        read_grads(last, odd_g_s, odd_p_s)
        return back_block(last - 1, carry, even_g_s, even_p_s)

    lax.fori_loop(0, blocks // 2, backward, jnp.zeros((state_dim, width), f32))
    read_grads(0, even_g_s, even_p_s)
    gq_s[...] += gqt_s[...]
    ge_s[...] += get_s[...]
    pe_s[...] += pet_s[...]

    xs = xs_ref[...].astype(f32)
    z = z_ref[...]
    skip = skip_ref[...].astype(f32)
    sig = jax.nn.sigmoid(z)
    mixed = y_s[...] + skip * xs
    gated = (mixed * (z * sig)).astype(bf16)
    gated_ref[...] = gated
    out_part = jnp.dot(gated, wo_ref[...], preferred_element_type=f32)
    gz_ref[...] = (gg_s[...] * mixed * (sig * (1.0 + z * (1.0 - sig)))).astype(bf16)
    gm = gm_s[...]
    s1 = s1_s[...]
    eps = eps_s[...]
    g_eps = xs * s1 - s2_s[...]
    sum_s[...] += jnp.broadcast_to(jnp.sum(g_eps * eps * eps, axis=1, keepdims=True), sum_s.shape)
    g_dt = (g_eps * slope_s[...]).astype(bf16)
    dtg_ref[...] = mm(low, g_dt, (1, 0))
    gxs_ref[...] = skip * gm + eps * s1
    small_ref[0:1, :] = jnp.sum(gm * xs, axis=0, keepdims=True)
    small_ref[1:2, :] = jnp.sum(g_dt.astype(f32), axis=0, keepdims=True)
    small_ref[2:, :] = jnp.zeros((6, width), f32)
    g_low = mm(wdt_ref[...], g_dt, (1, 1))

    @pl.when(step == 0)
    def _():
        gproj_s[...] = g_low
        acc_s[...] = out_part

    @pl.when(step > 0)
    def _():
        gproj_s[...] += g_low
        acc_s[...] += out_part

    @pl.when(step == pl.num_programs(0) - 1)
    def _():
        scale = sum_s[...].T[0:1, :]
        for b in range(blocks):
            cols = slice(b * BLOCK, (b + 1) * BLOCK)
            own_keys = ge_s[b, :, :BLOCK] - 2.0 * kt_s[b, :, :BLOCK] * (pe_s[b, :, :BLOCK] + scale[:, cols])
            tail_s[:state_dim, cols] = own_keys
            tail_s[state_dim:, cols] = gq_s[b, :, :BLOCK]
        gproj_ref[:rank, :] = gproj_s[...].astype(bf16)
        gproj_ref[rank:, :] = tail_s[...].astype(bf16)
        out_ref[...] = acc_s[...].astype(bf16)


def recurrence(keep, offs, parts, terms, xs, z, wo, wdt, dt_bias, skip):
    seq_len, inner = xs.shape
    model = wo.shape[1]
    rank = wdt.shape[0]
    columns = terms[0].shape[0]
    state_dim = (columns - rank) // 2
    wide = 512
    flat = BLOCK * state_dim
    blocks = seq_len // BLOCK
    vmem = pltpu.VMEM
    return pl.pallas_call(
        functools.partial(recurrence_kernel, state_dim, rank, len(parts)),
        grid=(inner // wide,),
        in_specs=[pl.BlockSpec(memory_space=pltpu.SMEM)] * 2
        + [whole_of(parts[0].shape)] * len(parts)
        + [whole_of((columns, seq_len))] * len(terms)
        + [
            blocks_of(seq_len, wide),
            blocks_of(seq_len, wide),
            pl.BlockSpec((wide, model), lambda c: (c, 0)),
            blocks_of(rank, wide),
            blocks_of(1, wide),
            blocks_of(1, wide),
        ],
        out_specs=[
            blocks_of(seq_len, wide),
            blocks_of(seq_len, wide),
            blocks_of(seq_len, wide),
            whole_of((columns, seq_len)),
            blocks_of(8, wide),
            blocks_of(rank, wide),
            whole_of((seq_len, model)),
            whole_of((seq_len, model)),
        ],
        out_shape=[
            jax.ShapeDtypeStruct((seq_len, inner), bf16),
            jax.ShapeDtypeStruct((seq_len, inner), bf16),
            jax.ShapeDtypeStruct((seq_len, inner), f32),
            jax.ShapeDtypeStruct((columns, seq_len), bf16),
            jax.ShapeDtypeStruct((8, inner), f32),
            jax.ShapeDtypeStruct((rank, inner), f32),
            jax.ShapeDtypeStruct((seq_len, model), bf16),
            jax.ShapeDtypeStruct((seq_len, model), bf16),
        ],
        scratch_shapes=[
            vmem((seq_len, wide), f32),
            vmem((columns, seq_len), f32),
            vmem((rank, seq_len), f32),
            vmem((seq_len, model), f32),
            vmem((seq_len, wide), f32),
        ]
        + [vmem((seq_len, wide), f32)] * 6
        + [vmem(((seq_len + 1) * state_dim, wide), bf16)]
        + [vmem((flat, wide), bf16)] * 4
        + [vmem((blocks, state_dim, LANES), f32)] * 2
        + [vmem((seq_len, flat), bf16)] * 3
        + [vmem((seq_len, LANES), f32)] * 2
        + [vmem((2 * state_dim, seq_len), f32)]
        + [vmem((blocks, state_dim, LANES), f32)] * 6,
        name="recurrence",
        cost_estimate=pl.CostEstimate(
            flops=60 * seq_len * state_dim * inner + 4 * seq_len * model * inner,
            bytes_accessed=2 * model * inner + 20 * seq_len * inner,
            transcendentals=6 * seq_len * inner,
        ),
    )(keep, offs, *parts, *terms, xs, z, wo, wdt, dt_bias, skip)


def grad_kernel(place_ref, la_ref, lb_ref, ra_ref, rb_ref, out_ref):
    out_ref[0] = (mm(la_ref[...], ra_ref[...], (0, 0)) + mm(lb_ref[...], rb_ref[...], (0, 0))).astype(bf16)


def grad_add_kernel(place_ref, la_ref, lb_ref, ra_ref, rb_ref, got_ref, out_ref):
    total = mm(la_ref[...], ra_ref[...], (0, 0)) + mm(lb_ref[...], rb_ref[...], (0, 0))
    out_ref[0] = (total + got_ref[0].astype(f32)).astype(bf16)


def grad_slices(left, right, own, parts, got=None):
    seq_len, model = left[0].shape
    inner = right[0].shape[1]
    rows = model // parts
    if rows % LANES:
        total = sum(mm(a, b, (0, 0)) for a, b in zip(left, right)).reshape(parts // 2, 2, rows, inner)
        total = take_bit(total, 1, own)
        return (total if got is None else total + got.astype(f32)).astype(bf16)
    place = own.reshape(1).astype(jnp.int32)
    lhs = pl.BlockSpec((seq_len, rows), lambda j, place: (0, 2 * j + place[0]))
    rhs = pl.BlockSpec((seq_len, inner), lambda j, place: (0, 0))
    block = pl.BlockSpec((1, rows, inner), lambda j, place: (j, 0, 0))
    kernel = grad_kernel if got is None else grad_add_kernel
    extra = () if got is None else (got,)
    return pl.pallas_call(
        kernel,
        grid_spec=pltpu.PrefetchScalarGridSpec(
            num_scalar_prefetch=1,
            grid=(parts // 2,),
            in_specs=[lhs, lhs, rhs, rhs] + [block] * len(extra),
            out_specs=block,
        ),
        out_shape=jax.ShapeDtypeStruct((parts // 2, rows, inner), bf16),
        name="weight_grad",
        cost_estimate=pl.CostEstimate(
            flops=2 * seq_len * model * inner,
            bytes_accessed=2 * seq_len * (model + 2 * inner) + 2 * model * inner,
            transcendentals=0,
        ),
    )(place, *left, *right, *extra)


def after(x, *others):
    return lax.optimization_barrier((x, others))[0]


def per_device(
    states_in,
    out_cotangent,
    segments,
    starts,
    norm_gain,
    in_x_weight,
    in_z_weight,
    conv_weight,
    conv_bias,
    x_proj_weight,
    dt_weight,
    dt_bias,
    skip_weight,
    out_weight,
):
    count, rows, model = states_in.shape
    span, inner = conv_weight.shape
    rank = dt_weight.shape[0]
    seq_len = segments.shape[1]
    dp = lax.axis_size("dp")
    gain = norm_gain.astype(f32)
    proj_weight = x_proj_weight.T
    keep = 1.0 - starts[:, ::8].astype(f32)
    seqs = range(count)
    me = lax.axis_index("fsdp")
    core = lax.rem(lax.axis_index("dp"), 2)
    offs = jnp.stack([(me ^ mask) * rows for mask in range(lax.axis_size("fsdp"))])[None, :].astype(jnp.int32)
    tap_bias = conv_bias[None, :]
    normed, xin, xs, z, masks, projs = [], [], [], [], [], []
    gated, gz, gxs, gprojs, small, dtg, cots, branch = [], [], [], [], [], [], [], []
    g_x_in, gn, rows_part, proj_part, gain_part = [], [], [], [], []
    tokens, cot_parts = [], []
    behind = ()
    for s in seqs:
        for source, into in ((states_in, tokens), (out_cotangent, cot_parts)):
            into.append(gather_parts(after(source[s], *behind), "fsdp"))
            behind = (into[s][-2],)
    for s in seqs:
        seg_ext = jnp.pad(segments[s], (span - 1, 0), constant_values=-1)
        mask = jnp.stack([(seg_ext[w : w + seq_len] == segments[s]).astype(f32) for w in range(span)], 1)
        masks.append(jnp.pad(mask, ((0, 0), (0, LANES - span))))

    def run_enter(s):
        got = enter(
            offs, tokens[s], norm_gain[None, :], masks[s], in_x_weight, in_z_weight, conv_weight, tap_bias, proj_weight
        )
        for into, value in zip((normed, xin, z, xs), got):
            into.append(value)
        projs.append(exchange_all(got[4], "fsdp"))

    def run_recurrence(s):
        got = recurrence(
            keep[s : s + 1],
            offs,
            cot_parts[s],
            projs[s],
            xs[s],
            z[s],
            out_weight,
            dt_weight,
            dt_bias[None, :],
            skip_weight[None, :],
        )
        for into, value in zip((gated, gz, gxs, gprojs, small, dtg, cots, branch), got):
            into.append(value)
        gprojs[s] = exchange_all(gprojs[s], "fsdp")
        branch[s] = scatter_of(branch[s], "fsdp")

    def run_leave(s, *behind):
        got = leave(
            gprojs[s],
            proj_weight,
            after(gxs[s], *behind),
            xin[s],
            xs[s],
            gz[s],
            masks[s],
            conv_weight,
            tap_bias,
            in_x_weight,
            in_z_weight,
            normed[s],
        )
        for into, value in zip((g_x_in, gn, rows_part, proj_part, gain_part), got):
            into.append(value)
        gn[s] = scatter_of(gn[s], "fsdp")

    run_enter(0)
    run_enter(1)
    run_recurrence(0)
    run_recurrence(1)
    first_a = branch[0].send()
    out_sent = swap(grad_slices(cots, [gated[0], after(gated[1], first_a)], 1 - core, dp), "dp", 1)
    z_sent = swap(grad_slices(normed, gz, 1 - core, dp), "dp", 1)
    branch[0].add()
    out_parts = scatter_rest(grad_slices(cots, gated, core, dp, out_sent))
    z_parts = scatter_rest(grad_slices(normed, gz, core, dp, z_sent))
    started = [part.send() for part in out_parts + z_parts]
    second_a = branch[0].send()
    run_leave(0, out_parts[0].x, z_parts[0].x)
    for part in out_parts:
        part.add()
        part.send()
    first_b = branch[1].send()
    first_gn = gn[0].send()
    run_leave(1, second_a, started[0], started[1], gn[0].x)
    for part in z_parts:
        part.add()
        part.send()
    gn[0].add()
    second_gn = gn[0].send()
    later = (started[2], started[3], out_parts[0].got, out_parts[1].got, first_gn, first_b)
    x_sent = swap(grad_slices(normed, [g_x_in[0], after(g_x_in[1], *later)], 1 - core, dp), "dp", 1)
    gn[1].send()
    x_parts = scatter_rest(grad_slices(normed, g_x_in, core, dp, x_sent))

    def join(parts):
        return jnp.concatenate([part.finish() for part in parts], 0)

    def end(scatter):
        if scatter.left:
            scatter.add()
        return scatter.finish()

    out_grad = jnp.concatenate([end(part) for part in out_parts], 0).T
    in_z_grad = jnp.concatenate([end(part) for part in z_parts], 0)
    in_x_grad = join(x_parts)
    outputs, input_grads = [], []
    for s in seqs:
        outputs.append((states_in[s].astype(f32) + end(branch[s])).astype(bf16))
        v = states_in[s].astype(f32)
        rscale = lax.rsqrt(jnp.mean(v * v, axis=1, keepdims=True) + norm_eps)
        scaled = end(gn[s]) * gain
        inner_mean = jnp.mean(scaled * v, axis=1, keepdims=True)
        input_grads.append(out_cotangent[s].astype(f32) + rscale * scaled - v * (rscale * rscale * rscale) * inner_mean)

    dt_grad = scatter_of(sum(dtg), "dp").finish()
    rows_sum = jnp.concatenate([sum(rows_part)[: span + 1], sum(small)[1::-1]], 0)
    packed = all_sum(jnp.concatenate([rows_sum, sum(proj_part), jnp.zeros((1, inner), f32)], 0), "dp")
    gain_grad = all_sum(all_sum(sum(gain_part)[0], "fsdp", f32), "dp", f32) / gain
    first = span + 3
    return (
        jnp.stack(outputs),
        jnp.stack(input_grads),
        gain_grad,
        in_x_grad,
        in_z_grad,
        packed[:span],
        packed[span],
        packed[first : first + proj_weight.shape[0]].T,
        dt_grad,
        packed[span + 1],
        packed[span + 2],
        out_grad,
    )


def solution(mesh):
    in_specs = (
        P("dp", "fsdp", None),
        P("dp", "fsdp", None),
        P("dp", None),
        P("dp", None),
        P(),
        P(None, "fsdp"),
        P(None, "fsdp"),
        P(None, "fsdp"),
        P("fsdp"),
        P("fsdp", None),
        P(None, "fsdp"),
        P("fsdp"),
        P("fsdp"),
        P("fsdp", None),
    )
    out_specs = (
        P("dp", "fsdp", None),
        P("dp", "fsdp", None),
        P(),
        P("dp", "fsdp"),
        P("dp", "fsdp"),
        P(None, "fsdp"),
        P("fsdp"),
        P("fsdp", None),
        P("dp", "fsdp"),
        P("fsdp"),
        P("fsdp"),
        P("fsdp", "dp"),
    )
    return jax.shard_map(per_device, mesh=mesh, in_specs=in_specs, out_specs=out_specs, check_vma=False)
```

time: 3020 us -> 345 us (0.11)
  waiting for transfers between devices: 1470 us -> 79.4 us
  other arithmetic: 854 us -> 29.5 us
  matrix products: 273 us -> 0 us
  blocking collectives: 221 us -> 0 us
  Pallas kernels: 0 us -> 129 us
  local copies, waits for them, and re-layouts: 165 us -> 39.9 us
  starting transfers between devices: 7.48 us -> 63.7 us
    all_gather x5 -> x0, waiting for transfers between devices: 782 us -> none  [the longest x1 270 us: per_device(): lax.all_gather(out_weight, 'fsdp', axis=0, tiled=True)]
    reduce_scatter x8 -> x0, waiting for transfers between devices: 626 us -> none  [the longest x1 205 us: per_device(): lax.psum_scatter(totals[8], 'dp', scatter_dimension=1, tiled=True)]
    reduce_sum x187 -> x1, other arithmetic: 407 us -> 1.48 us  [per_device(): rscale = lax.rsqrt(jnp.mean(v * v, axis=1, keepdims=True) + norm_eps)]
    dot_general x30 -> x0, matrix products: 273 us -> none  [the longest x10 133 us: rows_product(): lax.dot_general(left, right, (((0,), (0,)), ((), ())), preferred_element_...]
    mul x128 -> x0, other arithmetic: 203 us -> none  [the longest x8 89.9 us: reverse_block(): decay * (queries[position][:, None] * grad_mixed[position][None, :] + carry)]
    all_gather x10 -> x0, blocking collectives: 181 us -> none  [the longest x6 98.5 us: prefix(): lax.all_gather(a.astype(kind), axis)]
    add x27, other arithmetic: 189 us -> 15.8 us  [the longest x19 13.8 us: add(): self.x = self.kept.astype(f32) + self.got.astype(f32)]
    pallas_call x0 -> x12, Pallas kernels: none -> 129 us  [the longest x2 60 us: recurrence(): pl.pallas_call(functools.partial(recurrence_kernel, state_dim, rank, len(...]
  transfers between devices with their start and end apart: 18 -> 58, of which waited for: 14 -> 21; matrix products, arithmetic and copies ran while one was open for 26% -> 18% of each run, Pallas kernels for 0% -> 38%
where the time goes in v1:
time: 345 us; the launch traced here: 343 us
  Pallas kernels  129 us (37%)
  waiting for transfers between devices  79.4 us (23%)
  starting transfers between devices  63.7 us (18%)
  local copies, waits for them, and re-layouts  39.9 us (12%)
  other arithmetic  29.5 us (9%)
    ppermute x58, waiting for transfers between devices, swap(): lax.ppermute(x, axis, [(i, i ^ bit) for i in range(lax.axis_size(axis))])  79.4 us
    ppermute x58, starting transfers between devices, swap(): lax.ppermute(x, axis, [(i, i ^ bit) for i in range(lax.axis_size(axis))])  63.7 us
    pallas_call x2, Pallas kernels, recurrence(): pl.pallas_call(functools.partial(recurrence_kernel, state_dim, rank, len(...  60 us
    pallas_call x6, Pallas kernels, grad_slices(): pl.pallas_call(kernel, grid_spec=pltpu.PrefetchScalarGridSpec(num_scalar_...  30.5 us
    pallas_call x2, Pallas kernels, leave(): pl.pallas_call(functools.partial(leave_kernel, len(terms)), grid=(inner /...  20.2 us
    pallas_call x2, Pallas kernels, enter(): pl.pallas_call(functools.partial(enter_kernel, len(parts)), grid=(inner /...  18 us
    add x19, other arithmetic, add(): self.x = self.kept.astype(f32) + self.got.astype(f32)  13.8 us
    unnamed x110, local copies, waits for them, and re-layouts  7.56 us
  transfers between devices with their start and end apart: 58, of which 21 were waited for; matrix products, arithmetic and copies ran while one was open for 18% of the time, Pallas kernels for 38%

profile of v1, /device:TPU:0, one launch (start us, length us, event | category | flops | bytes accessed | tf_op | source)
XLA Modules:
  0.0 342.9 jit_solution(8447941686296687006)
XLA Ops:
  1.8 4.1 %collective-permute-start = (bf16[64,2048]{1,0:T(8,128)(2,1)S(1)}, bf16[64,2048]{1,0:T(8,128)(2,1)S(1)}, u32[]{:S(2)}, u32[]{:S(2)}) collective-permute-start(bf16[64,2048]{1,0:T(8,128)(2,1)S(1)} %get-tuple-element.121.refs_0_), channel_id=1, source_target_pairs={{0,2},{1,3},{2,0},{3,1},{4,6},{5,7},{6,4},{7,5},{8,10},{9,11},{10,... | collective-permute-start | bytes 786440 | tf_op jit(solution)/shard_map/ppermute | solution.py:22
  9.5 8.4 %collective-permute-done.refs_2_ = bf16[64,2048]{1,0:T(8,128)(2,1)S(1)} collective-permute-done((bf16[64,2048]{1,0:T(8,128)(2,1)S(1)}, bf16[64,2048]{1,0:T(8,128)(2,1)S(1)}, u32[]{:S(2)}, u32[]{:S(2)}) %collective-permute-start) | collective-permute-done | bytes 262176 | tf_op jit(solution)/shard_map/ppermute | solution.py:22
  20.1 4.0 %collective-permute-start.5 = (bf16[64,2048]{1,0:T(8,128)(2,1)S(1)}, bf16[64,2048]{1,0:T(8,128)(2,1)S(1)}, u32[]{:S(2)}, u32[]{:S(2)}) collective-permute-start(bf16[64,2048]{1,0:T(8,128)(2,1)S(1)} %collective-permute-done.refs_2_), channel_id=1, source_target_pairs={{0,1},{1,0},{2,3},{3,2},{4,5},{5,4},{6,7},{7,6},{8,9},{9,8},{10,11... | collective-permute-start | bytes 786440 | tf_op jit(solution)/shard_map/ppermute | solution.py:22
  24.1 8.0 %collective-permute-done.2.refs_2_ = bf16[64,2048]{1,0:T(8,128)(2,1)} collective-permute-done((bf16[64,2048]{1,0:T(8,128)(2,1)S(1)}, bf16[64,2048]{1,0:T(8,128)(2,1)}, u32[]{:S(2)}, u32[]{:S(2)}) %collective-permute-start.2) | collective-permute-done | bytes 262176 | tf_op jit(solution)/shard_map/ppermute | solution.py:22
  32.7 1.7 collective-permute-start.1
  35.5 9.0 %enter.2 = (bf16[256,2048]{1,0:T(8,128)(2,1)}, bf16[256,1024]{1,0:T(8,128)(2,1)}, f32[256,1024]{1,0:T(8,128)}, bf16[256,1024]{1,0:T(8,128)(2,1)}, bf16[160,256]{1,0:T(8,128)(2,1)}) custom-call(s32[1,4]{1,0:T(1,128)} %add_bitcast_fusion.offs_ref, bf16[64,2048]{1,0:T(8,128)(2,1)} %copy-done.20, bf16[64,2048]{1,0:T(8,128)(2,1)} %copy-done.29, ...), custom_call_target="tpu_custom_call" | custom-call | flops 2147483648 | bytes 11010048 | tf_op jit(solution)/shard_map/enter/pallas_call | solution.py:159
  44.5 1.8 collective-permute-start.6
  46.3 2.2 collective-permute-start.7
  51.5 9.3 %collective-permute-done.6.refs_5_ = bf16[160,256]{1,0:T(8,128)(2,1)S(1)} collective-permute-done((bf16[160,256]{1,0:T(8,128)(2,1)}, bf16[160,256]{1,0:T(8,128)(2,1)S(1)}, u32[]{:S(2)}, u32[]{:S(2)}) %collective-permute-start.6) | collective-permute-done | bytes 81952 | tf_op jit(solution)/shard_map/ppermute | solution.py:22
  61.3 1.8 collective-permute-start.16
  63.0 29.9 %recurrence.2 = (bf16[256,1024]{1,0:T(8,128)(2,1)}, bf16[256,1024]{1,0:T(8,128)(2,1)}, f32[256,1024]{1,0:T(8,128)}, bf16[160,256]{1,0:T(8,128)(2,1)}, f32[8,1024...) custom-call(f32[1,32]{1,0:T(1,128)} %get-tuple-element.130.keep_ref, ...), custom_call_target="tpu_custom_call" | custom-call | flops 2399141888 | bytes 9437184 | tf_op jit(solution)/shard_map/recurrence/pallas_call | solution.py:501
  98.4 9.0 %enter.3 = (bf16[256,2048]{1,0:T(8,128)(2,1)}, bf16[256,1024]{1,0:T(8,128)(2,1)}, f32[256,1024]{1,0:T(8,128)}, bf16[256,1024]{1,0:T(8,128)(2,1)}, bf16[160,256]{1,0:T(8,128)(2,1)}) custom-call(s32[1,4]{1,0:T(1,128)} %add_bitcast_fusion.offs_ref, bf16[64,2048]{1,0:T(8,128)(2,1)} %copy-done.19, bf16[64,2048]{1,0:T(8,128)(2,1)} %copy-done.30, ...), custom_call_target="tpu_custom_call" | custom-call | flops 2147483648 | bytes 11010048 | tf_op jit(solution)/shard_map/enter/pallas_call | solution.py:159
  108.0 2.8 collective-permute-start.18
  111.9 2.0 collective-permute-done.17.refs_5_
  114.3 3.0 collective-permute-done.19.refs_7_
  118.1 30.1 %recurrence.3 = (bf16[256,1024]{1,0:T(8,128)(2,1)}, bf16[256,1024]{1,0:T(8,128)(2,1)}, f32[256,1024]{1,0:T(8,128)}, bf16[160,256]{1,0:T(8,128)(2,1)}, f32[8,1024...) custom-call(f32[1,32]{1,0:T(1,128)} %get-tuple-element.131.keep_ref, ...), custom_call_target="tpu_custom_call" | custom-call | flops 2399141888 | bytes 9437184 | tf_op jit(solution)/shard_map/recurrence/pallas_call | solution.py:501
  149.0 4.9 %weight_grad.6 = bf16[4,256,1024]{2,1,0:T(8,128)(2,1)} custom-call(s32[1]{0:T(128)} %bitcast.31.place_ref, bf16[256,2048]{1,0:T(8,128)(2,1)} %get-tuple-element.68.la_ref, bf16[256,2048]{1,0:T(8,128)(2,1)} %get-tuple-element.69.lb_ref, bf16[256,1024]{1,0:T(8,128)(2,1)} %get-tuple-element.70.ra_ref, bf16[256,1024]{1,0:T(8,128)(2,1)} %get-tuple-element.72.rb_ref), custom_call_target="tpu_custom_call" | custom-call | flops 1073741824 | bytes 6291456 | tf_op jit(solution)/shard_map/weight_grad/pallas_call | solution.py:582
  155.6 4.9 %weight_grad.8 = bf16[4,256,1024]{2,1,0:T(8,128)(2,1)} custom-call(s32[1]{0:T(128)} %bitcast.31.place_ref, bf16[256,2048]{1,0:T(8,128)(2,1)} %get-tuple-element.73.la_ref.refs_14_, bf16[256,2048]{1,0:T(8,128)(2,1)} %get-tuple-element.74.lb_ref.refs_14_, bf16[256,1024]{1,0:T(8,128)(2,1)} %get-tuple-element.75.ra_ref.refs_8_, ...), custom_call_target="tpu_custom_call" | custom-call | flops 1073741824 | bytes 6291456 | tf_op jit(solution)/shard_map/weight_grad/pallas_call | solution.py:582
  160.5 1.9 dynamic-slice_bitcast_fusion.6
  165.8 2.4 collective-permute-done.56
  170.5 1.8 collective-permute-done.57
  172.3 2.2 collective-permute-start.23
  175.1 3.7 %collective-permute-done.20 = bf16[2,64,2048]{2,1,0:T(8,128)(2,1)} collective-permute-done((bf16[2,64,2048]{2,1,0:T(8,128)(2,1)}, bf16[2,64,2048]{2,1,0:T(8,128)(2,1)}, u32[]{:S(2)}, u32[]{:S(2)}) %collective-permute-start.20) | collective-permute-done | bytes 524320 | tf_op jit(solution)/shard_map/ppermute | solution.py:22
  184.2 5.3 %weight_grad.7 = bf16[4,256,1024]{2,1,0:T(8,128)(2,1)} custom-call(s32[1]{0:T(128)} %bitcast.30.place_ref, bf16[256,2048]{1,0:T(8,128)(2,1)} %get-tuple-element.68.la_ref, bf16[256,2048]{1,0:T(8,128)(2,1)} %get-tuple-element.69.lb_ref, bf16[256,1024]{1,0:T(8,128)(2,1)} %get-tuple-element.70.ra_ref, bf16[256,1024]{1,0:T(8,128)(2,1)} %get-tuple-element.72.rb_ref, ...), custom_call_target="tpu_custom_call" | custom-call | flops 1073741824 | bytes 6291456 | tf_op jit(solution)/shard_map/weight_grad/pallas_call | solution.py:582
  189.5 1.7 fusion.32
  193.1 2.1 collective-permute-start.30
  195.2 5.2 %weight_grad.9 = bf16[4,256,1024]{2,1,0:T(8,128)(2,1)} custom-call(s32[1]{0:T(128)} %bitcast.30.place_ref, bf16[256,2048]{1,0:T(8,128)(2,1)} %get-tuple-element.73.la_ref.refs_14_, bf16[256,2048]{1,0:T(8,128)(2,1)} %get-tuple-element.74.lb_ref.refs_14_, bf16[256,1024]{1,0:T(8,128)(2,1)} %get-tuple-element.75.ra_ref.refs_8_, ...), custom_call_target="tpu_custom_call" | custom-call | flops 1073741824 | bytes 6291456 | tf_op jit(solution)/shard_map/weight_grad/pallas_call | solution.py:582
  200.5 1.8 fusion.31
  203.4 2.0 copy.60
  206.2 1.7 collective-permute-start.32
  209.4 10.0 %leave.2 = (bf16[256,1024]{1,0:T(8,128)(2,1)}, bf16[256,2048]{1,0:T(8,128)(2,1)}, f32[8,1024]{1,0:T(8,128)}, f32[160,1024]{1,0:T(8,128)}, f32[1,2048]{1,0:T(1,128)}) custom-call(bf16[160,256]{1,0:T(8,128)(2,1)} %get-tuple-element.66.refs_0_, bf16[160,256]{1,0:T(8,128)(2,1)} %collective-permute-done.22.refs_1_, ...), custom_call_target="tpu_custom_call" | custom-call | flops 2147483648 | bytes 12058624 | tf_op jit(solution)/shard_map/leave/pallas_call | solution.py:244
  222.4 1.9 dynamic-slice_bitcast_fusion.5
  226.2 2.3 collective-permute-start.31
  230.3 6.0 %collective-permute-done.41 = bf16[2,128,1024]{2,1,0:T(8,128)(2,1)S(1)} collective-permute-done((bf16[2,128,1024]{2,1,0:T(8,128)(2,1)}, bf16[2,128,1024]{2,1,0:T(8,128)(2,1)S(1)}, u32[]{:S(2)}, u32[]{:S(2)}) %collective-permute-start.41) | collective-permute-done | bytes 524320 | tf_op jit(solution)/shard_map/ppermute | solution.py:22
  240.4 10.2 %leave.3 = (bf16[256,1024]{1,0:T(8,128)(2,1)}, bf16[256,2048]{1,0:T(8,128)(2,1)}, f32[8,1024]{1,0:T(8,128)}, f32[160,1024]{1,0:T(8,128)}, f32[1,2048]{1,0:T(1,128)}) custom-call(bf16[160,256]{1,0:T(8,128)(2,1)} %get-tuple-element.80.refs_0_, bf16[160,256]{1,0:T(8,128)(2,1)} %collective-permute-done.29.refs_1_, ...), custom_call_target="tpu_custom_call" | custom-call | flops 2147483648 | bytes 12058624 | tf_op jit(solution)/shard_map/leave/pallas_call | solution.py:244
  255.0 1.6 collective-permute-start.36
  258.7 2.6 collective-permute-start.37
  265.9 2.2 collective-permute-done.39
  269.8 2.0 collective-permute-done.40
  275.3 1.6 collective-permute-start.34
  278.1 2.6 collective-permute-start.28
  282.6 4.9 %weight_grad.10 = bf16[4,256,1024]{2,1,0:T(8,128)(2,1)} custom-call(s32[1]{0:T(128)} %bitcast.31.place_ref, bf16[256,2048]{1,0:T(8,128)(2,1)} %get-tuple-element.73.la_ref.refs_14_, bf16[256,2048]{1,0:T(8,128)(2,1)} %get-tuple-element.74.lb_ref.refs_14_, bf16[256,1024]{1,0:T(8,128)(2,1)} %get-tuple-element.87.ra_ref, bf16[256,1024]{1,0:T(8,128)(2,1)} %get-tuple-element.89.rb_ref), custom_call_target="tpu_custom_call" | custom-call | flops 1073741824 | bytes 6291456 | tf_op jit(solution)/shard_map/weight_grad/pallas_call | solution.py:582
  295.4 5.0 %collective-permute-done.53 = bf16[168,1024]{1,0:T(8,128)(2,1)S(1)} collective-permute-done((bf16[168,1024]{1,0:T(8,128)(2,1)S(1)}, bf16[168,1024]{1,0:T(8,128)(2,1)S(1)}, u32[]{:S(2)}, u32[]{:S(2)}) %collective-permute-start.53) | collective-permute-done | bytes 344096 | tf_op jit(solution)/shard_map/ppermute | solution.py:22
  301.5 6.0 %collective-permute-done.35 = bf16[64,2048]{1,0:T(8,128)(2,1)S(1)} collective-permute-done((bf16[64,2048]{1,0:T(8,128)(2,1)S(1)}, bf16[64,2048]{1,0:T(8,128)(2,1)S(1)}, u32[]{:S(2)}, u32[]{:S(2)}) %collective-permute-start.35) | collective-permute-done | bytes 262176 | tf_op jit(solution)/shard_map/ppermute | solution.py:22
  312.5 5.3 %weight_grad.11 = bf16[4,256,1024]{2,1,0:T(8,128)(2,1)} custom-call(s32[1]{0:T(128)} %bitcast.30.place_ref, bf16[256,2048]{1,0:T(8,128)(2,1)} %get-tuple-element.73.la_ref.refs_14_, bf16[256,2048]{1,0:T(8,128)(2,1)} %get-tuple-element.74.lb_ref.refs_14_, bf16[256,1024]{1,0:T(8,128)(2,1)} %get-tuple-element.87.ra_ref, ...), custom_call_target="tpu_custom_call" | custom-call | flops 1073741824 | bytes 6291456 | tf_op jit(solution)/shard_map/weight_grad/pallas_call | solution.py:582
  317.7 1.7 fusion.30
  322.3 11.0 %collective-permute-done.46 = bf16[2,128,1024]{2,1,0:T(8,128)(2,1)S(1)} collective-permute-done((bf16[2,128,1024]{2,1,0:T(8,128)(2,1)S(1)}, bf16[2,128,1024]{2,1,0:T(8,128)(2,1)S(1)}, u32[]{:S(2)}, u32[]{:S(2)}) %collective-permute-start.46) | collective-permute-done | bytes 524320 | tf_op jit(solution)/shard_map/ppermute | solution.py:22
  336.8 4.2 %collective-permute-done.47 = bf16[128,1024]{1,0:T(8,128)(2,1)S(1)} collective-permute-done((bf16[128,1024]{1,0:T(8,128)(2,1)S(1)}, bf16[128,1024]{1,0:T(8,128)(2,1)S(1)}, u32[]{:S(2)}, u32[]{:S(2)}) %collective-permute-start.47) | collective-permute-done | bytes 262176 | tf_op jit(solution)/shard_map/ppermute | solution.py:22
  (285 shorter events, 91.2 us)
Async XLA Ops:
  1.8 16.1 %collective-permute-start = (bf16[64,2048]{1,0:T(8,128)(2,1)S(1)}, bf16[64,2048]{1,0:T(8,128)(2,1)S(1)}, u32[]{:S(2)}, u32[]{:S(2)}) collective-permute-start(bf16[64,2048]{1,0:T(8,128)(2,1)S(1)} %get-tuple-element.121.refs_0_), channel_id=1, source_target_pairs={{0,2},{1,3},{2,0},{3,1},{4,6},{5,7},{6,4},{7,5},{8,10},{9,11},{10,... | collective-permute-start | bytes 786440 | tf_op jit(solution)/shard_map/ppermute | solution.py:22
  5.9 28.8 %collective-permute-start.4 = (bf16[64,2048]{1,0:T(8,128)(2,1)S(1)}, bf16[64,2048]{1,0:T(8,128)(2,1)S(1)}, u32[]{:S(2)}, u32[]{:S(2)}) collective-permute-start(bf16[64,2048]{1,0:T(8,128)(2,1)S(1)} %get-tuple-element.121.refs_0_), channel_id=1, source_target_pairs={{0,1},{1,0},{2,3},{3,2},{4,5},{5,4},{6,7},{7,6},{8,9},{9,8},{10,11... | collective-permute-start | bytes 786440 | tf_op jit(solution)/shard_map/ppermute | solution.py:22
  17.9 14.2 %collective-permute-start.2 = (bf16[64,2048]{1,0:T(8,128)(2,1)S(1)}, bf16[64,2048]{1,0:T(8,128)(2,1)}, u32[]{:S(2)}, u32[]{:S(2)}) collective-permute-start(bf16[64,2048]{1,0:T(8,128)(2,1)S(1)} %get-tuple-element.55.refs_0_), channel_id=1, source_target_pairs={{0,2},{1,3},{2,0},{3,1},{4,6},{5,7},{6,4},{7,5},{8,10},{9,11},{10,... | collective-permute-start | bytes 786440 | tf_op jit(solution)/shard_map/ppermute | solution.py:22
  20.1 14.6 %collective-permute-start.5 = (bf16[64,2048]{1,0:T(8,128)(2,1)S(1)}, bf16[64,2048]{1,0:T(8,128)(2,1)S(1)}, u32[]{:S(2)}, u32[]{:S(2)}) collective-permute-start(bf16[64,2048]{1,0:T(8,128)(2,1)S(1)} %collective-permute-done.refs_2_), channel_id=1, source_target_pairs={{0,1},{1,0},{2,3},{3,2},{4,5},{5,4},{6,7},{7,6},{8,9},{9,8},{10,11... | collective-permute-start | bytes 786440 | tf_op jit(solution)/shard_map/ppermute | solution.py:22
  32.1 16.5 %collective-permute-start.11 = (bf16[64,2048]{1,0:T(8,128)(2,1)S(1)}, bf16[64,2048]{1,0:T(8,128)(2,1)S(1)}, u32[]{:S(2)}, u32[]{:S(2)}) collective-permute-start(bf16[64,2048]{1,0:T(8,128)(2,1)S(1)} %get-tuple-element.60.refs_0_), channel_id=1, source_target_pairs={{0,2},{1,3},{2,0},{3,1},{4,6},{5,7},{6,4},{7,5},{8,10},{9,11},{10,... | collective-permute-start | bytes 786440 | tf_op jit(solution)/shard_map/ppermute | solution.py:22
  32.7 18.1 %collective-permute-start.1 = (bf16[64,2048]{1,0:T(8,128)(2,1)S(1)}, bf16[64,2048]{1,0:T(8,128)(2,1)}, u32[]{:S(2)}, u32[]{:S(2)}) collective-permute-start(bf16[64,2048]{1,0:T(8,128)(2,1)S(1)} %get-tuple-element.55.refs_0_), channel_id=1, source_target_pairs={{0,1},{1,0},{2,3},{3,2},{4,5},{5,4},{6,7},{7,6},{8,9},{9,8},{10,11... | collective-permute-start | bytes 786440 | tf_op jit(solution)/shard_map/ppermute | solution.py:22
  34.4 28.6 %collective-permute-start.3 = (bf16[64,2048]{1,0:T(8,128)(2,1)}, bf16[64,2048]{1,0:T(8,128)(2,1)}, u32[]{:S(2)}, u32[]{:S(2)}) collective-permute-start(bf16[64,2048]{1,0:T(8,128)(2,1)} %collective-permute-done.2.refs_2_), channel_id=1, source_target_pairs={{0,1},{1,0},{2,3},{3,2},{4,5},{5,4},{6,7},{7,6},{8,9},{9,8},{10,11... | collective-permute-start | bytes 786440 | tf_op jit(solution)/shard_map/ppermute | solution.py:22
  44.5 16.4 %collective-permute-start.6 = (bf16[160,256]{1,0:T(8,128)(2,1)}, bf16[160,256]{1,0:T(8,128)(2,1)S(1)}, u32[]{:S(2)}, u32[]{:S(2)}) collective-permute-start(bf16[160,256]{1,0:T(8,128)(2,1)} %get-tuple-element.56.refs_4_), channel_id=1, source_target_pairs={{0,1},{1,0},{2,3},{3,2},{4,5},{5,4},{6,7},{7,6},{8,9},{9,8},{10,11... | collective-permute-start | bytes 245768 | tf_op jit(solution)/shard_map/ppermute | solution.py:22
  46.3 14.6 %collective-permute-start.7 = (bf16[160,256]{1,0:T(8,128)(2,1)}, bf16[160,256]{1,0:T(8,128)(2,1)S(1)}, u32[]{:S(2)}, u32[]{:S(2)}) collective-permute-start(bf16[160,256]{1,0:T(8,128)(2,1)} %get-tuple-element.56.refs_4_), channel_id=1, source_target_pairs={{0,2},{1,3},{2,0},{3,1},{4,6},{5,7},{6,4},{7,5},{8,10},{9,11},{10,... | collective-permute-start | bytes 245768 | tf_op jit(solution)/shard_map/ppermute | solution.py:22
  48.6 12.7 %collective-permute-start.8 = (bf16[160,256]{1,0:T(8,128)(2,1)}, bf16[160,256]{1,0:T(8,128)(2,1)S(1)}, u32[]{:S(2)}, u32[]{:S(2)}) collective-permute-start(bf16[160,256]{1,0:T(8,128)(2,1)} %get-tuple-element.56.refs_4_), channel_id=1, source_target_pairs={{0,3},{1,2},{2,1},{3,0},{4,7},{5,6},{6,5},{7,4},{8,11},{9,10},{10,... | collective-permute-start | bytes 245768 | tf_op jit(solution)/shard_map/ppermute | solution.py:22
  50.8 46.2 %collective-permute-start.15 = (bf16[64,2048]{1,0:T(8,128)(2,1)S(1)}, bf16[64,2048]{1,0:T(8,128)(2,1)S(1)}, u32[]{:S(2)}, u32[]{:S(2)}) collective-permute-start(bf16[64,2048]{1,0:T(8,128)(2,1)S(1)} %get-tuple-element.60.refs_0_), channel_id=1, source_target_pairs={{0,1},{1,0},{2,3},{3,2},{4,5},{5,4},{6,7},{7,6},{8,9},{9,8},{10,11... | collective-permute-start | bytes 786440 | tf_op jit(solution)/shard_map/ppermute | solution.py:22
  60.9 34.6 %collective-permute-start.13 = (bf16[64,2048]{1,0:T(8,128)(2,1)S(1)}, bf16[64,2048]{1,0:T(8,128)(2,1)S(1)}, u32[]{:S(2)}, u32[]{:S(2)}) collective-permute-start(bf16[64,2048]{1,0:T(8,128)(2,1)S(1)} %get-tuple-element.61.refs_0_), channel_id=1, source_target_pairs={{0,2},{1,3},{2,0},{3,1},{4,6},{5,7},{6,4},{7,5},{8,10},{9,11},{10,... | collective-permute-start | bytes 786440 | tf_op jit(solution)/shard_map/ppermute | solution.py:22
  60.9 49.9 %collective-permute-start.12 = (bf16[64,2048]{1,0:T(8,128)(2,1)S(1)}, bf16[64,2048]{1,0:T(8,128)(2,1)S(1)}, u32[]{:S(2)}, u32[]{:S(2)}) collective-permute-start(bf16[64,2048]{1,0:T(8,128)(2,1)S(1)} %get-tuple-element.61.refs_0_), channel_id=1, source_target_pairs={{0,1},{1,0},{2,3},{3,2},{4,5},{5,4},{6,7},{7,6},{8,9},{9,8},{10,11... | collective-permute-start | bytes 786440 | tf_op jit(solution)/shard_map/ppermute | solution.py:22
  61.3 35.7 %collective-permute-start.16 = (bf16[64,2048]{1,0:T(8,128)(2,1)S(1)}, bf16[64,2048]{1,0:T(8,128)(2,1)S(1)}, u32[]{:S(2)}, u32[]{:S(2)}) collective-permute-start(bf16[64,2048]{1,0:T(8,128)(2,1)S(1)} %collective-permute-done.11.refs_2_), channel_id=1, source_target_pairs={{0,1},{1,0},{2,3},{3,2},{4,5},{5,4},{6,7},{7,6},{8,9},{9,8},{10,11... | collective-permute-start | bytes 786440 | tf_op jit(solution)/shard_map/ppermute | solution.py:22
  94.1 54.1 %collective-permute-start.9 = (bf16[2,64,2048]{2,1,0:T(8,128)(2,1)S(1)}, bf16[2,64,2048]{2,1,0:T(8,128)(2,1)S(1)}, u32[]{:S(2)}, u32[]{:S(2)}) collective-permute-start(bf16[2,64,2048]{2,1,0:T(8,128)(2,1)S(1)} %dynamic-slice_bitcast_fusion.7), channel_id=1, source_target_pairs={{0,1},{1,0},{2,3},{3,2},{4,5},{5,4},{6,7},{7,6},{8,9},{9,8},{10,11... | collective-permute-start | bytes 1572872 | tf_op jit(solution)/shard_map/ppermute | solution.py:22
  95.5 21.8 %collective-permute-start.14 = (bf16[64,2048]{1,0:T(8,128)(2,1)S(1)}, bf16[64,2048]{1,0:T(8,128)(2,1)S(1)}, u32[]{:S(2)}, u32[]{:S(2)}) collective-permute-start(bf16[64,2048]{1,0:T(8,128)(2,1)S(1)} %collective-permute-done.13.refs_2_), channel_id=1, source_target_pairs={{0,1},{1,0},{2,3},{3,2},{4,5},{5,4},{6,7},{7,6},{8,9},{9,8},{10,11... | collective-permute-start | bytes 786440 | tf_op jit(solution)/shard_map/ppermute | solution.py:22
  107.4 6.6 %collective-permute-start.17 = (bf16[160,256]{1,0:T(8,128)(2,1)}, bf16[160,256]{1,0:T(8,128)(2,1)S(1)}, u32[]{:S(2)}, u32[]{:S(2)}) collective-permute-start(bf16[160,256]{1,0:T(8,128)(2,1)} %get-tuple-element.62.refs_4_), channel_id=1, source_target_pairs={{0,1},{1,0},{2,3},{3,2},{4,5},{5,4},{6,7},{7,6},{8,9},{9,8},{10,11... | collective-permute-start | bytes 245768 | tf_op jit(solution)/shard_map/ppermute | solution.py:22
  114.0 91.4 %collective-permute-start.22 = (bf16[160,256]{1,0:T(8,128)(2,1)S(1)}, bf16[160,256]{1,0:T(8,128)(2,1)}, u32[]{:S(2)}, u32[]{:S(2)}) collective-permute-start(bf16[160,256]{1,0:T(8,128)(2,1)S(1)} %copy-done.35), channel_id=1, source_target_pairs={{0,1},{1,0},{2,3},{3,2},{4,5},{5,4},{6,7},{7,6},{8,9},{9,8},{10,11... | collective-permute-start | bytes 245768 | tf_op jit(solution)/shard_map/ppermute | solution.py:22
  153.9 29.0 %collective-permute-start.25 = (bf16[4,256,1024]{2,1,0:T(8,128)(2,1)}, bf16[4,256,1024]{2,1,0:T(8,128)(2,1)S(1)}, u32[]{:S(2)}, u32[]{:S(2)}) collective-permute-start(bf16[4,256,1024]{2,1,0:T(8,128)(2,1)} %weight_grad.6), channel_id=1, source_target_pairs={{0,4},{4,0},{8,12},{12,8},{16,20},{20,16},{24,28},{28,24},{1,5},{5... | collective-permute-start | bytes 6291464 | tf_op jit(solution)/shard_map/ppermute | solution.py:22
  155.0 8.6 %collective-permute-start.55 = (bf16[2,2,16,1024]{3,2,0,1:T(8,128)(2,1)S(1)}, bf16[2,2,16,1024]{3,2,0,1:T(8,128)(2,1)S(1)}, u32[]{:S(2)}, u32[]{:S(2)}) collective-permute-start(bf16[2,2,16,1024]{3,2,0,1:T(8,128)(2,1)S(1)} %fusion.26), channel_id=1, source_target_pairs={{0,4},{4,0},{8,12},{12,8},{16,20},{20,16},{24,28},{28,24},{1,5},{5... | collective-permute-start | bytes 393224 | tf_op jit(solution)/shard_map/ppermute | solution.py:22
  160.5 32.7 %collective-permute-start.26 = (bf16[4,256,1024]{2,1,0:T(8,128)(2,1)}, bf16[4,256,1024]{2,1,0:T(8,128)(2,1)}, u32[]{:S(2)}, u32[]{:S(2)}) collective-permute-start(bf16[4,256,1024]{2,1,0:T(8,128)(2,1)} %weight_grad.8), channel_id=1, source_target_pairs={{0,4},{4,0},{8,12},{12,8},{16,20},{20,16},{24,28},{28,24},{1,5},{5... | collective-permute-start | bytes 6291464 | tf_op jit(solution)/shard_map/ppermute | solution.py:22
  162.5 16.4 %collective-permute-start.20 = (bf16[2,64,2048]{2,1,0:T(8,128)(2,1)}, bf16[2,64,2048]{2,1,0:T(8,128)(2,1)}, u32[]{:S(2)}, u32[]{:S(2)}) collective-permute-start(bf16[2,64,2048]{2,1,0:T(8,128)(2,1)} %dynamic-slice_bitcast_fusion.6), channel_id=1, source_target_pairs={{0,1},{1,0},{2,3},{3,2},{4,5},{5,4},{6,7},{7,6},{8,9},{9,8},{10,11... | collective-permute-start | bytes 1572872 | tf_op jit(solution)/shard_map/ppermute | solution.py:22
  172.3 34.0 %collective-permute-start.23 = (bf16[160,256]{1,0:T(8,128)(2,1)S(1)}, bf16[160,256]{1,0:T(8,128)(2,1)}, u32[]{:S(2)}, u32[]{:S(2)}) collective-permute-start(bf16[160,256]{1,0:T(8,128)(2,1)S(1)} %copy-done.35), channel_id=1, source_target_pairs={{0,2},{1,3},{2,0},{3,1},{4,6},{5,7},{6,4},{7,5},{8,10},{9,11},{10,... | collective-permute-start | bytes 245768 | tf_op jit(solution)/shard_map/ppermute | solution.py:22
  178.8 29.1 %collective-permute-start.24 = (bf16[160,256]{1,0:T(8,128)(2,1)S(1)}, bf16[160,256]{1,0:T(8,128)(2,1)}, u32[]{:S(2)}, u32[]{:S(2)}) collective-permute-start(bf16[160,256]{1,0:T(8,128)(2,1)S(1)} %copy-done.35), channel_id=1, source_target_pairs={{0,3},{1,2},{2,1},{3,0},{4,7},{5,6},{6,5},{7,4},{8,11},{9,10},{10,... | collective-permute-start | bytes 245768 | tf_op jit(solution)/shard_map/ppermute | solution.py:22
  182.9 54.9 %collective-permute-start.29 = (bf16[160,256]{1,0:T(8,128)(2,1)}, bf16[160,256]{1,0:T(8,128)(2,1)}, u32[]{:S(2)}, u32[]{:S(2)}) collective-permute-start(bf16[160,256]{1,0:T(8,128)(2,1)} %get-tuple-element.80.refs_0_), channel_id=1, source_target_pairs={{0,1},{1,0},{2,3},{3,2},{4,5},{5,4},{6,7},{7,6},{8,9},{9,8},{10,11... | collective-permute-start | bytes 245768 | tf_op jit(solution)/shard_map/ppermute | solution.py:22
  193.1 45.1 %collective-permute-start.30 = (bf16[160,256]{1,0:T(8,128)(2,1)}, bf16[160,256]{1,0:T(8,128)(2,1)}, u32[]{:S(2)}, u32[]{:S(2)}) collective-permute-start(bf16[160,256]{1,0:T(8,128)(2,1)} %get-tuple-element.80.refs_0_), channel_id=1, source_target_pairs={{0,2},{1,3},{2,0},{3,1},{4,6},{5,7},{6,4},{7,5},{8,10},{9,11},{10,... | collective-permute-start | bytes 245768 | tf_op jit(solution)/shard_map/ppermute | solution.py:22
  205.4 20.8 %collective-permute-start.10 = (bf16[64,2048]{1,0:T(8,128)(2,1)}, bf16[64,2048]{1,0:T(8,128)(2,1)S(1)}, u32[]{:S(2)}, u32[]{:S(2)}) collective-permute-start(bf16[64,2048]{1,0:T(8,128)(2,1)} %fusion.14), channel_id=1, source_target_pairs={{0,2},{1,3},{2,0},{3,1},{4,6},{5,7},{6,4},{7,5},{8,10},{9,11},{10,... | collective-permute-start | bytes 786440 | tf_op jit(solution)/shard_map/ppermute | solution.py:22
  206.2 18.1 %collective-permute-start.32 = (bf16[2,128,1024]{1,2,0:T(8,128)(2,1)}, bf16[2,128,1024]{1,2,0:T(8,128)(2,1)}, u32[]{:S(2)}, u32[]{:S(2)}) collective-permute-start(bf16[2,128,1024]{1,2,0:T(8,128)(2,1)} %bitcast.230), channel_id=1, source_target_pairs={{0,8},{4,12},{8,0},{12,4},{16,24},{20,28},{24,16},{28,20},{1,9},{5... | collective-permute-start | bytes 1572872 | tf_op jit(solution)/shard_map/ppermute | solution.py:22
  207.9 20.5 %collective-permute-start.33 = (bf16[2,128,1024]{1,2,0:T(8,128)(2,1)}, bf16[2,128,1024]{1,2,0:T(8,128)(2,1)}, u32[]{:S(2)}, u32[]{:S(2)}) collective-permute-start(bf16[2,128,1024]{1,2,0:T(8,128)(2,1)} %bitcast.42), channel_id=1, source_target_pairs={{0,16},{4,20},{8,24},{12,28},{16,0},{20,4},{24,8},{28,12},{1,17},{... | collective-permute-start | bytes 1572872 | tf_op jit(solution)/shard_map/ppermute | solution.py:22
  224.3 12.0 %collective-permute-start.41 = (bf16[2,128,1024]{2,1,0:T(8,128)(2,1)}, bf16[2,128,1024]{2,1,0:T(8,128)(2,1)S(1)}, u32[]{:S(2)}, u32[]{:S(2)}) collective-permute-start(bf16[2,128,1024]{2,1,0:T(8,128)(2,1)} %dynamic-slice_bitcast_fusion.3), channel_id=1, source_target_pairs={{0,8},{4,12},{8,0},{12,4},{16,24},{20,28},{24,16},{28,20},{1,9},{5... | collective-permute-start | bytes 1572872 | tf_op jit(solution)/shard_map/ppermute | solution.py:22
  226.2 13.6 %collective-permute-start.31 = (bf16[160,256]{1,0:T(8,128)(2,1)}, bf16[160,256]{1,0:T(8,128)(2,1)S(1)}, u32[]{:S(2)}, u32[]{:S(2)}) collective-permute-start(bf16[160,256]{1,0:T(8,128)(2,1)} %get-tuple-element.80.refs_0_), channel_id=1, source_target_pairs={{0,3},{1,2},{2,1},{3,0},{4,7},{5,6},{6,5},{7,4},{8,11},{9,10},{10,... | collective-permute-start | bytes 245768 | tf_op jit(solution)/shard_map/ppermute | solution.py:22
  228.4 80.6 %collective-permute-start.21 = (bf16[64,2048]{1,0:T(8,128)(2,1)}, bf16[64,2048]{1,0:T(8,128)(2,1)}, u32[]{:S(2)}, u32[]{:S(2)}) collective-permute-start(bf16[64,2048]{1,0:T(8,128)(2,1)} %fusion.15), channel_id=1, source_target_pairs={{0,2},{1,3},{2,0},{3,1},{4,6},{5,7},{6,4},{7,5},{8,10},{9,11},{10,... | collective-permute-start | bytes 786440 | tf_op jit(solution)/shard_map/ppermute | solution.py:22
  236.3 18.6 %collective-permute-start.42 = (bf16[2,128,1024]{2,1,0:T(8,128)(2,1)}, bf16[2,128,1024]{2,1,0:T(8,128)(2,1)}, u32[]{:S(2)}, u32[]{:S(2)}) collective-permute-start(bf16[2,128,1024]{2,1,0:T(8,128)(2,1)} %dynamic-slice_bitcast_fusion.2), channel_id=1, source_target_pairs={{0,16},{4,20},{8,24},{12,28},{16,0},{20,4},{24,8},{28,12},{1,17},{... | collective-permute-start | bytes 1572872 | tf_op jit(solution)/shard_map/ppermute | solution.py:22
  237.8 15.8 %collective-permute-start.27 = (bf16[2,64,2048]{2,1,0:T(8,128)(2,1)}, bf16[2,64,2048]{2,1,0:T(8,128)(2,1)}, u32[]{:S(2)}, u32[]{:S(2)}) collective-permute-start(bf16[2,64,2048]{2,1,0:T(8,128)(2,1)} %dynamic-slice_bitcast_fusion.5), channel_id=1, source_target_pairs={{0,1},{1,0},{2,3},{3,2},{4,5},{5,4},{6,7},{7,6},{8,9},{9,8},{10,11... | collective-permute-start | bytes 1572872 | tf_op jit(solution)/shard_map/ppermute | solution.py:22
  238.3 35.0 %collective-permute-start.43 = (bf16[128,1024]{0,1:T(8,128)(2,1)}, bf16[128,1024]{0,1:T(8,128)(2,1)}, u32[]{:S(2)}, u32[]{:S(2)}) collective-permute-start(bf16[128,1024]{0,1:T(8,128)(2,1)} %fusion.18), channel_id=1, source_target_pairs={{0,16},{4,20},{8,24},{12,28},{16,0},{20,4},{24,8},{28,12},{1,17},{... | collective-permute-start | bytes 786440 | tf_op jit(solution)/shard_map/ppermute | solution.py:22
  239.8 35.5 %collective-permute-start.44 = (bf16[128,1024]{0,1:T(8,128)(2,1)}, bf16[128,1024]{0,1:T(8,128)(2,1)}, u32[]{:S(2)}, u32[]{:S(2)}) collective-permute-start(bf16[128,1024]{0,1:T(8,128)(2,1)} %fusion.19), channel_id=1, source_target_pairs={{0,8},{4,12},{8,0},{12,4},{16,24},{20,28},{24,16},{28,20},{1,9},{5... | collective-permute-start | bytes 786440 | tf_op jit(solution)/shard_map/ppermute | solution.py:22
  253.6 35.1 %collective-permute-start.52 = (bf16[168,1024]{1,0:T(8,128)(2,1)}, bf16[168,1024]{1,0:T(8,128)(2,1)}, u32[]{:S(2)}, u32[]{:S(2)}) collective-permute-start(bf16[168,1024]{1,0:T(8,128)(2,1)} %maximum_maximum_fusion), channel_id=1, source_target_pairs={{0,4},{4,0},{8,12},{12,8},{16,20},{20,16},{24,28},{28,24},{1,5},{5... | collective-permute-start | bytes 1032200 | tf_op jit(solution)/shard_map/ppermute | solution.py:22
  273.3 14.3 %collective-permute-start.51 = (bf16[128,1024]{1,0:T(8,128)(2,1)}, bf16[128,1024]{1,0:T(8,128)(2,1)}, u32[]{:S(2)}, u32[]{:S(2)}) collective-permute-start(bf16[128,1024]{1,0:T(8,128)(2,1)} %fusion.23), channel_id=1, source_target_pairs={{0,8},{4,12},{8,0},{12,4},{16,24},{20,28},{24,16},{28,20},{1,9},{5... | collective-permute-start | bytes 786440 | tf_op jit(solution)/shard_map/ppermute | solution.py:22
  275.3 17.1 %collective-permute-start.34 = (bf16[2,64,2048]{2,1,0:T(8,128)(2,1)}, bf16[2,64,2048]{2,1,0:T(8,128)(2,1)}, u32[]{:S(2)}, u32[]{:S(2)}) collective-permute-start(bf16[2,64,2048]{2,1,0:T(8,128)(2,1)} %dynamic-slice_bitcast_fusion.4), channel_id=1, source_target_pairs={{0,1},{1,0},{2,3},{3,2},{4,5},{5,4},{6,7},{7,6},{8,9},{9,8},{10,11... | collective-permute-start | bytes 1572872 | tf_op jit(solution)/shard_map/ppermute | solution.py:22
  278.1 23.4 %collective-permute-start.28 = (bf16[64,2048]{1,0:T(8,128)(2,1)}, bf16[64,2048]{1,0:T(8,128)(2,1)}, u32[]{:S(2)}, u32[]{:S(2)}) collective-permute-start(bf16[64,2048]{1,0:T(8,128)(2,1)} %fusion.16), channel_id=1, source_target_pairs={{0,2},{1,3},{2,0},{3,1},{4,6},{5,7},{6,4},{7,5},{8,10},{9,11},{10,... | collective-permute-start | bytes 786440 | tf_op jit(solution)/shard_map/ppermute | solution.py:22
  287.5 24.9 %collective-permute-start.45 = (bf16[4,256,1024]{2,1,0:T(8,128)(2,1)}, bf16[4,256,1024]{2,1,0:T(8,128)(2,1)}, u32[]{:S(2)}, u32[]{:S(2)}) collective-permute-start(bf16[4,256,1024]{2,1,0:T(8,128)(2,1)} %weight_grad.10), channel_id=1, source_target_pairs={{0,4},{4,0},{8,12},{12,8},{16,20},{20,16},{24,28},{28,24},{1,5},{5... | collective-permute-start | bytes 6291464 | tf_op jit(solution)/shard_map/ppermute | solution.py:22
  289.9 10.5 %collective-permute-start.53 = (bf16[168,1024]{1,0:T(8,128)(2,1)S(1)}, bf16[168,1024]{1,0:T(8,128)(2,1)S(1)}, u32[]{:S(2)}, u32[]{:S(2)}) collective-permute-start(bf16[168,1024]{1,0:T(8,128)(2,1)S(1)} %add_convert_fusion.1), channel_id=1, source_target_pairs={{0,8},{4,12},{8,0},{12,4},{16,24},{20,28},{24,16},{28,20},{1,9},{5... | collective-permute-start | bytes 1032200 | tf_op jit(solution)/shard_map/ppermute | solution.py:22
  293.7 13.8 %collective-permute-start.35 = (bf16[64,2048]{1,0:T(8,128)(2,1)S(1)}, bf16[64,2048]{1,0:T(8,128)(2,1)S(1)}, u32[]{:S(2)}, u32[]{:S(2)}) collective-permute-start(bf16[64,2048]{1,0:T(8,128)(2,1)S(1)} %fusion.17), channel_id=1, source_target_pairs={{0,2},{1,3},{2,0},{3,1},{4,6},{5,7},{6,4},{7,5},{8,10},{9,11},{10,... | collective-permute-start | bytes 786440 | tf_op jit(solution)/shard_map/ppermute | solution.py:22
  300.5 19.7 %collective-permute-start.54 = (bf16[168,1024]{1,0:T(8,128)(2,1)S(1)}, bf16[168,1024]{1,0:T(8,128)(2,1)S(1)}, u32[]{:S(2)}, u32[]{:S(2)}) collective-permute-start(bf16[168,1024]{1,0:T(8,128)(2,1)S(1)} %add_convert_fusion), channel_id=1, source_target_pairs={{0,16},{4,20},{8,24},{12,28},{16,0},{20,4},{24,8},{28,12},{1,17},{... | collective-permute-start | bytes 1032200 | tf_op jit(solution)/shard_map/ppermute | solution.py:22
  319.5 13.9 %collective-permute-start.46 = (bf16[2,128,1024]{2,1,0:T(8,128)(2,1)S(1)}, bf16[2,128,1024]{2,1,0:T(8,128)(2,1)S(1)}, u32[]{:S(2)}, u32[]{:S(2)}) collective-permute-start(bf16[2,128,1024]{2,1,0:T(8,128)(2,1)S(1)} %dynamic-slice_bitcast_fusion.1), channel_id=1, source_target_pairs={{0,8},{4,12},{8,0},{12,4},{16,24},{20,28},{24,16},{28,20},{1,9},{5... | collective-permute-start | bytes 1572872 | tf_op jit(solution)/shard_map/ppermute | solution.py:22
  320.4 14.0 %collective-permute-start.48 = (bf16[2,128,1024]{2,1,0:T(8,128)(2,1)S(1)}, bf16[2,128,1024]{2,1,0:T(8,128)(2,1)S(1)}, u32[]{:S(2)}, u32[]{:S(2)}) collective-permute-start(bf16[2,128,1024]{2,1,0:T(8,128)(2,1)S(1)} %dynamic-slice_bitcast_fusion), channel_id=1, source_target_pairs={{0,16},{4,20},{8,24},{12,28},{16,0},{20,4},{24,8},{28,12},{1,17},{... | collective-permute-start | bytes 1572872 | tf_op jit(solution)/shard_map/ppermute | solution.py:22
  333.6 7.4 %collective-permute-start.47 = (bf16[128,1024]{1,0:T(8,128)(2,1)S(1)}, bf16[128,1024]{1,0:T(8,128)(2,1)S(1)}, u32[]{:S(2)}, u32[]{:S(2)}) collective-permute-start(bf16[128,1024]{1,0:T(8,128)(2,1)S(1)} %fusion.20), channel_id=1, source_target_pairs={{0,16},{4,20},{8,24},{12,28},{16,0},{20,4},{24,8},{28,12},{1,17},{... | collective-permute-start | bytes 786440 | tf_op jit(solution)/shard_map/ppermute | solution.py:22
  334.6 7.2 %collective-permute-start.49 = (bf16[128,1024]{1,0:T(8,128)(2,1)S(1)}, bf16[128,1024]{1,0:T(8,128)(2,1)S(1)}, u32[]{:S(2)}, u32[]{:S(2)}) collective-permute-start(bf16[128,1024]{1,0:T(8,128)(2,1)S(1)} %fusion.21), channel_id=1, source_target_pairs={{0,8},{4,12},{8,0},{12,4},{16,24},{20,28},{24,16},{28,20},{1,9},{5... | collective-permute-start | bytes 786440 | tf_op jit(solution)/shard_map/ppermute | solution.py:22
  (64 other events, 702.3 us)

commit v2 on v1

--- a/solution.py
+++ b/solution.py
@@ -10,6 +10,10 @@
 BLOCK = 16
 LANES = 128
 norm_eps = 1e-05
+
+
+def takes(microseconds):
+    return pl.CostEstimate(flops=int(microseconds * 9e8), bytes_accessed=1, transcendentals=0)
 f32 = jnp.float32
 bf16 = jnp.bfloat16
 
@@ -26,12 +30,46 @@
     return [1 << k for k in range(count.bit_length() - 1)]
 
 
-def gather_parts(x, axis):
+def exchange_all(x, axis):
+    return [x] + [swap(x, axis, mask) for mask in range(1, lax.axis_size(axis))]
+
+
+def relay_all(x, axis):
     held = {0: x}
     for bit in reversed(bits_of(lax.axis_size(axis))):
         for mask in list(held):
             held[mask | bit] = swap(held[mask], axis, bit)
     return [held[mask] for mask in range(len(held))]
+
+
+class RowScatter:
+    def __init__(self, sent, kept, axis):
+        self.axis, self.bits = axis, bits_of(lax.axis_size(axis))
+        self.sent, self.kept = sent, kept
+
+    def send(self, *behind):
+        self.got = swap(after(self.sent, *behind), self.axis, self.bits.pop(0))
+
+    def mid(self):
+        self.sent = (self.kept[1::2].astype(f32) + self.got[1::2].astype(f32)).astype(bf16)
+        self.kept = (self.kept[0::2].astype(f32) + self.got[0::2].astype(f32))
+
+    def finish(self):
+        while self.bits:
+            self.mid()
+            self.send()
+        return self.kept[0].astype(f32) + self.got[0].astype(f32)
+
+
+def after(x, *others):
+    return lax.optimization_barrier((x, others))[0] if others else x
+
+
+def sum_pair(x, axis):
+    bits = bits_of(lax.axis_size(axis))
+    for bit in bits[:-1]:
+        x = (x.astype(f32) + swap(x, axis, bit).astype(f32)).astype(bf16)
+    return [x, swap(x, axis, bits[-1])]
 
 
 def take_bit(x, dim, value):
@@ -68,17 +106,6 @@
     return Scatter(x.reshape((2,) * n + (x.shape[0] // count,) + x.shape[1:]), axis, bits, range(n - 1, -1, -1))
 
 
-def scatter_rest(x):
-    bits = bits_of(lax.axis_size("dp"))[1:]
-    n = len(bits)
-    half = x.shape[1] // 2
-    parts = []
-    for start, order in ((0, list(range(n))), (half, list(range(n))[::-1])):
-        piece = x[:, start : start + half].reshape((2,) * n + (half,) + x.shape[2:])
-        parts.append(Scatter(piece, "dp", [bits[k] for k in order], [n - 1 - k for k in order]))
-    return parts
-
-
 def all_sum(x, axis, kind=bf16):
     for bit in bits_of(lax.axis_size(axis)):
         low = x.astype(kind)
@@ -86,8 +113,8 @@
     return x
 
 
-def exchange_all(x, axis):
-    return [x] + [swap(x, axis, mask) for mask in range(1, lax.axis_size(axis))]
+def far(x):
+    return pltpu.with_memory_space_constraint(x, pltpu.HBM)
 
 
 def add_up(refs):
@@ -186,20 +213,26 @@
         ],
         scratch_shapes=[pltpu.VMEM((wp.shape[0], seq_len), f32)],
         name="enter",
-        cost_estimate=pl.CostEstimate(
-            flops=4 * seq_len * model * inner,
-            bytes_accessed=4 * model * inner + 10 * seq_len * inner,
-            transcendentals=seq_len * inner,
-        ),
+        compiler_params=pltpu.CompilerParams(vmem_limit_bytes=20 * 1024 * 1024),
+        cost_estimate=takes(9),
     )(offs, *parts, gain, masks, wx, wz, taps, bias, wp)
 
 
-def leave_kernel(count, *refs):
+def write_parts(offs_ref, total_s, sent_ref, kept_ref):
+    count, rows = kept_ref.shape[0], kept_ref.shape[1]
+    for m in range(count):
+        for odd, out in ((0, kept_ref), (1, sent_ref)):
+            off = pl.multiple_of(offs_ref[0, 2 * m + odd], rows)
+            out[m] = total_s[pl.ds(off, rows), :].astype(bf16)
+
+
+def leave_kernel(count, offs_ref, *refs):
     terms = refs[:count]
     wp_ref, gxs_ref, xin_ref, xs_ref, gz_ref, mask_ref, taps_ref, bias_ref, wx_ref, wz_ref, normed_ref = refs[
         count : count + 11
     ]
-    gxin_ref, gn_ref, rows_ref, xpg_ref, gain_ref, acc_s = refs[count + 11 :]
+    gxin_ref, rows_ref, xpg_ref, gain_ref = refs[count + 11 : count + 15]
+    sent_ref, kept_ref, acc_s = refs[count + 15 :]
     step = pl.program_id(0)
     span = taps_ref.shape[0]
     seq_len = xin_ref.shape[0]
@@ -233,18 +266,20 @@
     @pl.when(step == pl.num_programs(0) - 1)
     def _():
         gn = acc_s[...]
-        gn_ref[...] = gn.astype(bf16)
+        write_parts(offs_ref, acc_s, sent_ref, kept_ref)
         gain_ref[...] = jnp.sum(gn * normed_ref[...].astype(f32), axis=0, keepdims=True)
 
 
-def leave(terms, wp, gxs, xin, xs, gz, masks, taps, bias, wx, wz, normed):
+def leave(offs, terms, wp, gxs, xin, xs, gz, masks, taps, bias, wx, wz, normed):
     seq_len, model = normed.shape
     inner = wx.shape[1]
+    count = offs.shape[1]
     wide = 256
     return pl.pallas_call(
         functools.partial(leave_kernel, len(terms)),
         grid=(inner // wide,),
-        in_specs=[whole_of(terms[0].shape)] * len(terms)
+        in_specs=[pl.BlockSpec(memory_space=pltpu.SMEM)]
+        + [whole_of(terms[0].shape)] * len(terms)
         + [
             blocks_of(wp.shape[0], wide),
             blocks_of(seq_len, wide),
@@ -260,32 +295,29 @@
         ],
         out_specs=[
             blocks_of(seq_len, wide),
-            whole_of((seq_len, model)),
             blocks_of(8, wide),
             blocks_of(wp.shape[0], wide),
             whole_of((1, model)),
-        ],
+        ]
+        + [whole_of((count // 2, seq_len // count, model))] * 2,
         out_shape=[
             jax.ShapeDtypeStruct((seq_len, inner), bf16),
-            jax.ShapeDtypeStruct((seq_len, model), bf16),
             jax.ShapeDtypeStruct((8, inner), f32),
             jax.ShapeDtypeStruct((wp.shape[0], inner), f32),
             jax.ShapeDtypeStruct((1, model), f32),
-        ],
+        ]
+        + [jax.ShapeDtypeStruct((count // 2, seq_len // count, model), bf16)] * 2,
         scratch_shapes=[pltpu.VMEM((seq_len, model), f32)],
         name="leave",
-        cost_estimate=pl.CostEstimate(
-            flops=4 * seq_len * model * inner,
-            bytes_accessed=4 * model * inner + 14 * seq_len * inner,
-            transcendentals=seq_len * inner,
-        ),
-    )(*terms, wp, gxs, xin, xs, gz, masks, taps, bias, wx, wz, normed)
+        compiler_params=pltpu.CompilerParams(vmem_limit_bytes=24 * 1024 * 1024),
+        cost_estimate=takes(10),
+    )(offs, *terms, wp, gxs, xin, xs, gz, masks, taps, bias, wx, wz, normed)
 
 
 def recurrence_kernel(state_dim, rank, count, keep_ref, offs_ref, *refs):
-    parts, terms = refs[:count], refs[count : 2 * count]
-    xs_ref, z_ref, wo_ref, wdt_ref, dtb_ref, skip_ref = refs[2 * count : 2 * count + 6]
-    gated_ref, gz_ref, gxs_ref, gproj_ref, small_ref, dtg_ref, cot_ref, out_ref = refs[2 * count + 6 : 2 * count + 14]
+    parts, terms, refs = refs[:count], refs[count : count + 2], refs[count + 2 :]
+    xs_ref, z_ref, wo_ref, wdt_ref, dtb_ref, skip_ref = refs[:6]
+    gated_ref, gz_ref, gxs_ref, gproj_ref, small_ref, dtg_ref, cot_ref, sent_ref, kept_ref = refs[6:15]
     (
         gg_s,
         proj_s,
@@ -317,7 +349,7 @@
         gqt_s,
         get_s,
         pet_s,
-    ) = refs[2 * count + 14 :]
+    ) = refs[15:]
     step = pl.program_id(0)
     seq_len, width = xs_ref.shape
     blocks = seq_len // BLOCK
@@ -485,7 +517,7 @@
             tail_s[state_dim:, cols] = gq_s[b, :, :BLOCK]
         gproj_ref[:rank, :] = gproj_s[...].astype(bf16)
         gproj_ref[rank:, :] = tail_s[...].astype(bf16)
-        out_ref[...] = acc_s[...].astype(bf16)
+        write_parts(offs_ref, acc_s, sent_ref, kept_ref)
 
 
 def recurrence(keep, offs, parts, terms, xs, z, wo, wdt, dt_bias, skip):
@@ -520,8 +552,8 @@
             blocks_of(8, wide),
             blocks_of(rank, wide),
             whole_of((seq_len, model)),
-            whole_of((seq_len, model)),
-        ],
+        ]
+        + [whole_of((len(parts) // 2,) + parts[0].shape)] * 2,
         out_shape=[
             jax.ShapeDtypeStruct((seq_len, inner), bf16),
             jax.ShapeDtypeStruct((seq_len, inner), bf16),
@@ -530,8 +562,8 @@
             jax.ShapeDtypeStruct((8, inner), f32),
             jax.ShapeDtypeStruct((rank, inner), f32),
             jax.ShapeDtypeStruct((seq_len, model), bf16),
-            jax.ShapeDtypeStruct((seq_len, model), bf16),
-        ],
+        ]
+        + [jax.ShapeDtypeStruct((len(parts) // 2,) + parts[0].shape, bf16)] * 2,
         scratch_shapes=[
             vmem((seq_len, wide), f32),
             vmem((columns, seq_len), f32),
@@ -548,57 +580,188 @@
         + [vmem((2 * state_dim, seq_len), f32)]
         + [vmem((blocks, state_dim, LANES), f32)] * 6,
         name="recurrence",
-        cost_estimate=pl.CostEstimate(
-            flops=60 * seq_len * state_dim * inner + 4 * seq_len * model * inner,
-            bytes_accessed=2 * model * inner + 20 * seq_len * inner,
-            transcendentals=6 * seq_len * inner,
-        ),
+        compiler_params=pltpu.CompilerParams(vmem_limit_bytes=30 * 1024 * 1024),
+        cost_estimate=takes(30),
     )(keep, offs, *parts, *terms, xs, z, wo, wdt, dt_bias, skip)
 
 
-def grad_kernel(place_ref, la_ref, lb_ref, ra_ref, rb_ref, out_ref):
-    out_ref[0] = (mm(la_ref[...], ra_ref[...], (0, 0)) + mm(lb_ref[...], rb_ref[...], (0, 0))).astype(bf16)
-
-
-def grad_add_kernel(place_ref, la_ref, lb_ref, ra_ref, rb_ref, got_ref, out_ref):
-    total = mm(la_ref[...], ra_ref[...], (0, 0)) + mm(lb_ref[...], rb_ref[...], (0, 0))
-    out_ref[0] = (total + got_ref[0].astype(f32)).astype(bf16)
-
-
-def grad_slices(left, right, own, parts, got=None):
-    seq_len, model = left[0].shape
-    inner = right[0].shape[1]
-    rows = model // parts
-    if rows % LANES:
-        total = sum(mm(a, b, (0, 0)) for a, b in zip(left, right)).reshape(parts // 2, 2, rows, inner)
-        total = take_bit(total, 1, own)
-        return (total if got is None else total + got.astype(f32)).astype(bf16)
-    place = own.reshape(1).astype(jnp.int32)
-    lhs = pl.BlockSpec((seq_len, rows), lambda j, place: (0, 2 * j + place[0]))
-    rhs = pl.BlockSpec((seq_len, inner), lambda j, place: (0, 0))
-    block = pl.BlockSpec((1, rows, inner), lambda j, place: (j, 0, 0))
-    kernel = grad_kernel if got is None else grad_add_kernel
-    extra = () if got is None else (got,)
-    return pl.pallas_call(
-        kernel,
-        grid_spec=pltpu.PrefetchScalarGridSpec(
-            num_scalar_prefetch=1,
-            grid=(parts // 2,),
-            in_specs=[lhs, lhs, rhs, rhs] + [block] * len(extra),
-            out_specs=block,
-        ),
-        out_shape=jax.ShapeDtypeStruct((parts // 2, rows, inner), bf16),
-        name="weight_grad",
-        cost_estimate=pl.CostEstimate(
-            flops=2 * seq_len * model * inner,
-            bytes_accessed=2 * seq_len * (model + 2 * inner) + 2 * model * inner,
-            transcendentals=0,
-        ),
-    )(place, *left, *right, *extra)
-
-
-def after(x, *others):
-    return lax.optimization_barrier((x, others))[0]
+def grad_of(lefts, rights):
+    total = mm(lefts[0][...], rights[0][...], (0, 0))
+    for left, right in zip(lefts[1:], rights[1:]):
+        total = total + mm(left[...], right[...], (0, 0))
+    return total
+
+
+def grad_send_kernel(pairs, count, place_ref, *refs):
+    out_ref = refs[2 * pairs * count]
+    for g in range(pairs):
+        lefts = refs[g * count : (g + 1) * count]
+        rights = refs[(pairs + g) * count : (pairs + g + 1) * count]
+        out_ref[g, 0] = grad_of(lefts, rights).astype(bf16)
+
+
+def grad_keep_kernel(pairs, count, place_ref, *refs):
+    got_ref, t1_ref, k1_ref, t2_ref, k2_ref = refs[2 * pairs * count :]
+    half = t1_ref.shape[2]
+    own_y = pl.program_id(0) == 1
+    own_x = pl.program_id(1) == 1
+    for g in range(pairs):
+        lefts = refs[g * count : (g + 1) * count]
+        rights = refs[(pairs + g) * count : (pairs + g + 1) * count]
+        total = (grad_of(lefts, rights) + got_ref[g, 0].astype(f32)).astype(bf16)
+
+        @pl.when(own_x)
+        def _():
+            k1_ref[g, 0] = total[:half]
+
+        @pl.when(jnp.logical_not(own_x))
+        def _():
+            t1_ref[g, 0] = total[:half]
+
+        @pl.when(own_y)
+        def _():
+            k2_ref[g, 0] = total[half:]
+
+        @pl.when(jnp.logical_not(own_y))
+        def _():
+            t2_ref[g, 0] = total[half:]
+
+
+def grad_mid_kernel(place_ref, k1_ref, g1_ref, k2_ref, g2_ref, o1_ref, m1_ref, o2_ref, m2_ref):
+    x, y = place_ref[1], place_ref[2]
+    for g in range(k1_ref.shape[0]):
+        for kept, got, out, mine, own in (
+            (k1_ref, g1_ref, o1_ref, m1_ref, y),
+            (k2_ref, g2_ref, o2_ref, m2_ref, x),
+        ):
+            out[g] = (kept[g, 1 - own].astype(f32) + got[g, 1 - own].astype(f32)).astype(bf16)
+            mine[g] = kept[g, own].astype(f32) + got[g, own].astype(f32)
+
+
+class GradScatter:
+    def __init__(self, lefts, rights, place):
+        self.lefts, self.rights, self.place = lefts, rights, place
+        self.pairs, self.count = len(lefts), len(lefts[0])
+        self.flat = [a for pair in lefts for a in pair] + [a for pair in rights for a in pair]
+        seq_len, model = lefts[0][0].shape
+        self.inner = rights[0][0].shape[1]
+        self.seq_len, self.rows = seq_len, model // 8
+
+    def specs(self, index):
+        n = self.pairs * self.count
+        lhs = pl.BlockSpec((self.seq_len, self.rows), index)
+        rhs = pl.BlockSpec((self.seq_len, self.inner), lambda *_: (0, 0))
+        return [lhs] * n + [rhs] * n
+
+    def send_core(self):
+        self.got = swap(
+            pl.pallas_call(
+                functools.partial(grad_send_kernel, self.pairs, self.count),
+                grid_spec=pltpu.PrefetchScalarGridSpec(
+                    num_scalar_prefetch=1,
+                    grid=(4,),
+                    in_specs=self.specs(lambda j, place: (0, 2 * j + 1 - place[0])),
+                    out_specs=pl.BlockSpec((self.pairs, 1, self.rows, self.inner), lambda j, place: (0, j, 0, 0)),
+                ),
+                out_shape=jax.ShapeDtypeStruct((self.pairs, 4, self.rows, self.inner), bf16),
+                name="grad_send",
+            compiler_params=pltpu.CompilerParams(vmem_limit_bytes=12 * 1024 * 1024),
+                cost_estimate=takes(5.5),
+            )(self.place, *self.flat),
+            "dp",
+            1,
+        )
+
+    def send_first(self, *behind):
+        half = self.rows // 2
+        shape = (self.pairs, 2, half, self.inner)
+        block = (self.pairs, 1, half, self.inner)
+
+        def at(i, own):
+            return (1 - own) + i * (2 * own - 1)
+
+        kinds = jax.ShapeDtypeStruct(shape, bf16)
+        t1, self.k1, t2, self.k2 = pl.pallas_call(
+            functools.partial(grad_keep_kernel, self.pairs, self.count),
+            grid_spec=pltpu.PrefetchScalarGridSpec(
+                num_scalar_prefetch=1,
+                grid=(2, 2),
+                in_specs=self.specs(lambda i, j, p: (0, 4 * at(i, p[2]) + 2 * at(j, p[1]) + p[0]))
+                + [
+                    pl.BlockSpec(
+                        (self.pairs, 1, self.rows, self.inner),
+                        lambda i, j, p: (0, 2 * at(i, p[2]) + at(j, p[1]), 0, 0),
+                    )
+                ],
+                out_specs=[
+                    pl.BlockSpec(block, lambda i, j, p: (0, at(i, p[2]), 0, 0)),
+                    pl.BlockSpec(block, lambda i, j, p: (0, at(i, p[2]), 0, 0)),
+                    pl.BlockSpec(block, lambda i, j, p: (0, at(jnp.maximum(i, j), p[1]), 0, 0)),
+                    pl.BlockSpec(block, lambda i, j, p: (0, at(jnp.minimum(i, j), p[1]), 0, 0)),
+                ],
+            ),
+            out_shape=[kinds] * 4,
+            name="grad_keep",
+            compiler_params=pltpu.CompilerParams(vmem_limit_bytes=14 * 1024 * 1024),
+            cost_estimate=takes(6.5),
+        )(self.place, *self.flat, after(self.got, *behind))
+        self.left = self.k1
+        self.g1, self.g2 = swap(t1, "dp", 2), swap(t2, "dp", 4)
+
+    def rest(self):
+        return self.left
+
+    def send_second(self, *behind):
+        half = self.rows // 2
+        shape = (self.pairs, half, self.inner)
+        whole = pl.BlockSpec((self.pairs, 2, half, self.inner), lambda i, p: (0, 0, 0, 0))
+        part = pl.BlockSpec(shape, lambda i, p: (0, 0, 0))
+        o1, self.m1, o2, self.m2 = pl.pallas_call(
+            grad_mid_kernel,
+            grid_spec=pltpu.PrefetchScalarGridSpec(
+                num_scalar_prefetch=1, grid=(1,), in_specs=[whole] * 4, out_specs=[part] * 4
+            ),
+            out_shape=[jax.ShapeDtypeStruct(shape, kind) for kind in (bf16, f32, bf16, f32)],
+            name="grad_mid",
+            compiler_params=pltpu.CompilerParams(vmem_limit_bytes=8 * 1024 * 1024),
+            cost_estimate=takes(3.5),
+        )(self.place, after(self.k1, *behind), self.g1, self.k2, self.g2)
+        self.left = self.m1
+        self.h1, self.h2 = swap(o1, "dp", 4), swap(o2, "dp", 2)
+
+    def finish(self, *behind):
+        self.m1, self.m2, self.h1, self.h2 = after((self.m1, self.m2, self.h1, self.h2), *behind)
+        return [
+            jnp.concatenate([self.m1[g] + self.h1[g].astype(f32), self.m2[g] + self.h2[g].astype(f32)], 0)
+            for g in range(self.pairs)
+        ]
+
+
+class PlainGradScatter:
+    def __init__(self, lefts, rights, place):
+        self.lefts, self.rights = lefts, rights
+
+    def send_core(self):
+        grads = [sum(mm(a, b, (0, 0)) for a, b in zip(left, right)) for left, right in zip(self.lefts, self.rights)]
+        self.parts = [scatter_of(grad, "dp") for grad in grads]
+        for part in self.parts:
+            self.got = part.send()
+
+    def send_first(self, *behind):
+        for part in self.parts:
+            part.add()
+        for part in self.parts:
+            part.send()
+
+    send_second = send_first
+
+    def rest(self):
+        return self.parts[0].kept
+
+    def finish(self, *behind):
+        for part in self.parts:
+            part.add()
+        return [part.finish() for part in self.parts]
 
 
 def per_device(
@@ -627,7 +790,6 @@
     keep = 1.0 - starts[:, ::8].astype(f32)
     seqs = range(count)
     me = lax.axis_index("fsdp")
-    core = lax.rem(lax.axis_index("dp"), 2)
     offs = jnp.stack([(me ^ mask) * rows for mask in range(lax.axis_size("fsdp"))])[None, :].astype(jnp.int32)
     tap_bias = conv_bias[None, :]
     normed, xin, xs, z, masks, projs = [], [], [], [], [], []
@@ -637,43 +799,53 @@
     behind = ()
     for s in seqs:
         for source, into in ((states_in, tokens), (out_cotangent, cot_parts)):
-            into.append(gather_parts(after(source[s], *behind), "fsdp"))
-            behind = (into[s][-2],)
+            gather = relay_all if behind else exchange_all
+            into.append(gather(after(source[s], *behind), "fsdp"))
+            behind = (into[s][1],)
     for s in seqs:
         seg_ext = jnp.pad(segments[s], (span - 1, 0), constant_values=-1)
         mask = jnp.stack([(seg_ext[w : w + seq_len] == segments[s]).astype(f32) for w in range(span)], 1)
         masks.append(jnp.pad(mask, ((0, 0), (0, LANES - span))))
 
-    def run_enter(s):
+    def run_enter(s, *behind):
         got = enter(
-            offs, tokens[s], norm_gain[None, :], masks[s], in_x_weight, in_z_weight, conv_weight, tap_bias, proj_weight
+            offs,
+            [far(part) for part in tokens[s]],
+            norm_gain[None, :],
+            after(masks[s], *behind),
+            far(in_x_weight),
+            far(in_z_weight),
+            conv_weight,
+            tap_bias,
+            far(proj_weight),
         )
         for into, value in zip((normed, xin, z, xs), got):
             into.append(value)
-        projs.append(exchange_all(got[4], "fsdp"))
-
-    def run_recurrence(s):
+        projs.append(sum_pair(got[4], "fsdp"))
+
+    def run_recurrence(s, *behind):
         got = recurrence(
             keep[s : s + 1],
             offs,
-            cot_parts[s],
-            projs[s],
-            xs[s],
+            [far(part) for part in cot_parts[s]],
+            [far(term) for term in projs[s]],
+            after(xs[s], *behind),
             z[s],
-            out_weight,
-            dt_weight,
+            far(out_weight),
+            far(dt_weight),
             dt_bias[None, :],
             skip_weight[None, :],
         )
-        for into, value in zip((gated, gz, gxs, gprojs, small, dtg, cots, branch), got):
+        for into, value in zip((gated, gz, gxs, gprojs, small, dtg, cots), got):
             into.append(value)
-        gprojs[s] = exchange_all(gprojs[s], "fsdp")
-        branch[s] = scatter_of(branch[s], "fsdp")
+        gprojs[s] = sum_pair(gprojs[s], "fsdp")
+        branch.append(RowScatter(*got[7:], "fsdp"))
 
     def run_leave(s, *behind):
         got = leave(
-            gprojs[s],
-            proj_weight,
+            offs,
+            [far(term) for term in gprojs[s]],
+            far(proj_weight),
             after(gxs[s], *behind),
             xin[s],
             xs[s],
@@ -681,81 +853,84 @@
             masks[s],
             conv_weight,
             tap_bias,
-            in_x_weight,
-            in_z_weight,
+            far(in_x_weight),
+            far(in_z_weight),
             normed[s],
         )
-        for into, value in zip((g_x_in, gn, rows_part, proj_part, gain_part), got):
+        for into, value in zip((g_x_in, rows_part, proj_part, gain_part), got):
             into.append(value)
-        gn[s] = scatter_of(gn[s], "fsdp")
-
+        gn.append(RowScatter(*got[4:], "fsdp"))
+
+    def total_of(parts):
+        total = [part.astype(f32) for part in parts]
+        while len(total) > 1:
+            total = [total[n] + total[n + 1] for n in range(0, len(total), 2)]
+        return total[0]
+
+    bits = [lax.rem(lax.axis_index("dp") // bit, 2) for bit in bits_of(dp)]
+    place = jnp.stack(bits).astype(jnp.int32)
+    scatter = GradScatter if dp == 8 and (model // dp) % 256 == 0 else PlainGradScatter
     run_enter(0)
-    run_enter(1)
     run_recurrence(0)
-    run_recurrence(1)
-    first_a = branch[0].send()
-    out_sent = swap(grad_slices(cots, [gated[0], after(gated[1], first_a)], 1 - core, dp), "dp", 1)
-    z_sent = swap(grad_slices(normed, gz, 1 - core, dp), "dp", 1)
-    branch[0].add()
-    out_parts = scatter_rest(grad_slices(cots, gated, core, dp, out_sent))
-    z_parts = scatter_rest(grad_slices(normed, gz, core, dp, z_sent))
-    started = [part.send() for part in out_parts + z_parts]
-    second_a = branch[0].send()
-    run_leave(0, out_parts[0].x, z_parts[0].x)
-    for part in out_parts:
-        part.add()
-        part.send()
-    first_b = branch[1].send()
-    first_gn = gn[0].send()
-    run_leave(1, second_a, started[0], started[1], gn[0].x)
-    for part in z_parts:
-        part.add()
-        part.send()
-    gn[0].add()
-    second_gn = gn[0].send()
-    later = (started[2], started[3], out_parts[0].got, out_parts[1].got, first_gn, first_b)
-    x_sent = swap(grad_slices(normed, [g_x_in[0], after(g_x_in[1], *later)], 1 - core, dp), "dp", 1)
+    branch[0].send()
+    run_enter(1, gated[0])
+    branch[0].mid()
+    branch[0].send()
+    run_leave(0, projs[1][0])
+    gn[0].send()
+    run_recurrence(1, g_x_in[0])
+    branch[1].send()
+    gate = (branch[0].got, gn[0].got)
+    out_sum = scatter([cots], [[gated[0], after(gated[1], *gate)]], place)
+    out_sum.send_core()
+    z_sum = scatter([normed], [gz], place)
+    z_sum.send_core()
+    gn[0].mid()
+    gn[0].send()
+    out_sum.send_first()
+    z_sum.send_first()
+    branch[1].mid()
+    branch[1].send()
+    run_leave(1, out_sum.rest(), z_sum.rest())
     gn[1].send()
-    x_parts = scatter_rest(grad_slices(normed, g_x_in, core, dp, x_sent))
-
-    def join(parts):
-        return jnp.concatenate([part.finish() for part in parts], 0)
-
-    def end(scatter):
-        if scatter.left:
-            scatter.add()
-        return scatter.finish()
-
-    out_grad = jnp.concatenate([end(part) for part in out_parts], 0).T
-    in_z_grad = jnp.concatenate([end(part) for part in z_parts], 0)
-    in_x_grad = join(x_parts)
+    out_sum.send_second(g_x_in[1])
+    z_sum.send_second(out_sum.rest())
+    x_sum = scatter([normed], [[g_x_in[0], after(g_x_in[1], z_sum.rest())]], place)
+    x_sum.send_core()
+    gn[1].mid()
+    gn[1].send()
+    x_sum.send_first()
+    packed = jnp.concatenate(
+        [sum(proj_part), sum(rows_part), sum(small), jnp.concatenate([sum(gain_part).reshape(-1, inner)] * 4, 0)], 0
+    )
+    packed = all_sum(after(packed, x_sum.rest()), "dp")
+    x_sum.send_second(branch[1].got)
+    gain_rows = packed[proj_weight.shape[0] + 16 : proj_weight.shape[0] + 16 + model // inner]
+    gain_grad = total_of(exchange_all(gain_rows, "fsdp")).reshape(-1) / gain
+    (out_grad,), (in_z_grad,), (in_x_grad,) = out_sum.finish(x_sum.rest()), z_sum.finish(x_sum.rest()), x_sum.finish()
     outputs, input_grads = [], []
     for s in seqs:
-        outputs.append((states_in[s].astype(f32) + end(branch[s])).astype(bf16))
-        v = states_in[s].astype(f32)
+        v = after(states_in[s], x_sum.rest()).astype(f32)
+        outputs.append((v + branch[s].finish()).astype(bf16))
         rscale = lax.rsqrt(jnp.mean(v * v, axis=1, keepdims=True) + norm_eps)
-        scaled = end(gn[s]) * gain
+        scaled = gn[s].finish() * gain
         inner_mean = jnp.mean(scaled * v, axis=1, keepdims=True)
         input_grads.append(out_cotangent[s].astype(f32) + rscale * scaled - v * (rscale * rscale * rscale) * inner_mean)
-
-    dt_grad = scatter_of(sum(dtg), "dp").finish()
-    rows_sum = jnp.concatenate([sum(rows_part)[: span + 1], sum(small)[1::-1]], 0)
-    packed = all_sum(jnp.concatenate([rows_sum, sum(proj_part), jnp.zeros((1, inner), f32)], 0), "dp")
-    gain_grad = all_sum(all_sum(sum(gain_part)[0], "fsdp", f32), "dp", f32) / gain
-    first = span + 3
+    dt_grad = scatter_of(after(sum(dtg), x_sum.rest()), "dp").finish()
+    tail = packed[proj_weight.shape[0] :]
     return (
         jnp.stack(outputs),
         jnp.stack(input_grads),
         gain_grad,
         in_x_grad,
         in_z_grad,
-        packed[:span],
-        packed[span],
-        packed[first : first + proj_weight.shape[0]].T,
+        tail[:span],
+        tail[span],
+        packed[: proj_weight.shape[0]].T,
         dt_grad,
-        packed[span + 1],
-        packed[span + 2],
-        out_grad,
+        tail[8 + 1],
+        tail[8],
+        out_grad.T,
     )
 
 

time: 345 us -> 311 us (0.901)
  Pallas kernels: 129 us -> 111 us
  starting transfers between devices: 63.7 us -> 76.8 us
  local copies, waits for them, and re-layouts: 39.9 us -> 27.2 us
  other arithmetic: 29.5 us -> 21.5 us
  waiting for transfers between devices: 79.4 us -> 72.8 us
    add x19 -> x3, other arithmetic: 13.8 us -> 0.68 us  [add(): self.x = self.kept.astype(f32) + self.got.astype(f32)]
    ppermute x58 -> x52, starting transfers between devices: 63.7 us -> 76.8 us  [swap(): lax.ppermute(x, axis, [(i, i ^ bit) for i in range(lax.axis_size(axis))])]
    unnamed x110 -> x167, local copies, waits for them, and re-layouts: 7.56 us -> 18.2 us
    pallas_call x6 -> x9, Pallas kernels: 30.5 us -> 22.8 us  [the longest x3 10.8 us: send_first(): pl.pallas_call(functools.partial(grad_keep_kernel, self.pairs, self.count...]
    ppermute x58 -> x52, waiting for transfers between devices: 79.4 us -> 72.8 us  [swap(): lax.ppermute(x, axis, [(i, i ^ bit) for i in range(lax.axis_size(axis))])]
    squeeze x10 -> x2, local copies, waits for them, and re-layouts: 9.65 us -> 3.7 us  [the longest x1 1.89 us: per_device(): into.append(gather(after(source[s], *behind), 'fsdp'))]
    slice x5 -> x3, local copies, waits for them, and re-layouts: 6.45 us -> 1.22 us  [the longest x1 0.61 us: per_device(): tail[:span]]
    dynamic_slice x4 -> x0, local copies, waits for them, and re-layouts: 4.97 us -> none  [take_bit(): return lax.dynamic_index_in_dim(x, value, dim, keepdims=False)]
  transfers between devices with their start and end apart: 58 -> 52, of which waited for: 21 -> 21; matrix products, arithmetic and copies ran while one was open for 18% -> 9% of each run, Pallas kernels for 38% -> 34%
where the time goes in v2:
time: 311 us; the launch traced here: 310 us
  Pallas kernels  111 us (36%)
  starting transfers between devices  76.8 us (25%)
  waiting for transfers between devices  72.8 us (23%)
  local copies, waits for them, and re-layouts  27.2 us (9%)
  other arithmetic  21.5 us (7%)
    ppermute x52, starting transfers between devices, swap(): lax.ppermute(x, axis, [(i, i ^ bit) for i in range(lax.axis_size(axis))])  76.8 us
    ppermute x52, waiting for transfers between devices, swap(): lax.ppermute(x, axis, [(i, i ^ bit) for i in range(lax.axis_size(axis))])  72.8 us
    pallas_call x2, Pallas kernels, recurrence(): pl.pallas_call(functools.partial(recurrence_kernel, state_dim, rank, len(...  56.4 us
    unnamed x167, local copies, waits for them, and re-layouts  18.2 us
    pallas_call x2, Pallas kernels, leave(): pl.pallas_call(functools.partial(leave_kernel, len(terms)), grid=(inner /...  16.1 us
    pallas_call x2, Pallas kernels, enter(): pl.pallas_call(functools.partial(enter_kernel, len(parts)), grid=(inner /...  15.3 us
    pallas_call x3, Pallas kernels, send_first(): pl.pallas_call(functools.partial(grad_keep_kernel, self.pairs, self.count...  10.8 us
    pallas_call x3, Pallas kernels, send_core(): pl.pallas_call(functools.partial(grad_send_kernel, self.pairs, self.count...  8.99 us
  transfers between devices with their start and end apart: 52, of which 21 were waited for; matrix products, arithmetic and copies ran while one was open for 9% of the time, Pallas kernels for 34%

profile of v2, /device:TPU:0, one launch (start us, length us, event | category | flops | bytes accessed | tf_op | source)
XLA Modules:
  0.0 310.5 jit_solution(1694679770853919592)
XLA Ops:
  0.7 1.8 slice_bitcast_fusion.4
  2.5 3.0 collective-permute-start
  5.5 2.6 collective-permute-start.1
  9.0 1.9 slice_bitcast_fusion.2
  11.5 5.2 %collective-permute-done.refs_1_ = bf16[64,2048]{1,0:T(8,128)(2,1)S(1)} collective-permute-done((bf16[64,2048]{1,0:T(8,128)(2,1)S(1)}, bf16[64,2048]{1,0:T(8,128)(2,1)S(1)}, u32[]{:S(2)}, u32[]{:S(2)}) %collective-permute-start) | collective-permute-done | bytes 262176 | tf_op jit(solution)/shard_map/ppermute | solution.py:26
  16.7 3.8 %collective-permute-start.7 = (bf16[64,2048]{1,0:T(8,128)(2,1)}, bf16[64,2048]{1,0:T(8,128)(2,1)}, u32[]{:S(2)}, u32[]{:S(2)}) collective-permute-start(bf16[64,2048]{1,0:T(8,128)(2,1)} %get-tuple-element.101.refs_0_), channel_id=1, source_target_pairs={{0,2},{1,3},{2,0},{3,1},{4,6},{5,7},{6,4},{7,5},{8,10},{9,11},{10,... | collective-permute-start | bytes 786440 | tf_op jit(solution)/shard_map/ppermute | solution.py:26
  20.4 6.5 %collective-permute-done.1.refs_2_ = bf16[64,2048]{1,0:T(8,128)(2,1)S(1)} collective-permute-done((bf16[64,2048]{1,0:T(8,128)(2,1)S(1)}, bf16[64,2048]{1,0:T(8,128)(2,1)S(1)}, u32[]{:S(2)}, u32[]{:S(2)}) %collective-permute-start.1) | collective-permute-done | bytes 262176 | tf_op jit(solution)/shard_map/ppermute | solution.py:26
  28.3 7.7 %enter.2 = (bf16[256,2048]{1,0:T(8,128)(2,1)S(1)}, bf16[256,1024]{1,0:T(8,128)(2,1)S(1)}, f32[256,1024]{1,0:T(8,128)S(1)}, bf16[256,1024]{1,0:T(8,128)(2,1)S(1)}, bf16[160,256]{1,0:T(8,128)(2,1)S(1)}) custom-call(s32[1,4]{1,0:T(1,128)S(1)} %add_bitcast_fusion.7.offs_ref, bf16[64,2048]{1,0:T(8,128)(2,1)} %copy-done.44, bf16[64,2048]{1,0:T(8,128)(2,1)} %copy-done.71, ...), custom_call_target="tpu_custom_call" | custom-call | flops 8099999744 | bytes 1 | tf_op jit(solution)/shard_map/enter/pallas_call | solution.py:186
  38.6 11.1 %collective-permute-start.9 = (bf16[160,256]{1,0:T(8,128)(2,1)S(1)}, bf16[160,256]{1,0:T(8,128)(2,1)S(1)}, u32[]{:S(2)}, u32[]{:S(2)}) collective-permute-start(bf16[160,256]{1,0:T(8,128)(2,1)S(1)} %get-tuple-element.103), channel_id=1, source_target_pairs={{0,1},{1,0},{2,3},{3,2},{4,5},{5,4},{6,7},{7,6},{8,9},{9,8},{10,11... | collective-permute-start | bytes 245768 | tf_op jit(solution)/shard_map/ppermute | solution.py:26
  50.0 3.0 collective-permute-start.5
  53.1 3.3 %collective-permute-done.9 = bf16[160,256]{1,0:T(8,128)(2,1)S(1)} collective-permute-done((bf16[160,256]{1,0:T(8,128)(2,1)S(1)}, bf16[160,256]{1,0:T(8,128)(2,1)S(1)}, u32[]{:S(2)}, u32[]{:S(2)}) %collective-permute-start.9) | collective-permute-done | bytes 81952 | tf_op jit(solution)/shard_map/ppermute | solution.py:26
  56.5 4.5 %collective-permute-start.10 = (bf16[160,256]{1,0:T(8,128)(2,1)S(1)}, bf16[160,256]{1,0:T(8,128)(2,1)S(1)}, u32[]{:S(2)}, u32[]{:S(2)}) collective-permute-start(bf16[160,256]{1,0:T(8,128)(2,1)S(1)} %add_convert_fusion.9.refs_4_), channel_id=1, source_target_pairs={{0,2},{1,3},{2,0},{3,1},{4,6},{5,7},{6,4},{7,5},{8,10},{9,11},{10,... | collective-permute-start | bytes 245768 | tf_op jit(solution)/shard_map/ppermute | solution.py:26
  61.1 4.5 %collective-permute-done.4.refs_1_ = bf16[64,2048]{1,0:T(8,128)(2,1)S(1)} collective-permute-done((bf16[64,2048]{1,0:T(8,128)(2,1)}, bf16[64,2048]{1,0:T(8,128)(2,1)S(1)}, u32[]{:S(2)}, u32[]{:S(2)}) %collective-permute-start.4) | collective-permute-done | bytes 262176 | tf_op jit(solution)/shard_map/ppermute | solution.py:26
  65.5 3.8 %collective-permute-start.15 = (bf16[64,2048]{1,0:T(8,128)(2,1)}, bf16[64,2048]{1,0:T(8,128)(2,1)S(1)}, u32[]{:S(2)}, u32[]{:S(2)}) collective-permute-start(bf16[64,2048]{1,0:T(8,128)(2,1)} %get-tuple-element.116.refs_0_), channel_id=1, source_target_pairs={{0,2},{1,3},{2,0},{3,1},{4,6},{5,7},{6,4},{7,5},{8,10},{9,11},{10,... | collective-permute-start | bytes 786440 | tf_op jit(solution)/shard_map/ppermute | solution.py:26
  70.7 2.6 collective-permute-done.8.refs_3_
  76.2 27.7 %recurrence.2 = (bf16[256,1024]{1,0:T(8,128)(2,1)S(1)}, bf16[256,1024]{1,0:T(8,128)(2,1)S(1)}, f32[256,1024]{1,0:T(8,128)S(1)}, bf16[160,256]{1,0:T(8,128)(2,1)S...) custom-call(f32[1,32]{1,0:T(1,128)S(1)} %get-tuple-element.247.keep_, ...), custom_call_target="tpu_custom_call" | custom-call | flops 27000000512 | bytes 1 | tf_op jit(solution)/shard_map/recurrence/pallas_call | solution.py:533
  106.8 7.6 %enter.3 = (bf16[256,2048]{1,0:T(8,128)(2,1)S(1)}, bf16[256,1024]{1,0:T(8,128)(2,1)S(1)}, f32[256,1024]{1,0:T(8,128)S(1)}, bf16[256,1024]{1,0:T(8,128)(2,1)S(1)}, bf16[160,256]{1,0:T(8,128)(2,1)S(1)}) custom-call(s32[1,4]{1,0:T(1,128)S(1)} %add_bitcast_fusion.7.offs_ref, bf16[64,2048]{1,0:T(8,128)(2,1)} %get-tuple-element.155.refs_0_, ...), custom_call_target="tpu_custom_call" | custom-call | flops 8099999744 | bytes 1 | tf_op jit(solution)/shard_map/enter/pallas_call | solution.py:186
  116.0 3.6 %collective-permute-start.12 = (bf16[160,256]{1,0:T(8,128)(2,1)S(1)}, bf16[160,256]{1,0:T(8,128)(2,1)S(1)}, u32[]{:S(2)}, u32[]{:S(2)}) collective-permute-start(bf16[160,256]{1,0:T(8,128)(2,1)S(1)} %add_convert_fusion.8.refs_0_), channel_id=1, source_target_pairs={{0,2},{1,3},{2,0},{3,1},{4,6},{5,7},{6,4},{7,5},{8,10},{9,11},{10,... | collective-permute-start | bytes 245768 | tf_op jit(solution)/shard_map/ppermute | solution.py:26
  119.8 6.3 %collective-permute-start.17 = (bf16[160,256]{1,0:T(8,128)(2,1)S(1)}, bf16[160,256]{1,0:T(8,128)(2,1)S(1)}, u32[]{:S(2)}, u32[]{:S(2)}) collective-permute-start(bf16[160,256]{1,0:T(8,128)(2,1)S(1)} %add_convert_fusion.7.refs_4_), channel_id=1, source_target_pairs={{0,2},{1,3},{2,0},{3,1},{4,6},{5,7},{6,4},{7,5},{8,10},{9,11},{10,... | collective-permute-start | bytes 245768 | tf_op jit(solution)/shard_map/ppermute | solution.py:26
  126.7 7.7 %leave.2 = (bf16[256,1024]{1,0:T(8,128)(2,1)S(1)}, f32[8,1024]{1,0:T(8,128)S(1)}, f32[160,1024]{1,0:T(8,128)S(1)}, f32[1,2048]{1,0:T(1,128)S(1)}, bf16[2,64,2048...) custom-call(s32[1,4]{1,0:T(1,128)S(1)} %add_bitcast_fusion.7.offs_ref, bf16[160,256]{1,0:T(8,128)(2,1)} %copy-done.59, ...), custom_call_target="tpu_custom_call" | custom-call | flops 8999999488 | bytes 1 | tf_op jit(solution)/shard_map/leave/pallas_call | solution.py:278
  134.4 2.7 collective-permute-start.22
  138.1 28.7 %recurrence.3 = (bf16[256,1024]{1,0:T(8,128)(2,1)S(1)}, bf16[256,1024]{1,0:T(8,128)(2,1)S(1)}, f32[256,1024]{1,0:T(8,128)S(1)}, bf16[160,256]{1,0:T(8,128)(2,1)S...) custom-call(f32[1,32]{1,0:T(1,128)S(1)} %get-tuple-element.248.keep_, ...), custom_call_target="tpu_custom_call" | custom-call | flops 27000000512 | bytes 1 | tf_op jit(solution)/shard_map/recurrence/pallas_call | solution.py:533
  166.8 2.6 grad_send.4
  169.5 2.6 grad_send.3
  172.9 4.3 %collective-permute-done.18 = bf16[160,256]{1,0:T(8,128)(2,1)S(1)} collective-permute-done((bf16[160,256]{1,0:T(8,128)(2,1)S(1)}, bf16[160,256]{1,0:T(8,128)(2,1)S(1)}, u32[]{:S(2)}, u32[]{:S(2)}) %collective-permute-start.18) | collective-permute-done | bytes 81952 | tf_op jit(solution)/shard_map/ppermute | solution.py:26
  177.2 3.0 collective-permute-start.19
  180.2 3.0 grad_keep.4
  186.3 3.0 grad_keep.3
  191.1 8.5 %leave.3 = (bf16[256,1024]{1,0:T(8,128)(2,1)S(1)}, f32[8,1024]{1,0:T(8,128)S(1)}, f32[160,1024]{1,0:T(8,128)S(1)}, f32[1,2048]{1,0:T(1,128)S(1)}, bf16[2,64,2048...) custom-call(s32[1,4]{1,0:T(1,128)S(1)} %copy-done.15, bf16[160,256]{1,0:T(8,128)(2,1)} %copy-done.56, ...), custom_call_target="tpu_custom_call" | custom-call | flops 8999999488 | bytes 1 | tf_op jit(solution)/shard_map/leave/pallas_call | solution.py:278
  199.5 7.5 %collective-permute-done.25.g1_ref = bf16[1,2,128,1024]{3,2,1,0:T(8,128)(2,1)S(1)} collective-permute-done((bf16[1,2,128,1024]{3,2,1,0:T(8,128)(2,1)S(1)}, bf16[1,2,128,1024]{3,2,1,0:T(8,128)(2,1)S(1)}, u32[]{:S(2)}, u32[]{:S(2)}) %collective-permute-start.25) | collective-permute-done | bytes 524320 | tf_op jit(solution)/shard_map/ppermute | solution.py:26
  212.3 3.7 %grad_send.5 = bf16[1,4,256,1024]{3,2,1,0:T(8,128)(2,1)} custom-call(s32[3]{0:T(128)S(1)} %pad_add_fusion.place_ref, bf16[256,2048]{1,0:T(8,128)(2,1)S(1)} %copy-done.29, bf16[256,2048]{1,0:T(8,128)(2,1)S(1)} %get-tuple-element.108.refs_1_.refs_12_, bf16[256,1024]{1,0:T(8,128)(2,1)S(1)} %get-tuple-element.115.refs_2_, ...), custom_call_target="tpu_custom_call" | custom-call | flops 4950000128 | bytes 1 | tf_op jit(solution)/shard_map/grad_send/pallas_call | solution.py:658
  218.2 1.9 add.261
  220.1 1.8 add_convert_fusion.3
  221.8 8.8 %collective-permute-done.30 = bf16[2,64,2048]{2,1,0:T(8,128)(2,1)} collective-permute-done((bf16[2,64,2048]{2,1,0:T(8,128)(2,1)}, bf16[2,64,2048]{2,1,0:T(8,128)(2,1)}, u32[]{:S(2)}, u32[]{:S(2)}) %collective-permute-start.30) | collective-permute-done | bytes 524320 | tf_op jit(solution)/shard_map/ppermute | solution.py:26
  230.7 1.7 add_convert_fusion.4
  234.4 1.9 concatenate.12
  242.5 4.8 %grad_keep.5 = (bf16[1,2,128,1024]{3,2,1,0:T(8,128)(2,1)S(1)}, bf16[1,2,128,1024]{3,2,1,0:T(8,128)(2,1)S(1)}, bf16[1,2,128,1024]{3,2,1,0:T(8,128)(2,1)S(1)}, bf16[1,2,128,1024]{3,2,1,0:T(8,128)(2,1)S(1)}) custom-call(s32[3]{0:T(128)S(1)} %copy-done.17, bf16[256,2048]{1,0:T(8,128)(2,1)S(1)} %copy-done.30, bf16[256,2048]{1,0:T(8,128)(2,1)S(1)} %copy-done.32, ...), custom_call_target="tpu_custom_call" | custom-call | flops 5849999872 | bytes 1 | tf_op jit(solution)/shard_map/grad_keep/pallas_call | solution.py:684
  248.4 3.5 %collective-permute-done.35 = bf16[2,64,2048]{2,1,0:T(8,128)(2,1)} collective-permute-done((bf16[2,64,2048]{2,1,0:T(8,128)(2,1)}, bf16[2,64,2048]{2,1,0:T(8,128)(2,1)}, u32[]{:S(2)}, u32[]{:S(2)}) %collective-permute-start.35) | collective-permute-done | bytes 524320 | tf_op jit(solution)/shard_map/ppermute | solution.py:26
  252.9 1.8 collective-permute-start.34
  257.3 3.2 %collective-permute-done.32.g1_ref = bf16[1,2,128,1024]{3,2,1,0:T(8,128)(2,1)S(1)} collective-permute-done((bf16[1,2,128,1024]{3,2,1,0:T(8,128)(2,1)S(1)}, bf16[1,2,128,1024]{3,2,1,0:T(8,128)(2,1)S(1)}, u32[]{:S(2)}, u32[]{:S(2)}) %collective-permute-start.32) | collective-permute-done | bytes 524320 | tf_op jit(solution)/shard_map/ppermute | solution.py:26
  260.5 1.7 collective-permute-start.51
  263.8 2.3 collective-permute-done.46
  268.2 3.6 %collective-permute-done.51 = bf16[1,128,1024]{2,1,0:T(8,128)(2,1)S(1)} collective-permute-done((bf16[1,128,1024]{2,1,0:T(8,128)(2,1)S(1)}, bf16[1,128,1024]{2,1,0:T(8,128)(2,1)S(1)}, u32[]{:S(2)}, u32[]{:S(2)}) %collective-permute-start.51) | collective-permute-done | bytes 262176 | tf_op jit(solution)/shard_map/ppermute | solution.py:26
  273.6 5.5 %collective-permute-done.36 = bf16[1,64,2048]{2,1,0:T(8,128)(2,1)S(1)} collective-permute-done((bf16[1,64,2048]{2,1,0:T(8,128)(2,1)S(1)}, bf16[1,64,2048]{2,1,0:T(8,128)(2,1)S(1)}, u32[]{:S(2)}, u32[]{:S(2)}) %collective-permute-start.36) | collective-permute-done | bytes 262176 | tf_op jit(solution)/shard_map/ppermute | solution.py:26
  279.2 2.0 fusion.1
  286.9 2.6 collective-permute-done.48
  299.1 4.8 %collective-permute-done.39 = bf16[184,1024]{1,0:T(8,128)(2,1)S(1)} collective-permute-done((bf16[184,1024]{1,0:T(8,128)(2,1)S(1)}, bf16[184,1024]{1,0:T(8,128)(2,1)S(1)}, u32[]{:S(2)}, u32[]{:S(2)}) %collective-permute-start.39) | collective-permute-done | bytes 376864 | tf_op jit(solution)/shard_map/ppermute | solution.py:26
  304.1 2.2 collective-permute-start.42
  (302 shorter events, 67.2 us)
Async XLA Ops:
  2.5 14.2 %collective-permute-start = (bf16[64,2048]{1,0:T(8,128)(2,1)S(1)}, bf16[64,2048]{1,0:T(8,128)(2,1)S(1)}, u32[]{:S(2)}, u32[]{:S(2)}) collective-permute-start(bf16[64,2048]{1,0:T(8,128)(2,1)S(1)} %get-tuple-element.154.refs_0_), channel_id=1, source_target_pairs={{0,1},{1,0},{2,3},{3,2},{4,5},{5,4},{6,7},{7,6},{8,9},{9,8},{10,11... | collective-permute-start | bytes 786440 | tf_op jit(solution)/shard_map/ppermute | solution.py:26
  5.5 21.4 %collective-permute-start.1 = (bf16[64,2048]{1,0:T(8,128)(2,1)S(1)}, bf16[64,2048]{1,0:T(8,128)(2,1)S(1)}, u32[]{:S(2)}, u32[]{:S(2)}) collective-permute-start(bf16[64,2048]{1,0:T(8,128)(2,1)S(1)} %get-tuple-element.154.refs_0_), channel_id=1, source_target_pairs={{0,2},{1,3},{2,0},{3,1},{4,6},{5,7},{6,4},{7,5},{8,10},{9,11},{10,... | collective-permute-start | bytes 786440 | tf_op jit(solution)/shard_map/ppermute | solution.py:26
  8.1 18.8 %collective-permute-start.2 = (bf16[64,2048]{1,0:T(8,128)(2,1)S(1)}, bf16[64,2048]{1,0:T(8,128)(2,1)S(1)}, u32[]{:S(2)}, u32[]{:S(2)}) collective-permute-start(bf16[64,2048]{1,0:T(8,128)(2,1)S(1)} %get-tuple-element.154.refs_0_), channel_id=1, source_target_pairs={{0,3},{1,2},{2,1},{3,0},{4,7},{5,6},{6,5},{7,4},{8,11},{9,10},{10,... | collective-permute-start | bytes 786440 | tf_op jit(solution)/shard_map/ppermute | solution.py:26
  16.7 33.2 %collective-permute-start.3 = (bf16[64,2048]{1,0:T(8,128)(2,1)}, bf16[64,2048]{1,0:T(8,128)(2,1)}, u32[]{:S(2)}, u32[]{:S(2)}) collective-permute-start(bf16[64,2048]{1,0:T(8,128)(2,1)} %get-tuple-element.101.refs_0_), channel_id=1, source_target_pairs={{0,1},{1,0},{2,3},{3,2},{4,5},{5,4},{6,7},{7,6},{8,9},{9,8},{10,11... | collective-permute-start | bytes 786440 | tf_op jit(solution)/shard_map/ppermute | solution.py:26
  16.7 36.4 %collective-permute-start.7 = (bf16[64,2048]{1,0:T(8,128)(2,1)}, bf16[64,2048]{1,0:T(8,128)(2,1)}, u32[]{:S(2)}, u32[]{:S(2)}) collective-permute-start(bf16[64,2048]{1,0:T(8,128)(2,1)} %get-tuple-element.101.refs_0_), channel_id=1, source_target_pairs={{0,2},{1,3},{2,0},{3,1},{4,6},{5,7},{6,4},{7,5},{8,10},{9,11},{10,... | collective-permute-start | bytes 786440 | tf_op jit(solution)/shard_map/ppermute | solution.py:26
  38.6 17.8 %collective-permute-start.9 = (bf16[160,256]{1,0:T(8,128)(2,1)S(1)}, bf16[160,256]{1,0:T(8,128)(2,1)S(1)}, u32[]{:S(2)}, u32[]{:S(2)}) collective-permute-start(bf16[160,256]{1,0:T(8,128)(2,1)S(1)} %get-tuple-element.103), channel_id=1, source_target_pairs={{0,1},{1,0},{2,3},{3,2},{4,5},{5,4},{6,7},{7,6},{8,9},{9,8},{10,11... | collective-permute-start | bytes 245768 | tf_op jit(solution)/shard_map/ppermute | solution.py:26
  49.9 15.6 %collective-permute-start.4 = (bf16[64,2048]{1,0:T(8,128)(2,1)}, bf16[64,2048]{1,0:T(8,128)(2,1)S(1)}, u32[]{:S(2)}, u32[]{:S(2)}) collective-permute-start(bf16[64,2048]{1,0:T(8,128)(2,1)} %get-tuple-element.155.refs_0_), channel_id=1, source_target_pairs={{0,1},{1,0},{2,3},{3,2},{4,5},{5,4},{6,7},{7,6},{8,9},{9,8},{10,11... | collective-permute-start | bytes 786440 | tf_op jit(solution)/shard_map/ppermute | solution.py:26
  50.0 19.3 %collective-permute-start.5 = (bf16[64,2048]{1,0:T(8,128)(2,1)}, bf16[64,2048]{1,0:T(8,128)(2,1)S(1)}, u32[]{:S(2)}, u32[]{:S(2)}) collective-permute-start(bf16[64,2048]{1,0:T(8,128)(2,1)} %get-tuple-element.155.refs_0_), channel_id=1, source_target_pairs={{0,2},{1,3},{2,0},{3,1},{4,6},{5,7},{6,4},{7,5},{8,10},{9,11},{10,... | collective-permute-start | bytes 786440 | tf_op jit(solution)/shard_map/ppermute | solution.py:26
  53.0 20.2 %collective-permute-start.8 = (bf16[64,2048]{1,0:T(8,128)(2,1)}, bf16[64,2048]{1,0:T(8,128)(2,1)S(1)}, u32[]{:S(2)}, u32[]{:S(2)}) collective-permute-start(bf16[64,2048]{1,0:T(8,128)(2,1)} %collective-permute-done.7.refs_2_), channel_id=1, source_target_pairs={{0,1},{1,0},{2,3},{3,2},{4,5},{5,4},{6,7},{7,6},{8,9},{9,8},{10,11... | collective-permute-start | bytes 786440 | tf_op jit(solution)/shard_map/ppermute | solution.py:26
  56.5 14.3 %collective-permute-start.10 = (bf16[160,256]{1,0:T(8,128)(2,1)S(1)}, bf16[160,256]{1,0:T(8,128)(2,1)S(1)}, u32[]{:S(2)}, u32[]{:S(2)}) collective-permute-start(bf16[160,256]{1,0:T(8,128)(2,1)S(1)} %add_convert_fusion.9.refs_4_), channel_id=1, source_target_pairs={{0,2},{1,3},{2,0},{3,1},{4,6},{5,7},{6,4},{7,5},{8,10},{9,11},{10,... | collective-permute-start | bytes 245768 | tf_op jit(solution)/shard_map/ppermute | solution.py:26
  65.5 71.7 %collective-permute-start.14 = (bf16[64,2048]{1,0:T(8,128)(2,1)}, bf16[64,2048]{1,0:T(8,128)(2,1)S(1)}, u32[]{:S(2)}, u32[]{:S(2)}) collective-permute-start(bf16[64,2048]{1,0:T(8,128)(2,1)} %get-tuple-element.116.refs_0_), channel_id=1, source_target_pairs={{0,1},{1,0},{2,3},{3,2},{4,5},{5,4},{6,7},{7,6},{8,9},{9,8},{10,11... | collective-permute-start | bytes 786440 | tf_op jit(solution)/shard_map/ppermute | solution.py:26
  65.5 54.1 %collective-permute-start.15 = (bf16[64,2048]{1,0:T(8,128)(2,1)}, bf16[64,2048]{1,0:T(8,128)(2,1)S(1)}, u32[]{:S(2)}, u32[]{:S(2)}) collective-permute-start(bf16[64,2048]{1,0:T(8,128)(2,1)} %get-tuple-element.116.refs_0_), channel_id=1, source_target_pairs={{0,2},{1,3},{2,0},{3,1},{4,6},{5,7},{6,4},{7,5},{8,10},{9,11},{10,... | collective-permute-start | bytes 786440 | tf_op jit(solution)/shard_map/ppermute | solution.py:26
  69.3 36.7 %collective-permute-start.6 = (bf16[64,2048]{1,0:T(8,128)(2,1)S(1)}, bf16[64,2048]{1,0:T(8,128)(2,1)S(1)}, u32[]{:S(2)}, u32[]{:S(2)}) collective-permute-start(bf16[64,2048]{1,0:T(8,128)(2,1)S(1)} %collective-permute-done.5.refs_2_), channel_id=1, source_target_pairs={{0,1},{1,0},{2,3},{3,2},{4,5},{5,4},{6,7},{7,6},{8,9},{9,8},{10,11... | collective-permute-start | bytes 786440 | tf_op jit(solution)/shard_map/ppermute | solution.py:26
  103.9 12.1 %collective-permute-start.11 = (bf16[160,256]{1,0:T(8,128)(2,1)S(1)}, bf16[160,256]{1,0:T(8,128)(2,1)S(1)}, u32[]{:S(2)}, u32[]{:S(2)}) collective-permute-start(bf16[160,256]{1,0:T(8,128)(2,1)S(1)} %get-tuple-element.109), channel_id=1, source_target_pairs={{0,1},{1,0},{2,3},{3,2},{4,5},{5,4},{6,7},{7,6},{8,9},{9,8},{10,11... | collective-permute-start | bytes 245768 | tf_op jit(solution)/shard_map/ppermute | solution.py:26
  105.5 31.5 %collective-permute-start.20 = (bf16[2,64,2048]{2,1,0:T(8,128)(2,1)S(1)}, bf16[2,64,2048]{2,1,0:T(8,128)(2,1)S(1)}, u32[]{:S(2)}, u32[]{:S(2)}) collective-permute-start(bf16[2,64,2048]{2,1,0:T(8,128)(2,1)S(1)} %get-tuple-element.126), channel_id=1, source_target_pairs={{0,1},{1,0},{2,3},{3,2},{4,5},{5,4},{6,7},{7,6},{8,9},{9,8},{10,11... | collective-permute-start | bytes 1572872 | tf_op jit(solution)/shard_map/ppermute | solution.py:26
  114.4 5.3 %collective-permute-start.13 = (bf16[160,256]{1,0:T(8,128)(2,1)S(1)}, bf16[160,256]{1,0:T(8,128)(2,1)S(1)}, u32[]{:S(2)}, u32[]{:S(2)}) collective-permute-start(bf16[160,256]{1,0:T(8,128)(2,1)S(1)} %get-tuple-element.111), channel_id=1, source_target_pairs={{0,1},{1,0},{2,3},{3,2},{4,5},{5,4},{6,7},{7,6},{8,9},{9,8},{10,11... | collective-permute-start | bytes 245768 | tf_op jit(solution)/shard_map/ppermute | solution.py:26
  116.0 10.0 %collective-permute-start.12 = (bf16[160,256]{1,0:T(8,128)(2,1)S(1)}, bf16[160,256]{1,0:T(8,128)(2,1)S(1)}, u32[]{:S(2)}, u32[]{:S(2)}) collective-permute-start(bf16[160,256]{1,0:T(8,128)(2,1)S(1)} %add_convert_fusion.8.refs_0_), channel_id=1, source_target_pairs={{0,2},{1,3},{2,0},{3,1},{4,6},{5,7},{6,4},{7,5},{8,10},{9,11},{10,... | collective-permute-start | bytes 245768 | tf_op jit(solution)/shard_map/ppermute | solution.py:26
  119.6 17.6 %collective-permute-start.16 = (bf16[64,2048]{1,0:T(8,128)(2,1)S(1)}, bf16[64,2048]{1,0:T(8,128)(2,1)S(1)}, u32[]{:S(2)}, u32[]{:S(2)}) collective-permute-start(bf16[64,2048]{1,0:T(8,128)(2,1)S(1)} %collective-permute-done.15.refs_2_), channel_id=1, source_target_pairs={{0,1},{1,0},{2,3},{3,2},{4,5},{5,4},{6,7},{7,6},{8,9},{9,8},{10,11... | collective-permute-start | bytes 786440 | tf_op jit(solution)/shard_map/ppermute | solution.py:26
  119.8 17.5 %collective-permute-start.17 = (bf16[160,256]{1,0:T(8,128)(2,1)S(1)}, bf16[160,256]{1,0:T(8,128)(2,1)S(1)}, u32[]{:S(2)}, u32[]{:S(2)}) collective-permute-start(bf16[160,256]{1,0:T(8,128)(2,1)S(1)} %add_convert_fusion.7.refs_4_), channel_id=1, source_target_pairs={{0,2},{1,3},{2,0},{3,1},{4,6},{5,7},{6,4},{7,5},{8,10},{9,11},{10,... | collective-permute-start | bytes 245768 | tf_op jit(solution)/shard_map/ppermute | solution.py:26
  134.4 35.2 %collective-permute-start.22 = (bf16[2,64,2048]{2,1,0:T(8,128)(2,1)S(1)}, bf16[2,64,2048]{2,1,0:T(8,128)(2,1)S(1)}, u32[]{:S(2)}, u32[]{:S(2)}) collective-permute-start(bf16[2,64,2048]{2,1,0:T(8,128)(2,1)S(1)} %get-tuple-element.127), channel_id=1, source_target_pairs={{0,1},{1,0},{2,3},{3,2},{4,5},{5,4},{6,7},{7,6},{8,9},{9,8},{10,11... | collective-permute-start | bytes 1572872 | tf_op jit(solution)/shard_map/ppermute | solution.py:26
  137.1 32.4 %collective-permute-start.21 = (bf16[1,64,2048]{2,1,0:T(8,128)(2,1)S(1)}, bf16[1,64,2048]{2,1,0:T(8,128)(2,1)S(1)}, u32[]{:S(2)}, u32[]{:S(2)}) collective-permute-start(bf16[1,64,2048]{2,1,0:T(8,128)(2,1)S(1)} %add_convert_fusion.5), channel_id=1, source_target_pairs={{0,2},{1,3},{2,0},{3,1},{4,6},{5,7},{6,4},{7,5},{8,10},{9,11},{10,... | collective-permute-start | bytes 786440 | tf_op jit(solution)/shard_map/ppermute | solution.py:26
  169.4 10.8 %collective-permute-start.24 = (bf16[1,4,256,1024]{3,2,1,0:T(8,128)(2,1)S(1)}, bf16[1,4,256,1024]{3,2,1,0:T(8,128)(2,1)S(1)}, u32[]{:S(2)}, u32[]{:S(2)}) collective-permute-start(bf16[1,4,256,1024]{3,2,1,0:T(8,128)(2,1)S(1)} %grad_send.4), channel_id=1, source_target_pairs={{0,4},{4,0},{8,12},{12,8},{16,20},{20,16},{24,28},{28,24},{1,5},{5... | collective-permute-start | bytes 6291464 | tf_op jit(solution)/shard_map/ppermute | solution.py:26
  172.2 14.1 %collective-permute-start.23 = (bf16[1,4,256,1024]{3,2,1,0:T(8,128)(2,1)S(1)}, bf16[1,4,256,1024]{3,2,1,0:T(8,128)(2,1)S(1)}, u32[]{:S(2)}, u32[]{:S(2)}) collective-permute-start(bf16[1,4,256,1024]{3,2,1,0:T(8,128)(2,1)S(1)} %grad_send.3), channel_id=1, source_target_pairs={{0,4},{4,0},{8,12},{12,8},{16,20},{20,16},{24,28},{28,24},{1,5},{5... | collective-permute-start | bytes 6291464 | tf_op jit(solution)/shard_map/ppermute | solution.py:26
  172.8 4.4 %collective-permute-start.18 = (bf16[160,256]{1,0:T(8,128)(2,1)S(1)}, bf16[160,256]{1,0:T(8,128)(2,1)S(1)}, u32[]{:S(2)}, u32[]{:S(2)}) collective-permute-start(bf16[160,256]{1,0:T(8,128)(2,1)S(1)} %get-tuple-element.120), channel_id=1, source_target_pairs={{0,1},{1,0},{2,3},{3,2},{4,5},{5,4},{6,7},{7,6},{8,9},{9,8},{10,11... | collective-permute-start | bytes 245768 | tf_op jit(solution)/shard_map/ppermute | solution.py:26
  177.2 13.2 %collective-permute-start.19 = (bf16[160,256]{1,0:T(8,128)(2,1)S(1)}, bf16[160,256]{1,0:T(8,128)(2,1)S(1)}, u32[]{:S(2)}, u32[]{:S(2)}) collective-permute-start(bf16[160,256]{1,0:T(8,128)(2,1)S(1)} %add_convert_fusion.6.refs_0_), channel_id=1, source_target_pairs={{0,2},{1,3},{2,0},{3,1},{4,6},{5,7},{6,4},{7,5},{8,10},{9,11},{10,... | collective-permute-start | bytes 245768 | tf_op jit(solution)/shard_map/ppermute | solution.py:26
  183.2 26.6 %collective-permute-start.27 = (bf16[1,2,128,1024]{3,2,1,0:T(8,128)(2,1)S(1)}, bf16[1,2,128,1024]{3,2,1,0:T(8,128)(2,1)S(1)}, u32[]{:S(2)}, u32[]{:S(2)}) collective-permute-start(bf16[1,2,128,1024]{3,2,1,0:T(8,128)(2,1)S(1)} %get-tuple-element.141), channel_id=1, source_target_pairs={{0,8},{4,12},{8,0},{12,4},{16,24},{20,28},{24,16},{28,20},{1,9},{5... | collective-permute-start | bytes 1572872 | tf_op jit(solution)/shard_map/ppermute | solution.py:26
  184.8 25.0 %collective-permute-start.28 = (bf16[1,2,128,1024]{3,2,1,0:T(8,128)(2,1)S(1)}, bf16[1,2,128,1024]{3,2,1,0:T(8,128)(2,1)S(1)}, u32[]{:S(2)}, u32[]{:S(2)}) collective-permute-start(bf16[1,2,128,1024]{3,2,1,0:T(8,128)(2,1)S(1)} %get-tuple-element.143), channel_id=1, source_target_pairs={{0,16},{4,20},{8,24},{12,28},{16,0},{20,4},{24,8},{28,12},{1,17},{... | collective-permute-start | bytes 1572872 | tf_op jit(solution)/shard_map/ppermute | solution.py:26
  189.3 17.7 %collective-permute-start.25 = (bf16[1,2,128,1024]{3,2,1,0:T(8,128)(2,1)S(1)}, bf16[1,2,128,1024]{3,2,1,0:T(8,128)(2,1)S(1)}, u32[]{:S(2)}, u32[]{:S(2)}) collective-permute-start(bf16[1,2,128,1024]{3,2,1,0:T(8,128)(2,1)S(1)} %get-tuple-element.136), channel_id=1, source_target_pairs={{0,8},{4,12},{8,0},{12,4},{16,24},{20,28},{24,16},{28,20},{1,9},{5... | collective-permute-start | bytes 1572872 | tf_op jit(solution)/shard_map/ppermute | solution.py:26
  189.9 18.3 %collective-permute-start.26 = (bf16[1,2,128,1024]{3,2,1,0:T(8,128)(2,1)S(1)}, bf16[1,2,128,1024]{3,2,1,0:T(8,128)(2,1)S(1)}, u32[]{:S(2)}, u32[]{:S(2)}) collective-permute-start(bf16[1,2,128,1024]{3,2,1,0:T(8,128)(2,1)S(1)} %get-tuple-element.138), channel_id=1, source_target_pairs={{0,16},{4,20},{8,24},{12,28},{16,0},{20,4},{24,8},{28,12},{1,17},{... | collective-permute-start | bytes 1572872 | tf_op jit(solution)/shard_map/ppermute | solution.py:26
  216.0 21.9 %collective-permute-start.29 = (bf16[1,4,256,1024]{3,2,1,0:T(8,128)(2,1)}, bf16[1,4,256,1024]{3,2,1,0:T(8,128)(2,1)}, u32[]{:S(2)}, u32[]{:S(2)}) collective-permute-start(bf16[1,4,256,1024]{3,2,1,0:T(8,128)(2,1)} %grad_send.5), channel_id=1, source_target_pairs={{0,4},{4,0},{8,12},{12,8},{16,20},{20,16},{24,28},{28,24},{1,5},{5... | collective-permute-start | bytes 6291464 | tf_op jit(solution)/shard_map/ppermute | solution.py:26
  216.0 14.7 %collective-permute-start.30 = (bf16[2,64,2048]{2,1,0:T(8,128)(2,1)}, bf16[2,64,2048]{2,1,0:T(8,128)(2,1)}, u32[]{:S(2)}, u32[]{:S(2)}) collective-permute-start(bf16[2,64,2048]{2,1,0:T(8,128)(2,1)} %get-tuple-element.148), channel_id=1, source_target_pairs={{0,1},{1,0},{2,3},{3,2},{4,5},{5,4},{6,7},{7,6},{8,9},{9,8},{10,11... | collective-permute-start | bytes 1572872 | tf_op jit(solution)/shard_map/ppermute | solution.py:26
  232.4 20.5 %collective-permute-start.31 = (bf16[1,64,2048]{2,1,0:T(8,128)(2,1)}, bf16[1,64,2048]{2,1,0:T(8,128)(2,1)}, u32[]{:S(2)}, u32[]{:S(2)}) collective-permute-start(bf16[1,64,2048]{2,1,0:T(8,128)(2,1)} %add_convert_fusion.4), channel_id=1, source_target_pairs={{0,2},{1,3},{2,0},{3,1},{4,6},{5,7},{6,4},{7,5},{8,10},{9,11},{10,... | collective-permute-start | bytes 786440 | tf_op jit(solution)/shard_map/ppermute | solution.py:26
  232.7 19.1 %collective-permute-start.35 = (bf16[2,64,2048]{2,1,0:T(8,128)(2,1)}, bf16[2,64,2048]{2,1,0:T(8,128)(2,1)}, u32[]{:S(2)}, u32[]{:S(2)}) collective-permute-start(bf16[2,64,2048]{2,1,0:T(8,128)(2,1)} %get-tuple-element.158), channel_id=1, source_target_pairs={{0,1},{1,0},{2,3},{3,2},{4,5},{5,4},{6,7},{7,6},{8,9},{9,8},{10,11... | collective-permute-start | bytes 1572872 | tf_op jit(solution)/shard_map/ppermute | solution.py:26
  236.3 20.4 %collective-permute-start.45 = (bf16[1,128,1024]{2,1,0:T(8,128)(2,1)S(1)}, bf16[1,128,1024]{2,1,0:T(8,128)(2,1)S(1)}, u32[]{:S(2)}, u32[]{:S(2)}) collective-permute-start(bf16[1,128,1024]{2,1,0:T(8,128)(2,1)S(1)} %copy-done.25), channel_id=1, source_target_pairs={{0,16},{4,20},{8,24},{12,28},{16,0},{20,4},{24,8},{28,12},{1,17},{... | collective-permute-start | bytes 786440 | tf_op jit(solution)/shard_map/ppermute | solution.py:26
  247.2 13.3 %collective-permute-start.32 = (bf16[1,2,128,1024]{3,2,1,0:T(8,128)(2,1)S(1)}, bf16[1,2,128,1024]{3,2,1,0:T(8,128)(2,1)S(1)}, u32[]{:S(2)}, u32[]{:S(2)}) collective-permute-start(bf16[1,2,128,1024]{3,2,1,0:T(8,128)(2,1)S(1)} %get-tuple-element.150), channel_id=1, source_target_pairs={{0,8},{4,12},{8,0},{12,4},{16,24},{20,28},{24,16},{28,20},{1,9},{5... | collective-permute-start | bytes 1572872 | tf_op jit(solution)/shard_map/ppermute | solution.py:26
  247.9 12.7 %collective-permute-start.33 = (bf16[1,2,128,1024]{3,2,1,0:T(8,128)(2,1)S(1)}, bf16[1,2,128,1024]{3,2,1,0:T(8,128)(2,1)S(1)}, u32[]{:S(2)}, u32[]{:S(2)}) collective-permute-start(bf16[1,2,128,1024]{3,2,1,0:T(8,128)(2,1)S(1)} %get-tuple-element.152), channel_id=1, source_target_pairs={{0,16},{4,20},{8,24},{12,28},{16,0},{20,4},{24,8},{28,12},{1,17},{... | collective-permute-start | bytes 1572872 | tf_op jit(solution)/shard_map/ppermute | solution.py:26
  252.9 20.7 %collective-permute-start.34 = (bf16[1,64,2048]{2,1,0:T(8,128)(2,1)S(1)}, bf16[1,64,2048]{2,1,0:T(8,128)(2,1)S(1)}, u32[]{:S(2)}, u32[]{:S(2)}) collective-permute-start(bf16[1,64,2048]{2,1,0:T(8,128)(2,1)S(1)} %copy-done.53), channel_id=1, source_target_pairs={{0,2},{1,3},{2,0},{3,1},{4,6},{5,7},{6,4},{7,5},{8,10},{9,11},{10,... | collective-permute-start | bytes 786440 | tf_op jit(solution)/shard_map/ppermute | solution.py:26
  254.7 24.5 %collective-permute-start.36 = (bf16[1,64,2048]{2,1,0:T(8,128)(2,1)S(1)}, bf16[1,64,2048]{2,1,0:T(8,128)(2,1)S(1)}, u32[]{:S(2)}, u32[]{:S(2)}) collective-permute-start(bf16[1,64,2048]{2,1,0:T(8,128)(2,1)S(1)} %add_convert_fusion.2), channel_id=1, source_target_pairs={{0,2},{1,3},{2,0},{3,1},{4,6},{5,7},{6,4},{7,5},{8,10},{9,11},{10,... | collective-permute-start | bytes 786440 | tf_op jit(solution)/shard_map/ppermute | solution.py:26
  256.8 9.3 %collective-permute-start.46 = (bf16[1,128,1024]{2,1,0:T(8,128)(2,1)S(1)}, bf16[1,128,1024]{2,1,0:T(8,128)(2,1)S(1)}, u32[]{:S(2)}, u32[]{:S(2)}) collective-permute-start(bf16[1,128,1024]{2,1,0:T(8,128)(2,1)S(1)} %copy-done.23), channel_id=1, source_target_pairs={{0,8},{4,12},{8,0},{12,4},{16,24},{20,28},{24,16},{28,20},{1,9},{5... | collective-permute-start | bytes 786440 | tf_op jit(solution)/shard_map/ppermute | solution.py:26
  260.5 6.4 %collective-permute-start.50 = (bf16[1,128,1024]{2,1,0:T(8,128)(2,1)S(1)}, bf16[1,128,1024]{2,1,0:T(8,128)(2,1)S(1)}, u32[]{:S(2)}, u32[]{:S(2)}) collective-permute-start(bf16[1,128,1024]{2,1,0:T(8,128)(2,1)S(1)} %copy-done.21), channel_id=1, source_target_pairs={{0,16},{4,20},{8,24},{12,28},{16,0},{20,4},{24,8},{28,12},{1,17},{... | collective-permute-start | bytes 786440 | tf_op jit(solution)/shard_map/ppermute | solution.py:26
  260.5 11.2 %collective-permute-start.51 = (bf16[1,128,1024]{2,1,0:T(8,128)(2,1)S(1)}, bf16[1,128,1024]{2,1,0:T(8,128)(2,1)S(1)}, u32[]{:S(2)}, u32[]{:S(2)}) collective-permute-start(bf16[1,128,1024]{2,1,0:T(8,128)(2,1)S(1)} %copy-done.19), channel_id=1, source_target_pairs={{0,8},{4,12},{8,0},{12,4},{16,24},{20,28},{24,16},{28,20},{1,9},{5... | collective-permute-start | bytes 786440 | tf_op jit(solution)/shard_map/ppermute | solution.py:26
  266.1 28.1 %collective-permute-start.38 = (bf16[184,1024]{1,0:T(8,128)(2,1)}, bf16[184,1024]{1,0:T(8,128)(2,1)S(1)}, u32[]{:S(2)}, u32[]{:S(2)}) collective-permute-start(bf16[184,1024]{1,0:T(8,128)(2,1)} %add_convert_fusion.1), channel_id=1, source_target_pairs={{0,8},{4,12},{8,0},{12,4},{16,24},{20,28},{24,16},{28,20},{1,9},{5... | collective-permute-start | bytes 1130504 | tf_op jit(solution)/shard_map/ppermute | solution.py:26
  266.9 30.1 %collective-permute-start.44 = (bf16[1,128,1024]{2,1,0:T(8,128)(2,1)}, bf16[1,128,1024]{2,1,0:T(8,128)(2,1)}, u32[]{:S(2)}, u32[]{:S(2)}) collective-permute-start(bf16[1,128,1024]{2,1,0:T(8,128)(2,1)} %get-tuple-element.170), channel_id=1, source_target_pairs={{0,8},{4,12},{8,0},{12,4},{16,24},{20,28},{24,16},{28,20},{1,9},{5... | collective-permute-start | bytes 786440 | tf_op jit(solution)/shard_map/ppermute | solution.py:26
  271.7 25.2 %collective-permute-start.43 = (bf16[1,128,1024]{2,1,0:T(8,128)(2,1)}, bf16[1,128,1024]{2,1,0:T(8,128)(2,1)S(1)}, u32[]{:S(2)}, u32[]{:S(2)}) collective-permute-start(bf16[1,128,1024]{2,1,0:T(8,128)(2,1)} %get-tuple-element.168), channel_id=1, source_target_pairs={{0,16},{4,20},{8,24},{12,28},{16,0},{20,4},{24,8},{28,12},{1,17},{... | collective-permute-start | bytes 786440 | tf_op jit(solution)/shard_map/ppermute | solution.py:26
  273.6 11.6 %collective-permute-start.47 = (bf16[2,2,16,1024]{3,2,0,1:T(8,128)(2,1)S(1)}, bf16[2,2,16,1024]{3,2,0,1:T(8,128)(2,1)S(1)}, u32[]{:S(2)}, u32[]{:S(2)}) collective-permute-start(bf16[2,2,16,1024]{3,2,0,1:T(8,128)(2,1)S(1)} %fusion.14), channel_id=1, source_target_pairs={{0,4},{4,0},{8,12},{12,8},{16,20},{20,16},{24,28},{28,24},{1,5},{5... | collective-permute-start | bytes 393224 | tf_op jit(solution)/shard_map/ppermute | solution.py:26
  295.3 8.5 %collective-permute-start.39 = (bf16[184,1024]{1,0:T(8,128)(2,1)S(1)}, bf16[184,1024]{1,0:T(8,128)(2,1)S(1)}, u32[]{:S(2)}, u32[]{:S(2)}) collective-permute-start(bf16[184,1024]{1,0:T(8,128)(2,1)S(1)} %add_convert_fusion), channel_id=1, source_target_pairs={{0,16},{4,20},{8,24},{12,28},{16,0},{20,4},{24,8},{28,12},{1,17},{... | collective-permute-start | bytes 1130504 | tf_op jit(solution)/shard_map/ppermute | solution.py:26
  304.0 5.7 %collective-permute-start.41 = (f32[2,1024]{1,0:T(2,128)S(1)}, f32[2,1024]{1,0:T(2,128)S(1)}, u32[]{:S(2)}, u32[]{:S(2)}) collective-permute-start(f32[2,1024]{1,0:T(2,128)S(1)} %slice.191), channel_id=1, source_target_pairs={{0,2},{1,3},{2,0},{3,1},{4,6},{5,7},{6,4},{7,5},{8,10},{9,11},{10,... | collective-permute-start | bytes 24584 | tf_op jit(solution)/shard_map/ppermute | solution.py:26
  304.1 5.6 %collective-permute-start.42 = (f32[2,1024]{1,0:T(2,128)S(1)}, f32[2,1024]{1,0:T(2,128)S(1)}, u32[]{:S(2)}, u32[]{:S(2)}) collective-permute-start(f32[2,1024]{1,0:T(2,128)S(1)} %slice.191), channel_id=1, source_target_pairs={{0,3},{1,2},{2,1},{3,0},{4,7},{5,6},{6,5},{7,4},{8,11},{9,10},{10,... | collective-permute-start | bytes 24584 | tf_op jit(solution)/shard_map/ppermute | solution.py:26
  (87 other events, 1441.8 us)

commit v3 on v2

--- a/solution.py
+++ b/solution.py
@@ -182,7 +182,7 @@
     rows, model = parts[0].shape
     seq_len = rows * len(parts)
     inner = wx.shape[1]
-    wide = 256
+    wide = 512
     return pl.pallas_call(
         functools.partial(enter_kernel, len(parts)),
         grid=(inner // wide,),
@@ -213,7 +213,7 @@
         ],
         scratch_shapes=[pltpu.VMEM((wp.shape[0], seq_len), f32)],
         name="enter",
-        compiler_params=pltpu.CompilerParams(vmem_limit_bytes=20 * 1024 * 1024),
+        compiler_params=pltpu.CompilerParams(vmem_limit_bytes=28 * 1024 * 1024),
         cost_estimate=takes(9),
     )(offs, *parts, gain, masks, wx, wz, taps, bias, wp)
 
@@ -738,6 +738,8 @@
 
 
 class PlainGradScatter:
+    h1 = h2 = ()
+
     def __init__(self, lefts, rights, place):
         self.lefts, self.rights = lefts, rights
 
@@ -897,14 +899,15 @@
     z_sum.send_second(out_sum.rest())
     x_sum = scatter([normed], [[g_x_in[0], after(g_x_in[1], z_sum.rest())]], place)
     x_sum.send_core()
+    x_sum.send_first()
+    gn[1].got = after(gn[1].got, x_sum.rest())
     gn[1].mid()
     gn[1].send()
-    x_sum.send_first()
     packed = jnp.concatenate(
         [sum(proj_part), sum(rows_part), sum(small), jnp.concatenate([sum(gain_part).reshape(-1, inner)] * 4, 0)], 0
     )
     packed = all_sum(after(packed, x_sum.rest()), "dp")
-    x_sum.send_second(branch[1].got)
+    x_sum.send_second(branch[1].got, out_sum.h1, out_sum.h2, z_sum.h1, z_sum.h2)
     gain_rows = packed[proj_weight.shape[0] + 16 : proj_weight.shape[0] + 16 + model // inner]
     gain_grad = total_of(exchange_all(gain_rows, "fsdp")).reshape(-1) / gain
     (out_grad,), (in_z_grad,), (in_x_grad,) = out_sum.finish(x_sum.rest()), z_sum.finish(x_sum.rest()), x_sum.finish()

time: 311 us -> 307 us (0.987)
  waiting for transfers between devices: 72.8 us -> 77.9 us
  starting transfers between devices: 76.8 us -> 72.5 us
  local copies, waits for them, and re-layouts: 27.2 us -> 23.4 us
    ppermute x52, waiting for transfers between devices: 72.8 us -> 77.9 us  [swap(): lax.ppermute(x, axis, [(i, i ^ bit) for i in range(lax.axis_size(axis))])]
    ppermute x52, starting transfers between devices: 76.8 us -> 72.5 us  [swap(): lax.ppermute(x, axis, [(i, i ^ bit) for i in range(lax.axis_size(axis))])]
    unnamed x167 -> x157, local copies, waits for them, and re-layouts: 18.2 us -> 15.1 us
  transfers between devices with their start and end apart: 52 -> 52, of which waited for: 21 -> 18; matrix products, arithmetic and copies ran while one was open for 9% -> 10% of each run, Pallas kernels for 34% -> 34%
where the time goes in v3:
time: 307 us; the launch traced here: 306 us
  Pallas kernels  109 us (36%)
  waiting for transfers between devices  77.9 us (25%)
  starting transfers between devices  72.5 us (24%)
  local copies, waits for them, and re-layouts  23.4 us (8%)
  other arithmetic  21.6 us (7%)
    ppermute x52, waiting for transfers between devices, swap(): lax.ppermute(x, axis, [(i, i ^ bit) for i in range(lax.axis_size(axis))])  77.9 us
    ppermute x52, starting transfers between devices, swap(): lax.ppermute(x, axis, [(i, i ^ bit) for i in range(lax.axis_size(axis))])  72.5 us
    pallas_call x2, Pallas kernels, recurrence(): pl.pallas_call(functools.partial(recurrence_kernel, state_dim, rank, len(...  56.3 us
    pallas_call x2, Pallas kernels, leave(): pl.pallas_call(functools.partial(leave_kernel, len(terms)), grid=(inner /...  16.2 us
    unnamed x157, local copies, waits for them, and re-layouts  15.1 us
    pallas_call x2, Pallas kernels, enter(): pl.pallas_call(functools.partial(enter_kernel, len(parts)), grid=(inner /...  14.8 us
    pallas_call x3, Pallas kernels, send_first(): pl.pallas_call(functools.partial(grad_keep_kernel, self.pairs, self.count...  10.8 us
    pallas_call x3, Pallas kernels, send_core(): pl.pallas_call(functools.partial(grad_send_kernel, self.pairs, self.count...  9.01 us
  transfers between devices with their start and end apart: 52, of which 18 were waited for; matrix products, arithmetic and copies ran while one was open for 10% of the time, Pallas kernels for 34%

profile of v3, /device:TPU:0, one launch (start us, length us, event | category | flops | bytes accessed | tf_op | source)
XLA Modules:
  0.0 306.5 jit_solution(4483964474790908986)
XLA Ops:
  1.8 3.1 %collective-permute-start = (bf16[64,2048]{1,0:T(8,128)(2,1)S(1)}, bf16[64,2048]{1,0:T(8,128)(2,1)S(1)}, u32[]{:S(2)}, u32[]{:S(2)}) collective-permute-start(bf16[64,2048]{1,0:T(8,128)(2,1)S(1)} %get-tuple-element.159.refs_0_), channel_id=1, source_target_pairs={{0,1},{1,0},{2,3},{3,2},{4,5},{5,4},{6,7},{7,6},{8,9},{9,8},{10,11... | collective-permute-start | bytes 786440 | tf_op jit(solution)/shard_map/ppermute | solution.py:26
  4.9 2.6 collective-permute-start.1
  8.4 1.9 slice_bitcast_fusion.2
  10.8 5.2 %collective-permute-done.refs_1_ = bf16[64,2048]{1,0:T(8,128)(2,1)S(1)} collective-permute-done((bf16[64,2048]{1,0:T(8,128)(2,1)S(1)}, bf16[64,2048]{1,0:T(8,128)(2,1)S(1)}, u32[]{:S(2)}, u32[]{:S(2)}) %collective-permute-start) | collective-permute-done | bytes 262176 | tf_op jit(solution)/shard_map/ppermute | solution.py:26
  16.0 3.8 %collective-permute-start.7 = (bf16[64,2048]{1,0:T(8,128)(2,1)}, bf16[64,2048]{1,0:T(8,128)(2,1)}, u32[]{:S(2)}, u32[]{:S(2)}) collective-permute-start(bf16[64,2048]{1,0:T(8,128)(2,1)} %get-tuple-element.102.refs_0_), channel_id=1, source_target_pairs={{0,2},{1,3},{2,0},{3,1},{4,6},{5,7},{6,4},{7,5},{8,10},{9,11},{10,... | collective-permute-start | bytes 786440 | tf_op jit(solution)/shard_map/ppermute | solution.py:26
  19.8 6.5 %collective-permute-done.1.refs_2_ = bf16[64,2048]{1,0:T(8,128)(2,1)S(1)} collective-permute-done((bf16[64,2048]{1,0:T(8,128)(2,1)S(1)}, bf16[64,2048]{1,0:T(8,128)(2,1)S(1)}, u32[]{:S(2)}, u32[]{:S(2)}) %collective-permute-start.1) | collective-permute-done | bytes 262176 | tf_op jit(solution)/shard_map/ppermute | solution.py:26
  27.7 7.4 %enter.2 = (bf16[256,2048]{1,0:T(8,128)(2,1)S(1)}, bf16[256,1024]{1,0:T(8,128)(2,1)S(1)}, f32[256,1024]{1,0:T(8,128)S(1)}, bf16[256,1024]{1,0:T(8,128)(2,1)S(1)}, bf16[160,256]{1,0:T(8,128)(2,1)S(1)}) custom-call(s32[1,4]{1,0:T(1,128)S(1)} %add_bitcast_fusion.7.offs_ref, bf16[64,2048]{1,0:T(8,128)(2,1)} %copy-done.37, bf16[64,2048]{1,0:T(8,128)(2,1)} %copy-done.66, ...), custom_call_target="tpu_custom_call" | custom-call | flops 8099999744 | bytes 1 | tf_op jit(solution)/shard_map/enter/pallas_call | solution.py:186
  36.1 11.1 %collective-permute-start.9 = (bf16[160,256]{1,0:T(8,128)(2,1)S(1)}, bf16[160,256]{1,0:T(8,128)(2,1)S(1)}, u32[]{:S(2)}, u32[]{:S(2)}) collective-permute-start(bf16[160,256]{1,0:T(8,128)(2,1)S(1)} %get-tuple-element.104), channel_id=1, source_target_pairs={{0,1},{1,0},{2,3},{3,2},{4,5},{5,4},{6,7},{7,6},{8,9},{9,8},{10,11... | collective-permute-start | bytes 245768 | tf_op jit(solution)/shard_map/ppermute | solution.py:26
  47.5 3.0 collective-permute-start.5
  51.1 2.6 collective-permute-start.10
  53.8 9.4 %collective-permute-done.4.refs_1_ = bf16[64,2048]{1,0:T(8,128)(2,1)S(1)} collective-permute-done((bf16[64,2048]{1,0:T(8,128)(2,1)S(1)}, bf16[64,2048]{1,0:T(8,128)(2,1)S(1)}, u32[]{:S(2)}, u32[]{:S(2)}) %collective-permute-start.4) | collective-permute-done | bytes 262176 | tf_op jit(solution)/shard_map/ppermute | solution.py:26
  63.2 3.2 %collective-permute-start.15 = (bf16[64,2048]{1,0:T(8,128)(2,1)}, bf16[64,2048]{1,0:T(8,128)(2,1)S(1)}, u32[]{:S(2)}, u32[]{:S(2)}) collective-permute-start(bf16[64,2048]{1,0:T(8,128)(2,1)} %get-tuple-element.117.refs_0_), channel_id=1, source_target_pairs={{0,2},{1,3},{2,0},{3,1},{4,6},{5,7},{6,4},{7,5},{8,10},{9,11},{10,... | collective-permute-start | bytes 786440 | tf_op jit(solution)/shard_map/ppermute | solution.py:26
  66.4 1.6 collective-permute-done.10.refs_5_
  68.0 3.0 collective-permute-done.8.refs_3_
  71.8 27.7 %recurrence.2 = (bf16[256,1024]{1,0:T(8,128)(2,1)S(1)}, bf16[256,1024]{1,0:T(8,128)(2,1)S(1)}, f32[256,1024]{1,0:T(8,128)S(1)}, bf16[160,256]{1,0:T(8,128)(2,1)S...) custom-call(f32[1,32]{1,0:T(1,128)S(1)} %get-tuple-element.249.keep_, ...), custom_call_target="tpu_custom_call" | custom-call | flops 27000000512 | bytes 1 | tf_op jit(solution)/shard_map/recurrence/pallas_call | solution.py:533
  102.3 7.4 %enter.3 = (bf16[256,2048]{1,0:T(8,128)(2,1)S(1)}, bf16[256,1024]{1,0:T(8,128)(2,1)S(1)}, f32[256,1024]{1,0:T(8,128)S(1)}, bf16[256,1024]{1,0:T(8,128)(2,1)S(1)}, bf16[160,256]{1,0:T(8,128)(2,1)S(1)}) custom-call(s32[1,4]{1,0:T(1,128)S(1)} %add_bitcast_fusion.7.offs_ref, bf16[64,2048]{1,0:T(8,128)(2,1)} %copy-done.39, bf16[64,2048]{1,0:T(8,128)(2,1)} %copy-done.69, ...), custom_call_target="tpu_custom_call" | custom-call | flops 8099999744 | bytes 1 | tf_op jit(solution)/shard_map/enter/pallas_call | solution.py:186
  111.0 3.4 %collective-permute-start.12 = (bf16[160,256]{1,0:T(8,128)(2,1)S(1)}, bf16[160,256]{1,0:T(8,128)(2,1)S(1)}, u32[]{:S(2)}, u32[]{:S(2)}) collective-permute-start(bf16[160,256]{1,0:T(8,128)(2,1)S(1)} %add_convert_fusion.8.refs_0_), channel_id=1, source_target_pairs={{0,2},{1,3},{2,0},{3,1},{4,6},{5,7},{6,4},{7,5},{8,10},{9,11},{10,... | collective-permute-start | bytes 245768 | tf_op jit(solution)/shard_map/ppermute | solution.py:26
  114.7 4.1 %collective-permute-start.17 = (bf16[160,256]{1,0:T(8,128)(2,1)S(1)}, bf16[160,256]{1,0:T(8,128)(2,1)S(1)}, u32[]{:S(2)}, u32[]{:S(2)}) collective-permute-start(bf16[160,256]{1,0:T(8,128)(2,1)S(1)} %add_convert_fusion.7.refs_4_), channel_id=1, source_target_pairs={{0,2},{1,3},{2,0},{3,1},{4,6},{5,7},{6,4},{7,5},{8,10},{9,11},{10,... | collective-permute-start | bytes 245768 | tf_op jit(solution)/shard_map/ppermute | solution.py:26
  119.4 7.7 %leave.2 = (bf16[256,1024]{1,0:T(8,128)(2,1)S(1)}, f32[8,1024]{1,0:T(8,128)S(1)}, f32[160,1024]{1,0:T(8,128)S(1)}, f32[1,2048]{1,0:T(1,128)S(1)}, bf16[2,64,2048...) custom-call(s32[1,4]{1,0:T(1,128)S(1)} %add_bitcast_fusion.7.offs_ref, bf16[160,256]{1,0:T(8,128)(2,1)} %copy-done.54, ...), custom_call_target="tpu_custom_call" | custom-call | flops 8999999488 | bytes 1 | tf_op jit(solution)/shard_map/leave/pallas_call | solution.py:278
  127.1 3.0 collective-permute-start.22
  131.2 28.6 %recurrence.3 = (bf16[256,1024]{1,0:T(8,128)(2,1)S(1)}, bf16[256,1024]{1,0:T(8,128)(2,1)S(1)}, f32[256,1024]{1,0:T(8,128)S(1)}, bf16[160,256]{1,0:T(8,128)(2,1)S...) custom-call(f32[1,32]{1,0:T(1,128)S(1)} %get-tuple-element.250.keep_, ...), custom_call_target="tpu_custom_call" | custom-call | flops 27000000512 | bytes 1 | tf_op jit(solution)/shard_map/recurrence/pallas_call | solution.py:533
  159.8 2.7 grad_send.4
  162.6 2.6 grad_send.3
  166.8 3.5 %collective-permute-done.18 = bf16[160,256]{1,0:T(8,128)(2,1)S(1)} collective-permute-done((bf16[160,256]{1,0:T(8,128)(2,1)S(1)}, bf16[160,256]{1,0:T(8,128)(2,1)S(1)}, u32[]{:S(2)}, u32[]{:S(2)}) %collective-permute-start.18) | collective-permute-done | bytes 81952 | tf_op jit(solution)/shard_map/ppermute | solution.py:26
  170.3 2.9 collective-permute-start.19
  173.2 3.0 grad_keep.4
  176.3 1.6 collective-permute-start.27
  179.3 3.0 grad_keep.3
  184.1 8.5 %leave.3 = (bf16[256,1024]{1,0:T(8,128)(2,1)S(1)}, f32[8,1024]{1,0:T(8,128)S(1)}, f32[160,1024]{1,0:T(8,128)S(1)}, f32[1,2048]{1,0:T(1,128)S(1)}, bf16[2,64,2048...) custom-call(s32[1,4]{1,0:T(1,128)S(1)} %copy-done.14, bf16[160,256]{1,0:T(8,128)(2,1)} %copy-done.51, ...), custom_call_target="tpu_custom_call" | custom-call | flops 8999999488 | bytes 1 | tf_op jit(solution)/shard_map/leave/pallas_call | solution.py:278
  192.6 7.5 %collective-permute-done.25.g1_ref = bf16[1,2,128,1024]{3,2,1,0:T(8,128)(2,1)S(1)} collective-permute-done((bf16[1,2,128,1024]{3,2,1,0:T(8,128)(2,1)S(1)}, bf16[1,2,128,1024]{3,2,1,0:T(8,128)(2,1)S(1)}, u32[]{:S(2)}, u32[]{:S(2)}) %collective-permute-start.25) | collective-permute-done | bytes 524320 | tf_op jit(solution)/shard_map/ppermute | solution.py:26
  206.1 3.7 %grad_send.5 = bf16[1,4,256,1024]{3,2,1,0:T(8,128)(2,1)} custom-call(s32[3]{0:T(128)S(1)} %pad_add_fusion.place_ref, bf16[256,2048]{1,0:T(8,128)(2,1)S(1)} %copy-done.25, bf16[256,2048]{1,0:T(8,128)(2,1)S(1)} %get-tuple-element.109.refs_1_.refs_12_, bf16[256,1024]{1,0:T(8,128)(2,1)S(1)} %get-tuple-element.116.refs_2_, ...), custom_call_target="tpu_custom_call" | custom-call | flops 4950000128 | bytes 1 | tf_op jit(solution)/shard_map/grad_send/pallas_call | solution.py:658
  211.9 1.9 add.261
  213.8 10.7 %collective-permute-done.30 = bf16[2,64,2048]{2,1,0:T(8,128)(2,1)} collective-permute-done((bf16[2,64,2048]{2,1,0:T(8,128)(2,1)}, bf16[2,64,2048]{2,1,0:T(8,128)(2,1)}, u32[]{:S(2)}, u32[]{:S(2)}) %collective-permute-start.30) | collective-permute-done | bytes 524320 | tf_op jit(solution)/shard_map/ppermute | solution.py:26
  224.5 1.8 add_convert_fusion.4
  229.1 1.9 concatenate.12
  230.9 1.6 collective-permute-start.32
  233.0 8.1 %collective-permute-done.31 = bf16[1,64,2048]{2,1,0:T(8,128)(2,1)} collective-permute-done((bf16[1,64,2048]{2,1,0:T(8,128)(2,1)}, bf16[1,64,2048]{2,1,0:T(8,128)(2,1)}, u32[]{:S(2)}, u32[]{:S(2)}) %collective-permute-start.31) | collective-permute-done | bytes 262176 | tf_op jit(solution)/shard_map/ppermute | solution.py:26
  247.7 4.8 %grad_keep.5 = (bf16[1,2,128,1024]{3,2,1,0:T(8,128)(2,1)S(1)}, bf16[1,2,128,1024]{3,2,1,0:T(8,128)(2,1)S(1)}, bf16[1,2,128,1024]{3,2,1,0:T(8,128)(2,1)S(1)}, bf16[1,2,128,1024]{3,2,1,0:T(8,128)(2,1)S(1)}) custom-call(s32[3]{0:T(128)S(1)} %copy-done.16, bf16[256,2048]{1,0:T(8,128)(2,1)S(1)} %copy-done.26, bf16[256,2048]{1,0:T(8,128)(2,1)S(1)} %copy-done.28, ...), custom_call_target="tpu_custom_call" | custom-call | flops 5849999872 | bytes 1 | tf_op jit(solution)/shard_map/grad_keep/pallas_call | solution.py:684
  255.7 3.0 collective-permute-start.40
  260.1 7.5 %collective-permute-done.36.g1_ref = bf16[1,2,128,1024]{3,2,1,0:T(8,128)(2,1)S(1)} collective-permute-done((bf16[1,2,128,1024]{3,2,1,0:T(8,128)(2,1)S(1)}, bf16[1,2,128,1024]{3,2,1,0:T(8,128)(2,1)S(1)}, u32[]{:S(2)}, u32[]{:S(2)}) %collective-permute-start.36) | collective-permute-done | bytes 524320 | tf_op jit(solution)/shard_map/ppermute | solution.py:26
  270.6 4.6 %collective-permute-done.40 = bf16[1,64,2048]{2,1,0:T(8,128)(2,1)S(1)} collective-permute-done((bf16[1,64,2048]{2,1,0:T(8,128)(2,1)S(1)}, bf16[1,64,2048]{2,1,0:T(8,128)(2,1)S(1)}, u32[]{:S(2)}, u32[]{:S(2)}) %collective-permute-start.40) | collective-permute-done | bytes 262176 | tf_op jit(solution)/shard_map/ppermute | solution.py:26
  275.3 2.0 fusion.1
  277.4 1.6 fusion.4
  283.9 1.7 collective-permute-done.50
  287.7 2.0 collective-permute-done.51
  295.2 4.8 %collective-permute-done.43 = bf16[184,1024]{1,0:T(8,128)(2,1)S(1)} collective-permute-done((bf16[184,1024]{1,0:T(8,128)(2,1)S(1)}, bf16[184,1024]{1,0:T(8,128)(2,1)S(1)}, u32[]{:S(2)}, u32[]{:S(2)}) %collective-permute-start.43) | collective-permute-done | bytes 376864 | tf_op jit(solution)/shard_map/ppermute | solution.py:26
  300.2 1.9 collective-permute-start.46
  302.1 1.6 collective-permute-start.44
  (292 shorter events, 58.4 us)
Async XLA Ops:
  1.8 14.2 %collective-permute-start = (bf16[64,2048]{1,0:T(8,128)(2,1)S(1)}, bf16[64,2048]{1,0:T(8,128)(2,1)S(1)}, u32[]{:S(2)}, u32[]{:S(2)}) collective-permute-start(bf16[64,2048]{1,0:T(8,128)(2,1)S(1)} %get-tuple-element.159.refs_0_), channel_id=1, source_target_pairs={{0,1},{1,0},{2,3},{3,2},{4,5},{5,4},{6,7},{7,6},{8,9},{9,8},{10,11... | collective-permute-start | bytes 786440 | tf_op jit(solution)/shard_map/ppermute | solution.py:26
  4.9 21.4 %collective-permute-start.1 = (bf16[64,2048]{1,0:T(8,128)(2,1)S(1)}, bf16[64,2048]{1,0:T(8,128)(2,1)S(1)}, u32[]{:S(2)}, u32[]{:S(2)}) collective-permute-start(bf16[64,2048]{1,0:T(8,128)(2,1)S(1)} %get-tuple-element.159.refs_0_), channel_id=1, source_target_pairs={{0,2},{1,3},{2,0},{3,1},{4,6},{5,7},{6,4},{7,5},{8,10},{9,11},{10,... | collective-permute-start | bytes 786440 | tf_op jit(solution)/shard_map/ppermute | solution.py:26
  7.5 18.8 %collective-permute-start.2 = (bf16[64,2048]{1,0:T(8,128)(2,1)S(1)}, bf16[64,2048]{1,0:T(8,128)(2,1)S(1)}, u32[]{:S(2)}, u32[]{:S(2)}) collective-permute-start(bf16[64,2048]{1,0:T(8,128)(2,1)S(1)} %get-tuple-element.159.refs_0_), channel_id=1, source_target_pairs={{0,3},{1,2},{2,1},{3,0},{4,7},{5,6},{6,5},{7,4},{8,11},{9,10},{10,... | collective-permute-start | bytes 786440 | tf_op jit(solution)/shard_map/ppermute | solution.py:26
  16.0 31.4 %collective-permute-start.3 = (bf16[64,2048]{1,0:T(8,128)(2,1)}, bf16[64,2048]{1,0:T(8,128)(2,1)}, u32[]{:S(2)}, u32[]{:S(2)}) collective-permute-start(bf16[64,2048]{1,0:T(8,128)(2,1)} %get-tuple-element.102.refs_0_), channel_id=1, source_target_pairs={{0,1},{1,0},{2,3},{3,2},{4,5},{5,4},{6,7},{7,6},{8,9},{9,8},{10,11... | collective-permute-start | bytes 786440 | tf_op jit(solution)/shard_map/ppermute | solution.py:26
  16.0 34.5 %collective-permute-start.7 = (bf16[64,2048]{1,0:T(8,128)(2,1)}, bf16[64,2048]{1,0:T(8,128)(2,1)}, u32[]{:S(2)}, u32[]{:S(2)}) collective-permute-start(bf16[64,2048]{1,0:T(8,128)(2,1)} %get-tuple-element.102.refs_0_), channel_id=1, source_target_pairs={{0,2},{1,3},{2,0},{3,1},{4,6},{5,7},{6,4},{7,5},{8,10},{9,11},{10,... | collective-permute-start | bytes 786440 | tf_op jit(solution)/shard_map/ppermute | solution.py:26
  36.1 15.0 %collective-permute-start.9 = (bf16[160,256]{1,0:T(8,128)(2,1)S(1)}, bf16[160,256]{1,0:T(8,128)(2,1)S(1)}, u32[]{:S(2)}, u32[]{:S(2)}) collective-permute-start(bf16[160,256]{1,0:T(8,128)(2,1)S(1)} %get-tuple-element.104), channel_id=1, source_target_pairs={{0,1},{1,0},{2,3},{3,2},{4,5},{5,4},{6,7},{7,6},{8,9},{9,8},{10,11... | collective-permute-start | bytes 245768 | tf_op jit(solution)/shard_map/ppermute | solution.py:26
  47.4 15.8 %collective-permute-start.4 = (bf16[64,2048]{1,0:T(8,128)(2,1)S(1)}, bf16[64,2048]{1,0:T(8,128)(2,1)S(1)}, u32[]{:S(2)}, u32[]{:S(2)}) collective-permute-start(bf16[64,2048]{1,0:T(8,128)(2,1)S(1)} %get-tuple-element.160.refs_0_), channel_id=1, source_target_pairs={{0,1},{1,0},{2,3},{3,2},{4,5},{5,4},{6,7},{7,6},{8,9},{9,8},{10,11... | collective-permute-start | bytes 786440 | tf_op jit(solution)/shard_map/ppermute | solution.py:26
  47.5 18.9 %collective-permute-start.5 = (bf16[64,2048]{1,0:T(8,128)(2,1)S(1)}, bf16[64,2048]{1,0:T(8,128)(2,1)S(1)}, u32[]{:S(2)}, u32[]{:S(2)}) collective-permute-start(bf16[64,2048]{1,0:T(8,128)(2,1)S(1)} %get-tuple-element.160.refs_0_), channel_id=1, source_target_pairs={{0,2},{1,3},{2,0},{3,1},{4,6},{5,7},{6,4},{7,5},{8,10},{9,11},{10,... | collective-permute-start | bytes 786440 | tf_op jit(solution)/shard_map/ppermute | solution.py:26
  50.5 20.5 %collective-permute-start.8 = (bf16[64,2048]{1,0:T(8,128)(2,1)}, bf16[64,2048]{1,0:T(8,128)(2,1)S(1)}, u32[]{:S(2)}, u32[]{:S(2)}) collective-permute-start(bf16[64,2048]{1,0:T(8,128)(2,1)} %collective-permute-done.7.refs_2_), channel_id=1, source_target_pairs={{0,1},{1,0},{2,3},{3,2},{4,5},{5,4},{6,7},{7,6},{8,9},{9,8},{10,11... | collective-permute-start | bytes 786440 | tf_op jit(solution)/shard_map/ppermute | solution.py:26
  51.1 16.9 %collective-permute-start.10 = (bf16[160,256]{1,0:T(8,128)(2,1)S(1)}, bf16[160,256]{1,0:T(8,128)(2,1)S(1)}, u32[]{:S(2)}, u32[]{:S(2)}) collective-permute-start(bf16[160,256]{1,0:T(8,128)(2,1)S(1)} %add_convert_fusion.9.refs_4_), channel_id=1, source_target_pairs={{0,2},{1,3},{2,0},{3,1},{4,6},{5,7},{6,4},{7,5},{8,10},{9,11},{10,... | collective-permute-start | bytes 245768 | tf_op jit(solution)/shard_map/ppermute | solution.py:26
  63.2 67.1 %collective-permute-start.14 = (bf16[64,2048]{1,0:T(8,128)(2,1)}, bf16[64,2048]{1,0:T(8,128)(2,1)S(1)}, u32[]{:S(2)}, u32[]{:S(2)}) collective-permute-start(bf16[64,2048]{1,0:T(8,128)(2,1)} %get-tuple-element.117.refs_0_), channel_id=1, source_target_pairs={{0,1},{1,0},{2,3},{3,2},{4,5},{5,4},{6,7},{7,6},{8,9},{9,8},{10,11... | collective-permute-start | bytes 786440 | tf_op jit(solution)/shard_map/ppermute | solution.py:26
  63.2 51.3 %collective-permute-start.15 = (bf16[64,2048]{1,0:T(8,128)(2,1)}, bf16[64,2048]{1,0:T(8,128)(2,1)S(1)}, u32[]{:S(2)}, u32[]{:S(2)}) collective-permute-start(bf16[64,2048]{1,0:T(8,128)(2,1)} %get-tuple-element.117.refs_0_), channel_id=1, source_target_pairs={{0,2},{1,3},{2,0},{3,1},{4,6},{5,7},{6,4},{7,5},{8,10},{9,11},{10,... | collective-permute-start | bytes 786440 | tf_op jit(solution)/shard_map/ppermute | solution.py:26
  66.4 35.2 %collective-permute-start.6 = (bf16[64,2048]{1,0:T(8,128)(2,1)S(1)}, bf16[64,2048]{1,0:T(8,128)(2,1)S(1)}, u32[]{:S(2)}, u32[]{:S(2)}) collective-permute-start(bf16[64,2048]{1,0:T(8,128)(2,1)S(1)} %collective-permute-done.5.refs_2_), channel_id=1, source_target_pairs={{0,1},{1,0},{2,3},{3,2},{4,5},{5,4},{6,7},{7,6},{8,9},{9,8},{10,11... | collective-permute-start | bytes 786440 | tf_op jit(solution)/shard_map/ppermute | solution.py:26
  99.5 11.5 %collective-permute-start.11 = (bf16[160,256]{1,0:T(8,128)(2,1)S(1)}, bf16[160,256]{1,0:T(8,128)(2,1)S(1)}, u32[]{:S(2)}, u32[]{:S(2)}) collective-permute-start(bf16[160,256]{1,0:T(8,128)(2,1)S(1)} %get-tuple-element.110), channel_id=1, source_target_pairs={{0,1},{1,0},{2,3},{3,2},{4,5},{5,4},{6,7},{7,6},{8,9},{9,8},{10,11... | collective-permute-start | bytes 245768 | tf_op jit(solution)/shard_map/ppermute | solution.py:26
  100.8 29.4 %collective-permute-start.20 = (bf16[2,64,2048]{2,1,0:T(8,128)(2,1)S(1)}, bf16[2,64,2048]{2,1,0:T(8,128)(2,1)S(1)}, u32[]{:S(2)}, u32[]{:S(2)}) collective-permute-start(bf16[2,64,2048]{2,1,0:T(8,128)(2,1)S(1)} %get-tuple-element.127), channel_id=1, source_target_pairs={{0,1},{1,0},{2,3},{3,2},{4,5},{5,4},{6,7},{7,6},{8,9},{9,8},{10,11... | collective-permute-start | bytes 1572872 | tf_op jit(solution)/shard_map/ppermute | solution.py:26
  109.7 4.9 %collective-permute-start.13 = (bf16[160,256]{1,0:T(8,128)(2,1)S(1)}, bf16[160,256]{1,0:T(8,128)(2,1)S(1)}, u32[]{:S(2)}, u32[]{:S(2)}) collective-permute-start(bf16[160,256]{1,0:T(8,128)(2,1)S(1)} %get-tuple-element.112), channel_id=1, source_target_pairs={{0,1},{1,0},{2,3},{3,2},{4,5},{5,4},{6,7},{7,6},{8,9},{9,8},{10,11... | collective-permute-start | bytes 245768 | tf_op jit(solution)/shard_map/ppermute | solution.py:26
  111.0 7.7 %collective-permute-start.12 = (bf16[160,256]{1,0:T(8,128)(2,1)S(1)}, bf16[160,256]{1,0:T(8,128)(2,1)S(1)}, u32[]{:S(2)}, u32[]{:S(2)}) collective-permute-start(bf16[160,256]{1,0:T(8,128)(2,1)S(1)} %add_convert_fusion.8.refs_0_), channel_id=1, source_target_pairs={{0,2},{1,3},{2,0},{3,1},{4,6},{5,7},{6,4},{7,5},{8,10},{9,11},{10,... | collective-permute-start | bytes 245768 | tf_op jit(solution)/shard_map/ppermute | solution.py:26
  114.5 15.9 %collective-permute-start.16 = (bf16[64,2048]{1,0:T(8,128)(2,1)S(1)}, bf16[64,2048]{1,0:T(8,128)(2,1)S(1)}, u32[]{:S(2)}, u32[]{:S(2)}) collective-permute-start(bf16[64,2048]{1,0:T(8,128)(2,1)S(1)} %collective-permute-done.15.refs_2_), channel_id=1, source_target_pairs={{0,1},{1,0},{2,3},{3,2},{4,5},{5,4},{6,7},{7,6},{8,9},{9,8},{10,11... | collective-permute-start | bytes 786440 | tf_op jit(solution)/shard_map/ppermute | solution.py:26
  114.7 15.7 %collective-permute-start.17 = (bf16[160,256]{1,0:T(8,128)(2,1)S(1)}, bf16[160,256]{1,0:T(8,128)(2,1)S(1)}, u32[]{:S(2)}, u32[]{:S(2)}) collective-permute-start(bf16[160,256]{1,0:T(8,128)(2,1)S(1)} %add_convert_fusion.7.refs_4_), channel_id=1, source_target_pairs={{0,2},{1,3},{2,0},{3,1},{4,6},{5,7},{6,4},{7,5},{8,10},{9,11},{10,... | collective-permute-start | bytes 245768 | tf_op jit(solution)/shard_map/ppermute | solution.py:26
  127.1 35.4 %collective-permute-start.22 = (bf16[2,64,2048]{2,1,0:T(8,128)(2,1)S(1)}, bf16[2,64,2048]{2,1,0:T(8,128)(2,1)S(1)}, u32[]{:S(2)}, u32[]{:S(2)}) collective-permute-start(bf16[2,64,2048]{2,1,0:T(8,128)(2,1)S(1)} %get-tuple-element.128), channel_id=1, source_target_pairs={{0,1},{1,0},{2,3},{3,2},{4,5},{5,4},{6,7},{7,6},{8,9},{9,8},{10,11... | collective-permute-start | bytes 1572872 | tf_op jit(solution)/shard_map/ppermute | solution.py:26
  130.3 32.3 %collective-permute-start.21 = (bf16[1,64,2048]{2,1,0:T(8,128)(2,1)S(1)}, bf16[1,64,2048]{2,1,0:T(8,128)(2,1)S(1)}, u32[]{:S(2)}, u32[]{:S(2)}) collective-permute-start(bf16[1,64,2048]{2,1,0:T(8,128)(2,1)S(1)} %add_convert_fusion.5), channel_id=1, source_target_pairs={{0,2},{1,3},{2,0},{3,1},{4,6},{5,7},{6,4},{7,5},{8,10},{9,11},{10,... | collective-permute-start | bytes 786440 | tf_op jit(solution)/shard_map/ppermute | solution.py:26
  162.5 10.7 %collective-permute-start.24 = (bf16[1,4,256,1024]{3,2,1,0:T(8,128)(2,1)S(1)}, bf16[1,4,256,1024]{3,2,1,0:T(8,128)(2,1)S(1)}, u32[]{:S(2)}, u32[]{:S(2)}) collective-permute-start(bf16[1,4,256,1024]{3,2,1,0:T(8,128)(2,1)S(1)} %grad_send.4), channel_id=1, source_target_pairs={{0,4},{4,0},{8,12},{12,8},{16,20},{20,16},{24,28},{28,24},{1,5},{5... | collective-permute-start | bytes 6291464 | tf_op jit(solution)/shard_map/ppermute | solution.py:26
  165.3 14.1 %collective-permute-start.23 = (bf16[1,4,256,1024]{3,2,1,0:T(8,128)(2,1)S(1)}, bf16[1,4,256,1024]{3,2,1,0:T(8,128)(2,1)S(1)}, u32[]{:S(2)}, u32[]{:S(2)}) collective-permute-start(bf16[1,4,256,1024]{3,2,1,0:T(8,128)(2,1)S(1)} %grad_send.3), channel_id=1, source_target_pairs={{0,4},{4,0},{8,12},{12,8},{16,20},{20,16},{24,28},{28,24},{1,5},{5... | collective-permute-start | bytes 6291464 | tf_op jit(solution)/shard_map/ppermute | solution.py:26
  165.8 4.4 %collective-permute-start.18 = (bf16[160,256]{1,0:T(8,128)(2,1)S(1)}, bf16[160,256]{1,0:T(8,128)(2,1)S(1)}, u32[]{:S(2)}, u32[]{:S(2)}) collective-permute-start(bf16[160,256]{1,0:T(8,128)(2,1)S(1)} %get-tuple-element.121), channel_id=1, source_target_pairs={{0,1},{1,0},{2,3},{3,2},{4,5},{5,4},{6,7},{7,6},{8,9},{9,8},{10,11... | collective-permute-start | bytes 245768 | tf_op jit(solution)/shard_map/ppermute | solution.py:26
  170.3 13.2 %collective-permute-start.19 = (bf16[160,256]{1,0:T(8,128)(2,1)S(1)}, bf16[160,256]{1,0:T(8,128)(2,1)S(1)}, u32[]{:S(2)}, u32[]{:S(2)}) collective-permute-start(bf16[160,256]{1,0:T(8,128)(2,1)S(1)} %add_convert_fusion.6.refs_0_), channel_id=1, source_target_pairs={{0,2},{1,3},{2,0},{3,1},{4,6},{5,7},{6,4},{7,5},{8,10},{9,11},{10,... | collective-permute-start | bytes 245768 | tf_op jit(solution)/shard_map/ppermute | solution.py:26
  176.3 26.6 %collective-permute-start.27 = (bf16[1,2,128,1024]{3,2,1,0:T(8,128)(2,1)S(1)}, bf16[1,2,128,1024]{3,2,1,0:T(8,128)(2,1)S(1)}, u32[]{:S(2)}, u32[]{:S(2)}) collective-permute-start(bf16[1,2,128,1024]{3,2,1,0:T(8,128)(2,1)S(1)} %get-tuple-element.142), channel_id=1, source_target_pairs={{0,8},{4,12},{8,0},{12,4},{16,24},{20,28},{24,16},{28,20},{1,9},{5... | collective-permute-start | bytes 1572872 | tf_op jit(solution)/shard_map/ppermute | solution.py:26
  177.8 25.0 %collective-permute-start.28 = (bf16[1,2,128,1024]{3,2,1,0:T(8,128)(2,1)S(1)}, bf16[1,2,128,1024]{3,2,1,0:T(8,128)(2,1)S(1)}, u32[]{:S(2)}, u32[]{:S(2)}) collective-permute-start(bf16[1,2,128,1024]{3,2,1,0:T(8,128)(2,1)S(1)} %get-tuple-element.144), channel_id=1, source_target_pairs={{0,16},{4,20},{8,24},{12,28},{16,0},{20,4},{24,8},{28,12},{1,17},{... | collective-permute-start | bytes 1572872 | tf_op jit(solution)/shard_map/ppermute | solution.py:26
  182.4 17.7 %collective-permute-start.25 = (bf16[1,2,128,1024]{3,2,1,0:T(8,128)(2,1)S(1)}, bf16[1,2,128,1024]{3,2,1,0:T(8,128)(2,1)S(1)}, u32[]{:S(2)}, u32[]{:S(2)}) collective-permute-start(bf16[1,2,128,1024]{3,2,1,0:T(8,128)(2,1)S(1)} %get-tuple-element.137), channel_id=1, source_target_pairs={{0,8},{4,12},{8,0},{12,4},{16,24},{20,28},{24,16},{28,20},{1,9},{5... | collective-permute-start | bytes 1572872 | tf_op jit(solution)/shard_map/ppermute | solution.py:26
  183.0 18.3 %collective-permute-start.26 = (bf16[1,2,128,1024]{3,2,1,0:T(8,128)(2,1)S(1)}, bf16[1,2,128,1024]{3,2,1,0:T(8,128)(2,1)S(1)}, u32[]{:S(2)}, u32[]{:S(2)}) collective-permute-start(bf16[1,2,128,1024]{3,2,1,0:T(8,128)(2,1)S(1)} %get-tuple-element.139), channel_id=1, source_target_pairs={{0,16},{4,20},{8,24},{12,28},{16,0},{20,4},{24,8},{28,12},{1,17},{... | collective-permute-start | bytes 1572872 | tf_op jit(solution)/shard_map/ppermute | solution.py:26
  209.8 32.8 %collective-permute-start.29 = (bf16[1,4,256,1024]{3,2,1,0:T(8,128)(2,1)}, bf16[1,4,256,1024]{3,2,1,0:T(8,128)(2,1)}, u32[]{:S(2)}, u32[]{:S(2)}) collective-permute-start(bf16[1,4,256,1024]{3,2,1,0:T(8,128)(2,1)} %grad_send.5), channel_id=1, source_target_pairs={{0,4},{4,0},{8,12},{12,8},{16,20},{20,16},{24,28},{28,24},{1,5},{5... | collective-permute-start | bytes 6291464 | tf_op jit(solution)/shard_map/ppermute | solution.py:26
  209.8 14.7 %collective-permute-start.30 = (bf16[2,64,2048]{2,1,0:T(8,128)(2,1)}, bf16[2,64,2048]{2,1,0:T(8,128)(2,1)}, u32[]{:S(2)}, u32[]{:S(2)}) collective-permute-start(bf16[2,64,2048]{2,1,0:T(8,128)(2,1)} %get-tuple-element.149), channel_id=1, source_target_pairs={{0,1},{1,0},{2,3},{3,2},{4,5},{5,4},{6,7},{7,6},{8,9},{9,8},{10,11... | collective-permute-start | bytes 1572872 | tf_op jit(solution)/shard_map/ppermute | solution.py:26
  226.3 14.9 %collective-permute-start.31 = (bf16[1,64,2048]{2,1,0:T(8,128)(2,1)}, bf16[1,64,2048]{2,1,0:T(8,128)(2,1)}, u32[]{:S(2)}, u32[]{:S(2)}) collective-permute-start(bf16[1,64,2048]{2,1,0:T(8,128)(2,1)} %add_convert_fusion.4), channel_id=1, source_target_pairs={{0,2},{1,3},{2,0},{3,1},{4,6},{5,7},{6,4},{7,5},{8,10},{9,11},{10,... | collective-permute-start | bytes 786440 | tf_op jit(solution)/shard_map/ppermute | solution.py:26
  227.3 27.4 %collective-permute-start.39 = (bf16[2,64,2048]{2,1,0:T(8,128)(2,1)}, bf16[2,64,2048]{2,1,0:T(8,128)(2,1)}, u32[]{:S(2)}, u32[]{:S(2)}) collective-permute-start(bf16[2,64,2048]{2,1,0:T(8,128)(2,1)} %get-tuple-element.163), channel_id=1, source_target_pairs={{0,1},{1,0},{2,3},{3,2},{4,5},{5,4},{6,7},{7,6},{8,9},{9,8},{10,11... | collective-permute-start | bytes 1572872 | tf_op jit(solution)/shard_map/ppermute | solution.py:26
  230.9 21.6 %collective-permute-start.32 = (bf16[1,128,1024]{2,1,0:T(8,128)(2,1)S(1)}, bf16[1,128,1024]{2,1,0:T(8,128)(2,1)S(1)}, u32[]{:S(2)}, u32[]{:S(2)}) collective-permute-start(bf16[1,128,1024]{2,1,0:T(8,128)(2,1)S(1)} %copy-done.20), channel_id=1, source_target_pairs={{0,16},{4,20},{8,24},{12,28},{16,0},{20,4},{24,8},{28,12},{1,17},{... | collective-permute-start | bytes 786440 | tf_op jit(solution)/shard_map/ppermute | solution.py:26
  232.5 20.1 %collective-permute-start.33 = (bf16[1,128,1024]{2,1,0:T(8,128)(2,1)S(1)}, bf16[1,128,1024]{2,1,0:T(8,128)(2,1)S(1)}, u32[]{:S(2)}, u32[]{:S(2)}) collective-permute-start(bf16[1,128,1024]{2,1,0:T(8,128)(2,1)S(1)} %copy-done.18), channel_id=1, source_target_pairs={{0,8},{4,12},{8,0},{12,4},{16,24},{20,28},{24,16},{28,20},{1,9},{5... | collective-permute-start | bytes 786440 | tf_op jit(solution)/shard_map/ppermute | solution.py:26
  241.1 11.5 %collective-permute-start.34 = (bf16[1,128,1024]{2,1,0:T(8,128)(2,1)}, bf16[1,128,1024]{2,1,0:T(8,128)(2,1)S(1)}, u32[]{:S(2)}, u32[]{:S(2)}) collective-permute-start(bf16[1,128,1024]{2,1,0:T(8,128)(2,1)} %copy-done.22), channel_id=1, source_target_pairs={{0,16},{4,20},{8,24},{12,28},{16,0},{20,4},{24,8},{28,12},{1,17},{... | collective-permute-start | bytes 786440 | tf_op jit(solution)/shard_map/ppermute | solution.py:26
  242.6 10.0 %collective-permute-start.35 = (bf16[1,128,1024]{2,1,0:T(8,128)(2,1)}, bf16[1,128,1024]{2,1,0:T(8,128)(2,1)S(1)}, u32[]{:S(2)}, u32[]{:S(2)}) collective-permute-start(bf16[1,128,1024]{2,1,0:T(8,128)(2,1)} %copy-done.21), channel_id=1, source_target_pairs={{0,8},{4,12},{8,0},{12,4},{16,24},{20,28},{24,16},{28,20},{1,9},{5... | collective-permute-start | bytes 786440 | tf_op jit(solution)/shard_map/ppermute | solution.py:26
  252.5 18.0 %collective-permute-start.38 = (bf16[1,64,2048]{2,1,0:T(8,128)(2,1)S(1)}, bf16[1,64,2048]{2,1,0:T(8,128)(2,1)S(1)}, u32[]{:S(2)}, u32[]{:S(2)}) collective-permute-start(bf16[1,64,2048]{2,1,0:T(8,128)(2,1)S(1)} %copy-done.48), channel_id=1, source_target_pairs={{0,2},{1,3},{2,0},{3,1},{4,6},{5,7},{6,4},{7,5},{8,10},{9,11},{10,... | collective-permute-start | bytes 786440 | tf_op jit(solution)/shard_map/ppermute | solution.py:26
  252.6 14.9 %collective-permute-start.36 = (bf16[1,2,128,1024]{3,2,1,0:T(8,128)(2,1)S(1)}, bf16[1,2,128,1024]{3,2,1,0:T(8,128)(2,1)S(1)}, u32[]{:S(2)}, u32[]{:S(2)}) collective-permute-start(bf16[1,2,128,1024]{3,2,1,0:T(8,128)(2,1)S(1)} %get-tuple-element.155), channel_id=1, source_target_pairs={{0,8},{4,12},{8,0},{12,4},{16,24},{20,28},{24,16},{28,20},{1,9},{5... | collective-permute-start | bytes 1572872 | tf_op jit(solution)/shard_map/ppermute | solution.py:26
  254.2 13.4 %collective-permute-start.37 = (bf16[1,2,128,1024]{3,2,1,0:T(8,128)(2,1)S(1)}, bf16[1,2,128,1024]{3,2,1,0:T(8,128)(2,1)S(1)}, u32[]{:S(2)}, u32[]{:S(2)}) collective-permute-start(bf16[1,2,128,1024]{3,2,1,0:T(8,128)(2,1)S(1)} %get-tuple-element.157), channel_id=1, source_target_pairs={{0,16},{4,20},{8,24},{12,28},{16,0},{20,4},{24,8},{28,12},{1,17},{... | collective-permute-start | bytes 1572872 | tf_op jit(solution)/shard_map/ppermute | solution.py:26
  255.7 19.5 %collective-permute-start.40 = (bf16[1,64,2048]{2,1,0:T(8,128)(2,1)S(1)}, bf16[1,64,2048]{2,1,0:T(8,128)(2,1)S(1)}, u32[]{:S(2)}, u32[]{:S(2)}) collective-permute-start(bf16[1,64,2048]{2,1,0:T(8,128)(2,1)S(1)} %add_convert_fusion.2), channel_id=1, source_target_pairs={{0,2},{1,3},{2,0},{3,1},{4,6},{5,7},{6,4},{7,5},{8,10},{9,11},{10,... | collective-permute-start | bytes 786440 | tf_op jit(solution)/shard_map/ppermute | solution.py:26
  259.6 30.8 %collective-permute-start.42 = (bf16[184,1024]{1,0:T(8,128)(2,1)}, bf16[184,1024]{1,0:T(8,128)(2,1)}, u32[]{:S(2)}, u32[]{:S(2)}) collective-permute-start(bf16[184,1024]{1,0:T(8,128)(2,1)} %add_convert_fusion.1), channel_id=1, source_target_pairs={{0,8},{4,12},{8,0},{12,4},{16,24},{20,28},{24,16},{28,20},{1,9},{5... | collective-permute-start | bytes 1130504 | tf_op jit(solution)/shard_map/ppermute | solution.py:26
  268.5 24.7 %collective-permute-start.48 = (bf16[1,128,1024]{2,1,0:T(8,128)(2,1)S(1)}, bf16[1,128,1024]{2,1,0:T(8,128)(2,1)}, u32[]{:S(2)}, u32[]{:S(2)}) collective-permute-start(bf16[1,128,1024]{2,1,0:T(8,128)(2,1)S(1)} %get-tuple-element.176), channel_id=1, source_target_pairs={{0,8},{4,12},{8,0},{12,4},{16,24},{20,28},{24,16},{28,20},{1,9},{5... | collective-permute-start | bytes 786440 | tf_op jit(solution)/shard_map/ppermute | solution.py:26
  270.0 22.1 %collective-permute-start.47 = (bf16[1,128,1024]{2,1,0:T(8,128)(2,1)S(1)}, bf16[1,128,1024]{2,1,0:T(8,128)(2,1)}, u32[]{:S(2)}, u32[]{:S(2)}) collective-permute-start(bf16[1,128,1024]{2,1,0:T(8,128)(2,1)S(1)} %get-tuple-element.174), channel_id=1, source_target_pairs={{0,16},{4,20},{8,24},{12,28},{16,0},{20,4},{24,8},{28,12},{1,17},{... | collective-permute-start | bytes 786440 | tf_op jit(solution)/shard_map/ppermute | solution.py:26
  270.6 10.7 %collective-permute-start.49 = (bf16[2,2,16,1024]{3,2,0,1:T(8,128)(2,1)S(1)}, bf16[2,2,16,1024]{3,2,0,1:T(8,128)(2,1)S(1)}, u32[]{:S(2)}, u32[]{:S(2)}) collective-permute-start(bf16[2,2,16,1024]{3,2,0,1:T(8,128)(2,1)S(1)} %fusion.14), channel_id=1, source_target_pairs={{0,4},{4,0},{8,12},{12,8},{16,20},{20,16},{24,28},{28,24},{1,5},{5... | collective-permute-start | bytes 393224 | tf_op jit(solution)/shard_map/ppermute | solution.py:26
  291.5 8.5 %collective-permute-start.43 = (bf16[184,1024]{1,0:T(8,128)(2,1)S(1)}, bf16[184,1024]{1,0:T(8,128)(2,1)S(1)}, u32[]{:S(2)}, u32[]{:S(2)}) collective-permute-start(bf16[184,1024]{1,0:T(8,128)(2,1)S(1)} %add_convert_fusion), channel_id=1, source_target_pairs={{0,16},{4,20},{8,24},{12,28},{16,0},{20,4},{24,8},{28,12},{1,17},{... | collective-permute-start | bytes 1130504 | tf_op jit(solution)/shard_map/ppermute | solution.py:26
  300.1 5.7 %collective-permute-start.45 = (f32[2,1024]{1,0:T(2,128)S(1)}, f32[2,1024]{1,0:T(2,128)S(1)}, u32[]{:S(2)}, u32[]{:S(2)}) collective-permute-start(f32[2,1024]{1,0:T(2,128)S(1)} %slice.189), channel_id=1, source_target_pairs={{0,2},{1,3},{2,0},{3,1},{4,6},{5,7},{6,4},{7,5},{8,10},{9,11},{10,... | collective-permute-start | bytes 24584 | tf_op jit(solution)/shard_map/ppermute | solution.py:26
  300.2 5.6 %collective-permute-start.46 = (f32[2,1024]{1,0:T(2,128)S(1)}, f32[2,1024]{1,0:T(2,128)S(1)}, u32[]{:S(2)}, u32[]{:S(2)}) collective-permute-start(f32[2,1024]{1,0:T(2,128)S(1)} %slice.189), channel_id=1, source_target_pairs={{0,3},{1,2},{2,1},{3,0},{4,7},{5,6},{6,5},{7,4},{8,11},{9,10},{10,... | collective-permute-start | bytes 24584 | tf_op jit(solution)/shard_map/ppermute | solution.py:26
  (82 other events, 1350.7 us)

commit v4 on v3

--- a/solution.py
+++ b/solution.py
@@ -910,7 +910,7 @@
     x_sum.send_second(branch[1].got, out_sum.h1, out_sum.h2, z_sum.h1, z_sum.h2)
     gain_rows = packed[proj_weight.shape[0] + 16 : proj_weight.shape[0] + 16 + model // inner]
     gain_grad = total_of(exchange_all(gain_rows, "fsdp")).reshape(-1) / gain
-    (out_grad,), (in_z_grad,), (in_x_grad,) = out_sum.finish(x_sum.rest()), z_sum.finish(x_sum.rest()), x_sum.finish()
+    (out_grad,), (in_z_grad,), (in_x_grad,) = out_sum.finish(x_sum.h1), z_sum.finish(x_sum.h1), x_sum.finish()
     outputs, input_grads = [], []
     for s in seqs:
         v = after(states_in[s], x_sum.rest()).astype(f32)

time: 307 us -> 305 us (level)
  waiting for transfers between devices: 77.9 us -> 74.6 us
    ppermute x52, waiting for transfers between devices: 77.9 us -> 74.6 us  [swap(): lax.ppermute(x, axis, [(i, i ^ bit) for i in range(lax.axis_size(axis))])]
    unnamed x157 -> x169, local copies, waits for them, and re-layouts: 15.1 us -> 16.1 us
  transfers between devices with their start and end apart: 52 -> 52, of which waited for: 18 -> 18; matrix products, arithmetic and copies ran while one was open for 10% -> 10% of each run, Pallas kernels for 34% -> 35%
where the time goes in v4:
time: 305 us; the launch traced here: 304 us
  Pallas kernels  109 us (36%)
  waiting for transfers between devices  74.6 us (24%)
  starting transfers between devices  72.1 us (24%)
  local copies, waits for them, and re-layouts  24.2 us (8%)
  other arithmetic  21.8 us (7%)
    ppermute x52, waiting for transfers between devices, swap(): lax.ppermute(x, axis, [(i, i ^ bit) for i in range(lax.axis_size(axis))])  74.6 us
    ppermute x52, starting transfers between devices, swap(): lax.ppermute(x, axis, [(i, i ^ bit) for i in range(lax.axis_size(axis))])  72.1 us
    pallas_call x2, Pallas kernels, recurrence(): pl.pallas_call(functools.partial(recurrence_kernel, state_dim, rank, len(...  56.4 us
    pallas_call x2, Pallas kernels, leave(): pl.pallas_call(functools.partial(leave_kernel, len(terms)), grid=(inner /...  16.1 us
    unnamed x169, local copies, waits for them, and re-layouts  16.1 us
    pallas_call x2, Pallas kernels, enter(): pl.pallas_call(functools.partial(enter_kernel, len(parts)), grid=(inner /...  14.8 us
    pallas_call x3, Pallas kernels, send_first(): pl.pallas_call(functools.partial(grad_keep_kernel, self.pairs, self.count...  10.8 us
    pallas_call x3, Pallas kernels, send_core(): pl.pallas_call(functools.partial(grad_send_kernel, self.pairs, self.count...  8.97 us
  transfers between devices with their start and end apart: 52, of which 18 were waited for; matrix products, arithmetic and copies ran while one was open for 10% of the time, Pallas kernels for 35%

profile of v4, /device:TPU:0, one launch (start us, length us, event | category | flops | bytes accessed | tf_op | source)
XLA Modules:
  0.0 303.8 jit_solution(8459143326855421219)
XLA Ops:
  1.8 3.1 %collective-permute-start = (bf16[64,2048]{1,0:T(8,128)(2,1)S(1)}, bf16[64,2048]{1,0:T(8,128)(2,1)S(1)}, u32[]{:S(2)}, u32[]{:S(2)}) collective-permute-start(bf16[64,2048]{1,0:T(8,128)(2,1)S(1)} %get-tuple-element.159.refs_0_), channel_id=1, source_target_pairs={{0,1},{1,0},{2,3},{3,2},{4,5},{5,4},{6,7},{7,6},{8,9},{9,8},{10,11... | collective-permute-start | bytes 786440 | tf_op jit(solution)/shard_map/ppermute | solution.py:26
  4.9 2.6 collective-permute-start.1
  8.4 1.8 slice_bitcast_fusion.2
  10.8 5.3 %collective-permute-done.refs_1_ = bf16[64,2048]{1,0:T(8,128)(2,1)S(1)} collective-permute-done((bf16[64,2048]{1,0:T(8,128)(2,1)S(1)}, bf16[64,2048]{1,0:T(8,128)(2,1)S(1)}, u32[]{:S(2)}, u32[]{:S(2)}) %collective-permute-start) | collective-permute-done | bytes 262176 | tf_op jit(solution)/shard_map/ppermute | solution.py:26
  16.0 3.8 %collective-permute-start.7 = (bf16[64,2048]{1,0:T(8,128)(2,1)S(1)}, bf16[64,2048]{1,0:T(8,128)(2,1)}, u32[]{:S(2)}, u32[]{:S(2)}) collective-permute-start(bf16[64,2048]{1,0:T(8,128)(2,1)S(1)} %get-tuple-element.102.refs_0_), channel_id=1, source_target_pairs={{0,2},{1,3},{2,0},{3,1},{4,6},{5,7},{6,4},{7,5},{8,10},{9,11},{10,... | collective-permute-start | bytes 786440 | tf_op jit(solution)/shard_map/ppermute | solution.py:26
  19.8 6.5 %collective-permute-done.1.refs_2_ = bf16[64,2048]{1,0:T(8,128)(2,1)S(1)} collective-permute-done((bf16[64,2048]{1,0:T(8,128)(2,1)S(1)}, bf16[64,2048]{1,0:T(8,128)(2,1)S(1)}, u32[]{:S(2)}, u32[]{:S(2)}) %collective-permute-start.1) | collective-permute-done | bytes 262176 | tf_op jit(solution)/shard_map/ppermute | solution.py:26
  27.7 7.4 %enter.2 = (bf16[256,2048]{1,0:T(8,128)(2,1)S(1)}, bf16[256,1024]{1,0:T(8,128)(2,1)S(1)}, f32[256,1024]{1,0:T(8,128)S(1)}, bf16[256,1024]{1,0:T(8,128)(2,1)S(1)}, bf16[160,256]{1,0:T(8,128)(2,1)S(1)}) custom-call(s32[1,4]{1,0:T(1,128)S(1)} %add_bitcast_fusion.7.offs_ref, bf16[64,2048]{1,0:T(8,128)(2,1)} %copy-done.37, bf16[64,2048]{1,0:T(8,128)(2,1)} %copy-done.72, ...), custom_call_target="tpu_custom_call" | custom-call | flops 8099999744 | bytes 1 | tf_op jit(solution)/shard_map/enter/pallas_call | solution.py:186
  36.1 11.1 %collective-permute-start.9 = (bf16[160,256]{1,0:T(8,128)(2,1)S(1)}, bf16[160,256]{1,0:T(8,128)(2,1)S(1)}, u32[]{:S(2)}, u32[]{:S(2)}) collective-permute-start(bf16[160,256]{1,0:T(8,128)(2,1)S(1)} %get-tuple-element.104), channel_id=1, source_target_pairs={{0,1},{1,0},{2,3},{3,2},{4,5},{5,4},{6,7},{7,6},{8,9},{9,8},{10,11... | collective-permute-start | bytes 245768 | tf_op jit(solution)/shard_map/ppermute | solution.py:26
  47.6 3.0 collective-permute-start.5
  51.1 2.6 collective-permute-start.10
  53.8 9.4 %collective-permute-done.4.refs_1_ = bf16[64,2048]{1,0:T(8,128)(2,1)S(1)} collective-permute-done((bf16[64,2048]{1,0:T(8,128)(2,1)S(1)}, bf16[64,2048]{1,0:T(8,128)(2,1)S(1)}, u32[]{:S(2)}, u32[]{:S(2)}) %collective-permute-start.4) | collective-permute-done | bytes 262176 | tf_op jit(solution)/shard_map/ppermute | solution.py:26
  63.2 3.2 %collective-permute-start.15 = (bf16[64,2048]{1,0:T(8,128)(2,1)}, bf16[64,2048]{1,0:T(8,128)(2,1)S(1)}, u32[]{:S(2)}, u32[]{:S(2)}) collective-permute-start(bf16[64,2048]{1,0:T(8,128)(2,1)} %get-tuple-element.117.refs_0_), channel_id=1, source_target_pairs={{0,2},{1,3},{2,0},{3,1},{4,6},{5,7},{6,4},{7,5},{8,10},{9,11},{10,... | collective-permute-start | bytes 786440 | tf_op jit(solution)/shard_map/ppermute | solution.py:26
  66.4 1.6 collective-permute-done.10.refs_5_
  68.0 3.0 collective-permute-done.8.refs_3_
  73.0 27.7 %recurrence.2 = (bf16[256,1024]{1,0:T(8,128)(2,1)S(1)}, bf16[256,1024]{1,0:T(8,128)(2,1)S(1)}, f32[256,1024]{1,0:T(8,128)S(1)}, bf16[160,256]{1,0:T(8,128)(2,1)S...) custom-call(f32[1,32]{1,0:T(1,128)S(1)} %get-tuple-element.249.keep_, ...), custom_call_target="tpu_custom_call" | custom-call | flops 27000000512 | bytes 1 | tf_op jit(solution)/shard_map/recurrence/pallas_call | solution.py:533
  103.5 7.4 %enter.3 = (bf16[256,2048]{1,0:T(8,128)(2,1)S(1)}, bf16[256,1024]{1,0:T(8,128)(2,1)S(1)}, f32[256,1024]{1,0:T(8,128)S(1)}, bf16[256,1024]{1,0:T(8,128)(2,1)S(1)}, bf16[160,256]{1,0:T(8,128)(2,1)S(1)}) custom-call(s32[1,4]{1,0:T(1,128)S(1)} %add_bitcast_fusion.7.offs_ref, bf16[64,2048]{1,0:T(8,128)(2,1)} %copy-done.39, bf16[64,2048]{1,0:T(8,128)(2,1)} %copy-done.75, ...), custom_call_target="tpu_custom_call" | custom-call | flops 8099999744 | bytes 1 | tf_op jit(solution)/shard_map/enter/pallas_call | solution.py:186
  112.2 3.4 %collective-permute-start.12 = (bf16[160,256]{1,0:T(8,128)(2,1)S(1)}, bf16[160,256]{1,0:T(8,128)(2,1)S(1)}, u32[]{:S(2)}, u32[]{:S(2)}) collective-permute-start(bf16[160,256]{1,0:T(8,128)(2,1)S(1)} %add_convert_fusion.8.refs_0_), channel_id=1, source_target_pairs={{0,2},{1,3},{2,0},{3,1},{4,6},{5,7},{6,4},{7,5},{8,10},{9,11},{10,... | collective-permute-start | bytes 245768 | tf_op jit(solution)/shard_map/ppermute | solution.py:26
  115.9 3.9 %collective-permute-start.17 = (bf16[160,256]{1,0:T(8,128)(2,1)S(1)}, bf16[160,256]{1,0:T(8,128)(2,1)S(1)}, u32[]{:S(2)}, u32[]{:S(2)}) collective-permute-start(bf16[160,256]{1,0:T(8,128)(2,1)S(1)} %add_convert_fusion.7.refs_4_), channel_id=1, source_target_pairs={{0,2},{1,3},{2,0},{3,1},{4,6},{5,7},{6,4},{7,5},{8,10},{9,11},{10,... | collective-permute-start | bytes 245768 | tf_op jit(solution)/shard_map/ppermute | solution.py:26
  120.5 7.7 %leave.2 = (bf16[256,1024]{1,0:T(8,128)(2,1)S(1)}, f32[8,1024]{1,0:T(8,128)S(1)}, f32[160,1024]{1,0:T(8,128)S(1)}, f32[1,2048]{1,0:T(1,128)S(1)}, bf16[2,64,2048...) custom-call(s32[1,4]{1,0:T(1,128)S(1)} %add_bitcast_fusion.7.offs_ref, bf16[160,256]{1,0:T(8,128)(2,1)} %copy-done.60, ...), custom_call_target="tpu_custom_call" | custom-call | flops 8999999488 | bytes 1 | tf_op jit(solution)/shard_map/leave/pallas_call | solution.py:278
  128.2 3.0 %collective-permute-start.22 = (bf16[2,64,2048]{2,1,0:T(8,128)(2,1)S(1)}, bf16[2,64,2048]{2,1,0:T(8,128)(2,1)S(1)}, u32[]{:S(2)}, u32[]{:S(2)}) collective-permute-start(bf16[2,64,2048]{2,1,0:T(8,128)(2,1)S(1)} %get-tuple-element.128), channel_id=1, source_target_pairs={{0,1},{1,0},{2,3},{3,2},{4,5},{5,4},{6,7},{7,6},{8,9},{9,8},{10,11... | collective-permute-start | bytes 1572872 | tf_op jit(solution)/shard_map/ppermute | solution.py:26
  132.2 28.7 %recurrence.3 = (bf16[256,1024]{1,0:T(8,128)(2,1)S(1)}, bf16[256,1024]{1,0:T(8,128)(2,1)S(1)}, f32[256,1024]{1,0:T(8,128)S(1)}, bf16[160,256]{1,0:T(8,128)(2,1)S...) custom-call(f32[1,32]{1,0:T(1,128)S(1)} %get-tuple-element.250.keep_, ...), custom_call_target="tpu_custom_call" | custom-call | flops 27000000512 | bytes 1 | tf_op jit(solution)/shard_map/recurrence/pallas_call | solution.py:533
  161.0 2.6 grad_send.4
  164.4 2.6 grad_send.3
  168.7 3.3 %collective-permute-done.18 = bf16[160,256]{1,0:T(8,128)(2,1)S(1)} collective-permute-done((bf16[160,256]{1,0:T(8,128)(2,1)S(1)}, bf16[160,256]{1,0:T(8,128)(2,1)S(1)}, u32[]{:S(2)}, u32[]{:S(2)}) %collective-permute-start.18) | collective-permute-done | bytes 81952 | tf_op jit(solution)/shard_map/ppermute | solution.py:26
  172.1 2.9 collective-permute-start.19
  175.0 3.0 grad_keep.4
  178.0 1.7 collective-permute-start.27
  181.1 3.0 grad_keep.3
  185.9 8.5 %leave.3 = (bf16[256,1024]{1,0:T(8,128)(2,1)S(1)}, f32[8,1024]{1,0:T(8,128)S(1)}, f32[160,1024]{1,0:T(8,128)S(1)}, f32[1,2048]{1,0:T(1,128)S(1)}, bf16[2,64,2048...) custom-call(s32[1,4]{1,0:T(1,128)S(1)} %copy-done.13, bf16[160,256]{1,0:T(8,128)(2,1)} %copy-done.57, ...), custom_call_target="tpu_custom_call" | custom-call | flops 8999999488 | bytes 1 | tf_op jit(solution)/shard_map/leave/pallas_call | solution.py:278
  194.3 7.5 %collective-permute-done.25.g1_ref = bf16[1,2,128,1024]{3,2,1,0:T(8,128)(2,1)S(1)} collective-permute-done((bf16[1,2,128,1024]{3,2,1,0:T(8,128)(2,1)S(1)}, bf16[1,2,128,1024]{3,2,1,0:T(8,128)(2,1)S(1)}, u32[]{:S(2)}, u32[]{:S(2)}) %collective-permute-start.25) | collective-permute-done | bytes 524320 | tf_op jit(solution)/shard_map/ppermute | solution.py:26
  205.1 3.7 %grad_send.5 = bf16[1,4,256,1024]{3,2,1,0:T(8,128)(2,1)} custom-call(s32[3]{0:T(128)S(1)} %pad_add_fusion.place_ref, bf16[256,2048]{1,0:T(8,128)(2,1)S(1)} %copy-done.23, bf16[256,2048]{1,0:T(8,128)(2,1)S(1)} %get-tuple-element.109.refs_1_.refs_12_, bf16[256,1024]{1,0:T(8,128)(2,1)S(1)} %get-tuple-element.116.refs_2_, ...), custom_call_target="tpu_custom_call" | custom-call | flops 4950000128 | bytes 1 | tf_op jit(solution)/shard_map/grad_send/pallas_call | solution.py:658
  211.0 2.1 add.261
  213.1 10.4 %collective-permute-done.30 = bf16[2,64,2048]{2,1,0:T(8,128)(2,1)} collective-permute-done((bf16[2,64,2048]{2,1,0:T(8,128)(2,1)}, bf16[2,64,2048]{2,1,0:T(8,128)(2,1)}, u32[]{:S(2)}, u32[]{:S(2)}) %collective-permute-start.30) | collective-permute-done | bytes 524320 | tf_op jit(solution)/shard_map/ppermute | solution.py:26
  223.5 1.8 add_convert_fusion.4
  228.1 1.9 concatenate.12
  230.0 1.4 collective-permute-start.32
  232.1 8.0 %collective-permute-done.31 = bf16[1,64,2048]{2,1,0:T(8,128)(2,1)} collective-permute-done((bf16[1,64,2048]{2,1,0:T(8,128)(2,1)}, bf16[1,64,2048]{2,1,0:T(8,128)(2,1)}, u32[]{:S(2)}, u32[]{:S(2)}) %collective-permute-start.31) | collective-permute-done | bytes 262176 | tf_op jit(solution)/shard_map/ppermute | solution.py:26
  246.7 4.8 %grad_keep.5 = (bf16[1,2,128,1024]{3,2,1,0:T(8,128)(2,1)S(1)}, bf16[1,2,128,1024]{3,2,1,0:T(8,128)(2,1)S(1)}, bf16[1,2,128,1024]{3,2,1,0:T(8,128)(2,1)S(1)}, bf16[1,2,128,1024]{3,2,1,0:T(8,128)(2,1)S(1)}) custom-call(s32[3]{0:T(128)S(1)} %copy-done.15, bf16[256,2048]{1,0:T(8,128)(2,1)S(1)} %copy-done.24, bf16[256,2048]{1,0:T(8,128)(2,1)S(1)} %copy-done.26, ...), custom_call_target="tpu_custom_call" | custom-call | flops 5849999872 | bytes 1 | tf_op jit(solution)/shard_map/grad_keep/pallas_call | solution.py:684
  255.5 3.0 collective-permute-start.40
  259.0 8.3 %collective-permute-done.36.g1_ref = bf16[1,2,128,1024]{3,2,1,0:T(8,128)(2,1)S(1)} collective-permute-done((bf16[1,2,128,1024]{3,2,1,0:T(8,128)(2,1)S(1)}, bf16[1,2,128,1024]{3,2,1,0:T(8,128)(2,1)S(1)}, u32[]{:S(2)}, u32[]{:S(2)}) %collective-permute-start.36) | collective-permute-done | bytes 524320 | tf_op jit(solution)/shard_map/ppermute | solution.py:26
  270.4 3.9 %collective-permute-done.40 = bf16[1,64,2048]{2,1,0:T(8,128)(2,1)S(1)} collective-permute-done((bf16[1,64,2048]{2,1,0:T(8,128)(2,1)S(1)}, bf16[1,64,2048]{2,1,0:T(8,128)(2,1)S(1)}, u32[]{:S(2)}, u32[]{:S(2)}) %collective-permute-start.40) | collective-permute-done | bytes 262176 | tf_op jit(solution)/shard_map/ppermute | solution.py:26
  274.3 2.0 fusion.1
  276.4 1.5 fusion.4
  277.9 1.4 collective-permute-start.50
  280.4 1.8 collective-permute-done.50
  283.6 2.7 collective-permute-done.51
  288.7 2.5 copy.42
  297.6 1.9 collective-permute-start.46
  (304 shorter events, 57.7 us)
Async XLA Ops:
  1.8 14.2 %collective-permute-start = (bf16[64,2048]{1,0:T(8,128)(2,1)S(1)}, bf16[64,2048]{1,0:T(8,128)(2,1)S(1)}, u32[]{:S(2)}, u32[]{:S(2)}) collective-permute-start(bf16[64,2048]{1,0:T(8,128)(2,1)S(1)} %get-tuple-element.159.refs_0_), channel_id=1, source_target_pairs={{0,1},{1,0},{2,3},{3,2},{4,5},{5,4},{6,7},{7,6},{8,9},{9,8},{10,11... | collective-permute-start | bytes 786440 | tf_op jit(solution)/shard_map/ppermute | solution.py:26
  4.9 21.4 %collective-permute-start.1 = (bf16[64,2048]{1,0:T(8,128)(2,1)S(1)}, bf16[64,2048]{1,0:T(8,128)(2,1)S(1)}, u32[]{:S(2)}, u32[]{:S(2)}) collective-permute-start(bf16[64,2048]{1,0:T(8,128)(2,1)S(1)} %get-tuple-element.159.refs_0_), channel_id=1, source_target_pairs={{0,2},{1,3},{2,0},{3,1},{4,6},{5,7},{6,4},{7,5},{8,10},{9,11},{10,... | collective-permute-start | bytes 786440 | tf_op jit(solution)/shard_map/ppermute | solution.py:26
  7.5 18.8 %collective-permute-start.2 = (bf16[64,2048]{1,0:T(8,128)(2,1)S(1)}, bf16[64,2048]{1,0:T(8,128)(2,1)S(1)}, u32[]{:S(2)}, u32[]{:S(2)}) collective-permute-start(bf16[64,2048]{1,0:T(8,128)(2,1)S(1)} %get-tuple-element.159.refs_0_), channel_id=1, source_target_pairs={{0,3},{1,2},{2,1},{3,0},{4,7},{5,6},{6,5},{7,4},{8,11},{9,10},{10,... | collective-permute-start | bytes 786440 | tf_op jit(solution)/shard_map/ppermute | solution.py:26
  16.0 31.4 %collective-permute-start.3 = (bf16[64,2048]{1,0:T(8,128)(2,1)S(1)}, bf16[64,2048]{1,0:T(8,128)(2,1)}, u32[]{:S(2)}, u32[]{:S(2)}) collective-permute-start(bf16[64,2048]{1,0:T(8,128)(2,1)S(1)} %get-tuple-element.102.refs_0_), channel_id=1, source_target_pairs={{0,1},{1,0},{2,3},{3,2},{4,5},{5,4},{6,7},{7,6},{8,9},{9,8},{10,11... | collective-permute-start | bytes 786440 | tf_op jit(solution)/shard_map/ppermute | solution.py:26
  16.0 34.5 %collective-permute-start.7 = (bf16[64,2048]{1,0:T(8,128)(2,1)S(1)}, bf16[64,2048]{1,0:T(8,128)(2,1)}, u32[]{:S(2)}, u32[]{:S(2)}) collective-permute-start(bf16[64,2048]{1,0:T(8,128)(2,1)S(1)} %get-tuple-element.102.refs_0_), channel_id=1, source_target_pairs={{0,2},{1,3},{2,0},{3,1},{4,6},{5,7},{6,4},{7,5},{8,10},{9,11},{10,... | collective-permute-start | bytes 786440 | tf_op jit(solution)/shard_map/ppermute | solution.py:26
  36.1 15.0 %collective-permute-start.9 = (bf16[160,256]{1,0:T(8,128)(2,1)S(1)}, bf16[160,256]{1,0:T(8,128)(2,1)S(1)}, u32[]{:S(2)}, u32[]{:S(2)}) collective-permute-start(bf16[160,256]{1,0:T(8,128)(2,1)S(1)} %get-tuple-element.104), channel_id=1, source_target_pairs={{0,1},{1,0},{2,3},{3,2},{4,5},{5,4},{6,7},{7,6},{8,9},{9,8},{10,11... | collective-permute-start | bytes 245768 | tf_op jit(solution)/shard_map/ppermute | solution.py:26
  47.4 15.8 %collective-permute-start.4 = (bf16[64,2048]{1,0:T(8,128)(2,1)S(1)}, bf16[64,2048]{1,0:T(8,128)(2,1)S(1)}, u32[]{:S(2)}, u32[]{:S(2)}) collective-permute-start(bf16[64,2048]{1,0:T(8,128)(2,1)S(1)} %get-tuple-element.160.refs_0_), channel_id=1, source_target_pairs={{0,1},{1,0},{2,3},{3,2},{4,5},{5,4},{6,7},{7,6},{8,9},{9,8},{10,11... | collective-permute-start | bytes 786440 | tf_op jit(solution)/shard_map/ppermute | solution.py:26
  47.6 18.9 %collective-permute-start.5 = (bf16[64,2048]{1,0:T(8,128)(2,1)S(1)}, bf16[64,2048]{1,0:T(8,128)(2,1)S(1)}, u32[]{:S(2)}, u32[]{:S(2)}) collective-permute-start(bf16[64,2048]{1,0:T(8,128)(2,1)S(1)} %get-tuple-element.160.refs_0_), channel_id=1, source_target_pairs={{0,2},{1,3},{2,0},{3,1},{4,6},{5,7},{6,4},{7,5},{8,10},{9,11},{10,... | collective-permute-start | bytes 786440 | tf_op jit(solution)/shard_map/ppermute | solution.py:26
  50.5 20.5 %collective-permute-start.8 = (bf16[64,2048]{1,0:T(8,128)(2,1)}, bf16[64,2048]{1,0:T(8,128)(2,1)S(1)}, u32[]{:S(2)}, u32[]{:S(2)}) collective-permute-start(bf16[64,2048]{1,0:T(8,128)(2,1)} %collective-permute-done.7.refs_2_), channel_id=1, source_target_pairs={{0,1},{1,0},{2,3},{3,2},{4,5},{5,4},{6,7},{7,6},{8,9},{9,8},{10,11... | collective-permute-start | bytes 786440 | tf_op jit(solution)/shard_map/ppermute | solution.py:26
  51.1 16.9 %collective-permute-start.10 = (bf16[160,256]{1,0:T(8,128)(2,1)S(1)}, bf16[160,256]{1,0:T(8,128)(2,1)S(1)}, u32[]{:S(2)}, u32[]{:S(2)}) collective-permute-start(bf16[160,256]{1,0:T(8,128)(2,1)S(1)} %add_convert_fusion.9.refs_4_), channel_id=1, source_target_pairs={{0,2},{1,3},{2,0},{3,1},{4,6},{5,7},{6,4},{7,5},{8,10},{9,11},{10,... | collective-permute-start | bytes 245768 | tf_op jit(solution)/shard_map/ppermute | solution.py:26
  63.2 68.2 %collective-permute-start.14 = (bf16[64,2048]{1,0:T(8,128)(2,1)}, bf16[64,2048]{1,0:T(8,128)(2,1)S(1)}, u32[]{:S(2)}, u32[]{:S(2)}) collective-permute-start(bf16[64,2048]{1,0:T(8,128)(2,1)} %get-tuple-element.117.refs_0_), channel_id=1, source_target_pairs={{0,1},{1,0},{2,3},{3,2},{4,5},{5,4},{6,7},{7,6},{8,9},{9,8},{10,11... | collective-permute-start | bytes 786440 | tf_op jit(solution)/shard_map/ppermute | solution.py:26
  63.2 52.5 %collective-permute-start.15 = (bf16[64,2048]{1,0:T(8,128)(2,1)}, bf16[64,2048]{1,0:T(8,128)(2,1)S(1)}, u32[]{:S(2)}, u32[]{:S(2)}) collective-permute-start(bf16[64,2048]{1,0:T(8,128)(2,1)} %get-tuple-element.117.refs_0_), channel_id=1, source_target_pairs={{0,2},{1,3},{2,0},{3,1},{4,6},{5,7},{6,4},{7,5},{8,10},{9,11},{10,... | collective-permute-start | bytes 786440 | tf_op jit(solution)/shard_map/ppermute | solution.py:26
  66.4 36.4 %collective-permute-start.6 = (bf16[64,2048]{1,0:T(8,128)(2,1)S(1)}, bf16[64,2048]{1,0:T(8,128)(2,1)S(1)}, u32[]{:S(2)}, u32[]{:S(2)}) collective-permute-start(bf16[64,2048]{1,0:T(8,128)(2,1)S(1)} %collective-permute-done.5.refs_2_), channel_id=1, source_target_pairs={{0,1},{1,0},{2,3},{3,2},{4,5},{5,4},{6,7},{7,6},{8,9},{9,8},{10,11... | collective-permute-start | bytes 786440 | tf_op jit(solution)/shard_map/ppermute | solution.py:26
  100.7 11.5 %collective-permute-start.11 = (bf16[160,256]{1,0:T(8,128)(2,1)S(1)}, bf16[160,256]{1,0:T(8,128)(2,1)S(1)}, u32[]{:S(2)}, u32[]{:S(2)}) collective-permute-start(bf16[160,256]{1,0:T(8,128)(2,1)S(1)} %get-tuple-element.110), channel_id=1, source_target_pairs={{0,1},{1,0},{2,3},{3,2},{4,5},{5,4},{6,7},{7,6},{8,9},{9,8},{10,11... | collective-permute-start | bytes 245768 | tf_op jit(solution)/shard_map/ppermute | solution.py:26
  102.0 29.2 %collective-permute-start.20 = (bf16[2,64,2048]{2,1,0:T(8,128)(2,1)S(1)}, bf16[2,64,2048]{2,1,0:T(8,128)(2,1)S(1)}, u32[]{:S(2)}, u32[]{:S(2)}) collective-permute-start(bf16[2,64,2048]{2,1,0:T(8,128)(2,1)S(1)} %get-tuple-element.127), channel_id=1, source_target_pairs={{0,1},{1,0},{2,3},{3,2},{4,5},{5,4},{6,7},{7,6},{8,9},{9,8},{10,11... | collective-permute-start | bytes 1572872 | tf_op jit(solution)/shard_map/ppermute | solution.py:26
  110.9 5.0 %collective-permute-start.13 = (bf16[160,256]{1,0:T(8,128)(2,1)S(1)}, bf16[160,256]{1,0:T(8,128)(2,1)S(1)}, u32[]{:S(2)}, u32[]{:S(2)}) collective-permute-start(bf16[160,256]{1,0:T(8,128)(2,1)S(1)} %get-tuple-element.112), channel_id=1, source_target_pairs={{0,1},{1,0},{2,3},{3,2},{4,5},{5,4},{6,7},{7,6},{8,9},{9,8},{10,11... | collective-permute-start | bytes 245768 | tf_op jit(solution)/shard_map/ppermute | solution.py:26
  112.2 7.6 %collective-permute-start.12 = (bf16[160,256]{1,0:T(8,128)(2,1)S(1)}, bf16[160,256]{1,0:T(8,128)(2,1)S(1)}, u32[]{:S(2)}, u32[]{:S(2)}) collective-permute-start(bf16[160,256]{1,0:T(8,128)(2,1)S(1)} %add_convert_fusion.8.refs_0_), channel_id=1, source_target_pairs={{0,2},{1,3},{2,0},{3,1},{4,6},{5,7},{6,4},{7,5},{8,10},{9,11},{10,... | collective-permute-start | bytes 245768 | tf_op jit(solution)/shard_map/ppermute | solution.py:26
  115.7 15.7 %collective-permute-start.16 = (bf16[64,2048]{1,0:T(8,128)(2,1)S(1)}, bf16[64,2048]{1,0:T(8,128)(2,1)S(1)}, u32[]{:S(2)}, u32[]{:S(2)}) collective-permute-start(bf16[64,2048]{1,0:T(8,128)(2,1)S(1)} %collective-permute-done.15.refs_2_), channel_id=1, source_target_pairs={{0,1},{1,0},{2,3},{3,2},{4,5},{5,4},{6,7},{7,6},{8,9},{9,8},{10,11... | collective-permute-start | bytes 786440 | tf_op jit(solution)/shard_map/ppermute | solution.py:26
  115.9 15.5 %collective-permute-start.17 = (bf16[160,256]{1,0:T(8,128)(2,1)S(1)}, bf16[160,256]{1,0:T(8,128)(2,1)S(1)}, u32[]{:S(2)}, u32[]{:S(2)}) collective-permute-start(bf16[160,256]{1,0:T(8,128)(2,1)S(1)} %add_convert_fusion.7.refs_4_), channel_id=1, source_target_pairs={{0,2},{1,3},{2,0},{3,1},{4,6},{5,7},{6,4},{7,5},{8,10},{9,11},{10,... | collective-permute-start | bytes 245768 | tf_op jit(solution)/shard_map/ppermute | solution.py:26
  128.2 35.6 %collective-permute-start.22 = (bf16[2,64,2048]{2,1,0:T(8,128)(2,1)S(1)}, bf16[2,64,2048]{2,1,0:T(8,128)(2,1)S(1)}, u32[]{:S(2)}, u32[]{:S(2)}) collective-permute-start(bf16[2,64,2048]{2,1,0:T(8,128)(2,1)S(1)} %get-tuple-element.128), channel_id=1, source_target_pairs={{0,1},{1,0},{2,3},{3,2},{4,5},{5,4},{6,7},{7,6},{8,9},{9,8},{10,11... | collective-permute-start | bytes 1572872 | tf_op jit(solution)/shard_map/ppermute | solution.py:26
  131.3 32.4 %collective-permute-start.21 = (bf16[1,64,2048]{2,1,0:T(8,128)(2,1)S(1)}, bf16[1,64,2048]{2,1,0:T(8,128)(2,1)S(1)}, u32[]{:S(2)}, u32[]{:S(2)}) collective-permute-start(bf16[1,64,2048]{2,1,0:T(8,128)(2,1)S(1)} %add_convert_fusion.5), channel_id=1, source_target_pairs={{0,2},{1,3},{2,0},{3,1},{4,6},{5,7},{6,4},{7,5},{8,10},{9,11},{10,... | collective-permute-start | bytes 786440 | tf_op jit(solution)/shard_map/ppermute | solution.py:26
  163.6 11.4 %collective-permute-start.24 = (bf16[1,4,256,1024]{3,2,1,0:T(8,128)(2,1)S(1)}, bf16[1,4,256,1024]{3,2,1,0:T(8,128)(2,1)S(1)}, u32[]{:S(2)}, u32[]{:S(2)}) collective-permute-start(bf16[1,4,256,1024]{3,2,1,0:T(8,128)(2,1)S(1)} %grad_send.4), channel_id=1, source_target_pairs={{0,4},{4,0},{8,12},{12,8},{16,20},{20,16},{24,28},{28,24},{1,5},{5... | collective-permute-start | bytes 6291464 | tf_op jit(solution)/shard_map/ppermute | solution.py:26
  167.0 14.0 %collective-permute-start.23 = (bf16[1,4,256,1024]{3,2,1,0:T(8,128)(2,1)S(1)}, bf16[1,4,256,1024]{3,2,1,0:T(8,128)(2,1)S(1)}, u32[]{:S(2)}, u32[]{:S(2)}) collective-permute-start(bf16[1,4,256,1024]{3,2,1,0:T(8,128)(2,1)S(1)} %grad_send.3), channel_id=1, source_target_pairs={{0,4},{4,0},{8,12},{12,8},{16,20},{20,16},{24,28},{28,24},{1,5},{5... | collective-permute-start | bytes 6291464 | tf_op jit(solution)/shard_map/ppermute | solution.py:26
  167.6 4.4 %collective-permute-start.18 = (bf16[160,256]{1,0:T(8,128)(2,1)S(1)}, bf16[160,256]{1,0:T(8,128)(2,1)S(1)}, u32[]{:S(2)}, u32[]{:S(2)}) collective-permute-start(bf16[160,256]{1,0:T(8,128)(2,1)S(1)} %get-tuple-element.121), channel_id=1, source_target_pairs={{0,1},{1,0},{2,3},{3,2},{4,5},{5,4},{6,7},{7,6},{8,9},{9,8},{10,11... | collective-permute-start | bytes 245768 | tf_op jit(solution)/shard_map/ppermute | solution.py:26
  172.1 13.2 %collective-permute-start.19 = (bf16[160,256]{1,0:T(8,128)(2,1)S(1)}, bf16[160,256]{1,0:T(8,128)(2,1)S(1)}, u32[]{:S(2)}, u32[]{:S(2)}) collective-permute-start(bf16[160,256]{1,0:T(8,128)(2,1)S(1)} %add_convert_fusion.6.refs_0_), channel_id=1, source_target_pairs={{0,2},{1,3},{2,0},{3,1},{4,6},{5,7},{6,4},{7,5},{8,10},{9,11},{10,... | collective-permute-start | bytes 245768 | tf_op jit(solution)/shard_map/ppermute | solution.py:26
  178.0 26.0 %collective-permute-start.27 = (bf16[1,2,128,1024]{3,2,1,0:T(8,128)(2,1)S(1)}, bf16[1,2,128,1024]{3,2,1,0:T(8,128)(2,1)S(1)}, u32[]{:S(2)}, u32[]{:S(2)}) collective-permute-start(bf16[1,2,128,1024]{3,2,1,0:T(8,128)(2,1)S(1)} %get-tuple-element.142), channel_id=1, source_target_pairs={{0,8},{4,12},{8,0},{12,4},{16,24},{20,28},{24,16},{28,20},{1,9},{5... | collective-permute-start | bytes 1572872 | tf_op jit(solution)/shard_map/ppermute | solution.py:26
  179.8 24.3 %collective-permute-start.28 = (bf16[1,2,128,1024]{3,2,1,0:T(8,128)(2,1)S(1)}, bf16[1,2,128,1024]{3,2,1,0:T(8,128)(2,1)S(1)}, u32[]{:S(2)}, u32[]{:S(2)}) collective-permute-start(bf16[1,2,128,1024]{3,2,1,0:T(8,128)(2,1)S(1)} %get-tuple-element.144), channel_id=1, source_target_pairs={{0,16},{4,20},{8,24},{12,28},{16,0},{20,4},{24,8},{28,12},{1,17},{... | collective-permute-start | bytes 1572872 | tf_op jit(solution)/shard_map/ppermute | solution.py:26
  184.1 17.7 %collective-permute-start.25 = (bf16[1,2,128,1024]{3,2,1,0:T(8,128)(2,1)S(1)}, bf16[1,2,128,1024]{3,2,1,0:T(8,128)(2,1)S(1)}, u32[]{:S(2)}, u32[]{:S(2)}) collective-permute-start(bf16[1,2,128,1024]{3,2,1,0:T(8,128)(2,1)S(1)} %get-tuple-element.137), channel_id=1, source_target_pairs={{0,8},{4,12},{8,0},{12,4},{16,24},{20,28},{24,16},{28,20},{1,9},{5... | collective-permute-start | bytes 1572872 | tf_op jit(solution)/shard_map/ppermute | solution.py:26
  184.9 18.3 %collective-permute-start.26 = (bf16[1,2,128,1024]{3,2,1,0:T(8,128)(2,1)S(1)}, bf16[1,2,128,1024]{3,2,1,0:T(8,128)(2,1)S(1)}, u32[]{:S(2)}, u32[]{:S(2)}) collective-permute-start(bf16[1,2,128,1024]{3,2,1,0:T(8,128)(2,1)S(1)} %get-tuple-element.139), channel_id=1, source_target_pairs={{0,16},{4,20},{8,24},{12,28},{16,0},{20,4},{24,8},{28,12},{1,17},{... | collective-permute-start | bytes 1572872 | tf_op jit(solution)/shard_map/ppermute | solution.py:26
  208.8 32.7 %collective-permute-start.29 = (bf16[1,4,256,1024]{3,2,1,0:T(8,128)(2,1)}, bf16[1,4,256,1024]{3,2,1,0:T(8,128)(2,1)}, u32[]{:S(2)}, u32[]{:S(2)}) collective-permute-start(bf16[1,4,256,1024]{3,2,1,0:T(8,128)(2,1)} %grad_send.5), channel_id=1, source_target_pairs={{0,4},{4,0},{8,12},{12,8},{16,20},{20,16},{24,28},{28,24},{1,5},{5... | collective-permute-start | bytes 6291464 | tf_op jit(solution)/shard_map/ppermute | solution.py:26
  208.9 14.7 %collective-permute-start.30 = (bf16[2,64,2048]{2,1,0:T(8,128)(2,1)}, bf16[2,64,2048]{2,1,0:T(8,128)(2,1)}, u32[]{:S(2)}, u32[]{:S(2)}) collective-permute-start(bf16[2,64,2048]{2,1,0:T(8,128)(2,1)} %get-tuple-element.149), channel_id=1, source_target_pairs={{0,1},{1,0},{2,3},{3,2},{4,5},{5,4},{6,7},{7,6},{8,9},{9,8},{10,11... | collective-permute-start | bytes 1572872 | tf_op jit(solution)/shard_map/ppermute | solution.py:26
  225.3 14.8 %collective-permute-start.31 = (bf16[1,64,2048]{2,1,0:T(8,128)(2,1)}, bf16[1,64,2048]{2,1,0:T(8,128)(2,1)}, u32[]{:S(2)}, u32[]{:S(2)}) collective-permute-start(bf16[1,64,2048]{2,1,0:T(8,128)(2,1)} %add_convert_fusion.4), channel_id=1, source_target_pairs={{0,2},{1,3},{2,0},{3,1},{4,6},{5,7},{6,4},{7,5},{8,10},{9,11},{10,... | collective-permute-start | bytes 786440 | tf_op jit(solution)/shard_map/ppermute | solution.py:26
  226.4 28.1 %collective-permute-start.39 = (bf16[2,64,2048]{2,1,0:T(8,128)(2,1)}, bf16[2,64,2048]{2,1,0:T(8,128)(2,1)}, u32[]{:S(2)}, u32[]{:S(2)}) collective-permute-start(bf16[2,64,2048]{2,1,0:T(8,128)(2,1)} %get-tuple-element.163), channel_id=1, source_target_pairs={{0,1},{1,0},{2,3},{3,2},{4,5},{5,4},{6,7},{7,6},{8,9},{9,8},{10,11... | collective-permute-start | bytes 1572872 | tf_op jit(solution)/shard_map/ppermute | solution.py:26
  230.0 21.5 %collective-permute-start.32 = (bf16[1,128,1024]{2,1,0:T(8,128)(2,1)}, bf16[1,128,1024]{2,1,0:T(8,128)(2,1)S(1)}, u32[]{:S(2)}, u32[]{:S(2)}) collective-permute-start(bf16[1,128,1024]{2,1,0:T(8,128)(2,1)} %copy-done.17), channel_id=1, source_target_pairs={{0,16},{4,20},{8,24},{12,28},{16,0},{20,4},{24,8},{28,12},{1,17},{... | collective-permute-start | bytes 786440 | tf_op jit(solution)/shard_map/ppermute | solution.py:26
  231.4 20.2 %collective-permute-start.33 = (bf16[1,128,1024]{2,1,0:T(8,128)(2,1)}, bf16[1,128,1024]{2,1,0:T(8,128)(2,1)S(1)}, u32[]{:S(2)}, u32[]{:S(2)}) collective-permute-start(bf16[1,128,1024]{2,1,0:T(8,128)(2,1)} %copy-done.16), channel_id=1, source_target_pairs={{0,8},{4,12},{8,0},{12,4},{16,24},{20,28},{24,16},{28,20},{1,9},{5... | collective-permute-start | bytes 786440 | tf_op jit(solution)/shard_map/ppermute | solution.py:26
  240.1 11.5 %collective-permute-start.34 = (bf16[1,128,1024]{2,1,0:T(8,128)(2,1)}, bf16[1,128,1024]{2,1,0:T(8,128)(2,1)S(1)}, u32[]{:S(2)}, u32[]{:S(2)}) collective-permute-start(bf16[1,128,1024]{2,1,0:T(8,128)(2,1)} %copy-done.19), channel_id=1, source_target_pairs={{0,16},{4,20},{8,24},{12,28},{16,0},{20,4},{24,8},{28,12},{1,17},{... | collective-permute-start | bytes 786440 | tf_op jit(solution)/shard_map/ppermute | solution.py:26
  241.5 10.2 %collective-permute-start.35 = (bf16[1,128,1024]{2,1,0:T(8,128)(2,1)}, bf16[1,128,1024]{2,1,0:T(8,128)(2,1)S(1)}, u32[]{:S(2)}, u32[]{:S(2)}) collective-permute-start(bf16[1,128,1024]{2,1,0:T(8,128)(2,1)} %copy-done.18), channel_id=1, source_target_pairs={{0,8},{4,12},{8,0},{12,4},{16,24},{20,28},{24,16},{28,20},{1,9},{5... | collective-permute-start | bytes 786440 | tf_op jit(solution)/shard_map/ppermute | solution.py:26
  251.5 18.7 %collective-permute-start.38 = (bf16[1,64,2048]{2,1,0:T(8,128)(2,1)S(1)}, bf16[1,64,2048]{2,1,0:T(8,128)(2,1)S(1)}, u32[]{:S(2)}, u32[]{:S(2)}) collective-permute-start(bf16[1,64,2048]{2,1,0:T(8,128)(2,1)S(1)} %copy-done.52), channel_id=1, source_target_pairs={{0,2},{1,3},{2,0},{3,1},{4,6},{5,7},{6,4},{7,5},{8,10},{9,11},{10,... | collective-permute-start | bytes 786440 | tf_op jit(solution)/shard_map/ppermute | solution.py:26
  252.5 14.9 %collective-permute-start.36 = (bf16[1,2,128,1024]{3,2,1,0:T(8,128)(2,1)S(1)}, bf16[1,2,128,1024]{3,2,1,0:T(8,128)(2,1)S(1)}, u32[]{:S(2)}, u32[]{:S(2)}) collective-permute-start(bf16[1,2,128,1024]{3,2,1,0:T(8,128)(2,1)S(1)} %get-tuple-element.155), channel_id=1, source_target_pairs={{0,8},{4,12},{8,0},{12,4},{16,24},{20,28},{24,16},{28,20},{1,9},{5... | collective-permute-start | bytes 1572872 | tf_op jit(solution)/shard_map/ppermute | solution.py:26
  253.8 13.6 %collective-permute-start.37 = (bf16[1,2,128,1024]{3,2,1,0:T(8,128)(2,1)S(1)}, bf16[1,2,128,1024]{3,2,1,0:T(8,128)(2,1)S(1)}, u32[]{:S(2)}, u32[]{:S(2)}) collective-permute-start(bf16[1,2,128,1024]{3,2,1,0:T(8,128)(2,1)S(1)} %get-tuple-element.157), channel_id=1, source_target_pairs={{0,16},{4,20},{8,24},{12,28},{16,0},{20,4},{24,8},{28,12},{1,17},{... | collective-permute-start | bytes 1572872 | tf_op jit(solution)/shard_map/ppermute | solution.py:26
  255.5 18.8 %collective-permute-start.40 = (bf16[1,64,2048]{2,1,0:T(8,128)(2,1)S(1)}, bf16[1,64,2048]{2,1,0:T(8,128)(2,1)S(1)}, u32[]{:S(2)}, u32[]{:S(2)}) collective-permute-start(bf16[1,64,2048]{2,1,0:T(8,128)(2,1)S(1)} %add_convert_fusion.2), channel_id=1, source_target_pairs={{0,2},{1,3},{2,0},{3,1},{4,6},{5,7},{6,4},{7,5},{8,10},{9,11},{10,... | collective-permute-start | bytes 786440 | tf_op jit(solution)/shard_map/ppermute | solution.py:26
  258.6 28.3 %collective-permute-start.42 = (bf16[184,1024]{1,0:T(8,128)(2,1)S(1)}, bf16[184,1024]{1,0:T(8,128)(2,1)S(1)}, u32[]{:S(2)}, u32[]{:S(2)}) collective-permute-start(bf16[184,1024]{1,0:T(8,128)(2,1)S(1)} %add_convert_fusion.1), channel_id=1, source_target_pairs={{0,8},{4,12},{8,0},{12,4},{16,24},{20,28},{24,16},{28,20},{1,9},{5... | collective-permute-start | bytes 1130504 | tf_op jit(solution)/shard_map/ppermute | solution.py:26
  268.2 24.1 %collective-permute-start.48 = (bf16[1,128,1024]{2,1,0:T(8,128)(2,1)S(1)}, bf16[1,128,1024]{2,1,0:T(8,128)(2,1)}, u32[]{:S(2)}, u32[]{:S(2)}) collective-permute-start(bf16[1,128,1024]{2,1,0:T(8,128)(2,1)S(1)} %get-tuple-element.176), channel_id=1, source_target_pairs={{0,8},{4,12},{8,0},{12,4},{16,24},{20,28},{24,16},{28,20},{1,9},{5... | collective-permute-start | bytes 786440 | tf_op jit(solution)/shard_map/ppermute | solution.py:26
  269.5 17.9 %collective-permute-start.47 = (bf16[1,128,1024]{2,1,0:T(8,128)(2,1)S(1)}, bf16[1,128,1024]{2,1,0:T(8,128)(2,1)S(1)}, u32[]{:S(2)}, u32[]{:S(2)}) collective-permute-start(bf16[1,128,1024]{2,1,0:T(8,128)(2,1)S(1)} %get-tuple-element.174), channel_id=1, source_target_pairs={{0,16},{4,20},{8,24},{12,28},{16,0},{20,4},{24,8},{28,12},{1,17},{... | collective-permute-start | bytes 786440 | tf_op jit(solution)/shard_map/ppermute | solution.py:26
  270.3 7.6 %collective-permute-start.49 = (bf16[2,2,16,1024]{3,2,0,1:T(8,128)(2,1)S(1)}, bf16[2,2,16,1024]{3,2,0,1:T(8,128)(2,1)S(1)}, u32[]{:S(2)}, u32[]{:S(2)}) collective-permute-start(bf16[2,2,16,1024]{3,2,0,1:T(8,128)(2,1)S(1)} %fusion.14), channel_id=1, source_target_pairs={{0,4},{4,0},{8,12},{12,8},{16,20},{20,16},{24,28},{28,24},{1,5},{5... | collective-permute-start | bytes 393224 | tf_op jit(solution)/shard_map/ppermute | solution.py:26
  287.0 8.6 %collective-permute-start.43 = (bf16[184,1024]{1,0:T(8,128)(2,1)S(1)}, bf16[184,1024]{1,0:T(8,128)(2,1)}, u32[]{:S(2)}, u32[]{:S(2)}) collective-permute-start(bf16[184,1024]{1,0:T(8,128)(2,1)S(1)} %add_convert_fusion), channel_id=1, source_target_pairs={{0,16},{4,20},{8,24},{12,28},{16,0},{20,4},{24,8},{28,12},{1,17},{... | collective-permute-start | bytes 1130504 | tf_op jit(solution)/shard_map/ppermute | solution.py:26
  296.8 5.7 %collective-permute-start.45 = (f32[2,1024]{1,0:T(2,128)S(1)}, f32[2,1024]{1,0:T(2,128)S(1)}, u32[]{:S(2)}, u32[]{:S(2)}) collective-permute-start(f32[2,1024]{1,0:T(2,128)S(1)} %slice.189), channel_id=1, source_target_pairs={{0,2},{1,3},{2,0},{3,1},{4,6},{5,7},{6,4},{7,5},{8,10},{9,11},{10,... | collective-permute-start | bytes 24584 | tf_op jit(solution)/shard_map/ppermute | solution.py:26
  297.6 5.5 %collective-permute-start.46 = (f32[2,1024]{1,0:T(2,128)S(1)}, f32[2,1024]{1,0:T(2,128)S(1)}, u32[]{:S(2)}, u32[]{:S(2)}) collective-permute-start(f32[2,1024]{1,0:T(2,128)S(1)} %slice.189), channel_id=1, source_target_pairs={{0,3},{1,2},{2,1},{3,0},{4,7},{5,6},{6,5},{7,4},{8,11},{9,10},{10,... | collective-permute-start | bytes 24584 | tf_op jit(solution)/shard_map/ppermute | solution.py:26
  (88 other events, 1489.2 us)
